TPU v7x, 32 devices: a whole 2x2x4 slice. The times are simulated.
32 devices in a mesh: seq: 8 (over y, x, core), head: 4 (over z).
Axes of the slice: x: 2, y: 2, z: 4, core: 2. Of those that a mesh axis runs over, the one named last changes fastest.
Arguments:
- queries: bfloat16 [2048, 4096], P('seq', 'head'), may hold values from -40 to 40
- key_rows: bfloat16 [2048, 1024], P('seq', 'head'), may hold values from -10 to 10
- value_rows: bfloat16 [2048, 1024], P('seq', 'head'), may hold values from -6 to 6
- out_weight: bfloat16 [4096, 4096], P('head'), may hold values from -0.09375 to 0.09375
- ssm_input: bfloat16 [2048, 8192], P('seq', 'head'), may hold values from -6 to 6
- bc_input: bfloat16 [2048, 2, 1024], P('seq', None, 'head'), may hold values from -6 to 6
- conv_input: float32 [4, 8192], P(None, 'head'), may hold values from -3 to 3
- conv_bc: float32 [4, 2, 1024], P(None, None, 'head'), may hold values from -3 to 3
- step_size: float32 [2048, 128], P('seq', 'head'), may hold values from 0.01 to 0.1
- decay_rate: float32 [128], P('head'), may hold values from 1e-05 to 1
- skip_gain: float32 [128], P('head'), may hold values from 0.5 to 1.5
- doc_ids: int32 [2048], P('seq'), may hold values from 0 to 7, never falling along the last dimension, each value on 1 to 1024 neighbouring positions
Outputs:
- attn_out: bfloat16 [2048, 4096], P(('seq', 'head'))
- ssm_out: bfloat16 [2048, 8192], P('seq', 'head')
Inputs may be any that keep to these rules, and one draw needn't show every extreme that they name: `doc_ids`: never falling along the sequence; each document covers at most 1024 positions and one covers exactly that many.
All inputs are finite; a program needn't handle non-finite values.
Results may differ from a plain program's by a relative error of at most 0.012.
Values may be sent and summed in bfloat16 or wider, within the bound.
No kernel may reach another device: no remote copies, remote signals or barrier semaphores. Data moves between devices by JAX's collectives and lax.ppermute only.
A program may use at most 192 MiB of HBM per device.

v0:
```python
import math

import jax
import jax.numpy as jnp
from jax import lax
from jax.sharding import PartitionSpec as P

HEAD_DIM = 128
STATE = 128
SB = 128


NEG_BIG = -1e30


def padded_2(cells, sides, width):
    for axis, dim in sides:
        count = lax.axis_size(axis)
        ends = count - 1
        head = lax.slice_in_dim(cells, 0, width, axis=dim)
        tail = lax.slice_in_dim(cells, cells.shape[dim] - width, cells.shape[dim], axis=dim)
        cells = jnp.concatenate(
            [
                lax.ppermute(tail, axis, [(i, (i + 1) % count) for i in range(ends)]),
                cells,
                lax.ppermute(head, axis, [((i + 1) % count, i) for i in range(ends)]),
            ],
            axis=dim,
        )
    return cells


def entering(x, axis, combine, identity, reverse):
    size, here = (lax.axis_size(axis), lax.axis_index(axis))
    everything = jax.tree.map(
        lambda part, kind: lax.all_gather(part.astype(kind), axis), x, (jnp.bfloat16, jnp.bfloat16)
    )
    start = jax.tree.map(
        lambda part, zero: jnp.broadcast_to(jnp.asarray(zero, part.dtype), part.shape), x, identity
    )

    def hop(k, before):
        at = size - 1 - k if reverse else k
        reached = at > here if reverse else at < here
        new = combine(
            before, jax.tree.map(lambda part, own: part[at].astype(own.dtype), everything, x)
        )
        return jax.tree.map(lambda a, b: jnp.where(reached, a, b), new, before)

    return lax.fori_loop(0, size, hop, start)


def layout_place(row_ids, rows_dev, seq_count):
    half_rows = rows_dev // 2
    device = row_ids // rows_dev
    within = row_ids % rows_dev
    block_id = jnp.where(within < half_rows, device, 2 * seq_count - 1 - device)
    return block_id * half_rows + within % half_rows


def ssd_block(block_carry, block_part, head_rates):
    state_in, last_doc = block_carry
    x_block, b_block, c_block, step_block, doc_block = block_part
    block_rows = x_block.shape[0]
    log_decay = jnp.cumsum(-head_rates[None] * step_block, axis=0)
    log_rows = jnp.transpose(log_decay, (1, 2, 0))
    row_ids = jnp.arange(block_rows)
    same_doc = (doc_block[:, None] == doc_block[None, :]) & (row_ids[:, None] >= row_ids[None, :])
    logit_scores = jnp.einsum("tgn,sgn->gts", c_block, b_block, preferred_element_type=jnp.float32)
    log_gap = jnp.where(same_doc, log_rows[..., :, None] - log_rows[..., None, :], 0.0)
    step_cols = jnp.transpose(step_block, (1, 2, 0))
    weights = jnp.where(
        same_doc, logit_scores[:, None] * jnp.exp(log_gap) * step_cols[..., None, :], 0.0
    )
    inner_sum = jnp.einsum(
        "gets,sgep->tgep", weights.astype(jnp.bfloat16), x_block, preferred_element_type=jnp.float32
    )
    alive_rows = (doc_block == last_doc).astype(jnp.float32)
    reach_rows = jnp.exp(log_decay) * alive_rows[:, None, None]
    carried = jnp.einsum(
        "tgn,gepn->tgep", c_block.astype(jnp.float32), state_in, precision=lax.Precision.HIGHEST
    )
    block_out = inner_sum + reach_rows[..., None] * carried
    end_doc = doc_block[block_rows - 1]
    keep_rows = (doc_block == end_doc).astype(jnp.float32)
    log_end = log_decay[block_rows - 1]
    fade_rows = jnp.exp(log_end[None] - log_decay) * step_block * keep_rows[:, None, None]
    scaled = (fade_rows[..., None] * x_block.astype(jnp.float32)).astype(jnp.bfloat16)
    fresh_state = jnp.einsum("sgep,sgn->gepn", scaled, b_block, preferred_element_type=jnp.float32)
    keep_state = jnp.exp(log_end) * (end_doc == last_doc).astype(jnp.float32)
    new_state = keep_state[..., None, None] * state_in + fresh_state
    return ((new_state, end_doc), block_out)


def ssd_half(x_conv, bc_conv, step_rows, doc_rows, doc_prev, head_rates):
    half_rows = x_conv.shape[0]
    block_count = half_rows // SB
    group_local = head_rates.shape[0]
    per_group = head_rates.shape[1]
    head_size = x_conv.shape[1] // (group_local * per_group)
    state_size = bc_conv.shape[2] // group_local
    x_blocks = x_conv.reshape(block_count, SB, group_local, per_group, head_size)
    b_blocks = bc_conv[:, 0].reshape(block_count, SB, group_local, state_size)
    c_rows = bc_conv[:, 1].reshape(half_rows, group_local, state_size)
    c_blocks = c_rows.reshape(block_count, SB, group_local, state_size)
    step_heads = step_rows.reshape(half_rows, group_local, per_group)
    step_blocks = step_heads.reshape(block_count, SB, group_local, per_group)
    doc_blocks = doc_rows.reshape(block_count, SB)
    start_carry = (
        jnp.zeros((group_local, per_group, head_size, state_size), jnp.float32),
        doc_prev,
    )

    def ssd_block_step(block_carry, block_part):
        return ssd_block(block_carry, block_part, head_rates)

    final_carry, outputs = lax.scan(
        ssd_block_step, start_carry, (x_blocks, b_blocks, c_blocks, step_blocks, doc_blocks)
    )
    log_decay = jnp.cumsum(-head_rates[None] * step_heads, axis=0)
    fade_out = jnp.exp(log_decay[half_rows - 1]) * (doc_rows[half_rows - 1] == doc_prev).astype(
        jnp.float32
    )
    reach_in = jnp.exp(log_decay) * (doc_rows == doc_prev).astype(jnp.float32)[:, None, None]
    local_out = outputs.reshape(half_rows, group_local, per_group, head_size)
    return (local_out, fade_out, final_carry[0], reach_in, c_rows)


def conv_half(ext_values, ext_docs, conv_all):
    lead_rows = conv_all.shape[0] - 1
    half_rows = ext_values.shape[0] - lead_rows
    own_docs = ext_docs[lead_rows:]
    accum = jnp.zeros((half_rows, ext_values.shape[1]), jnp.float32)
    for tap_index in range(lead_rows + 1):
        shifted = ext_values[lead_rows - tap_index : lead_rows - tap_index + half_rows].astype(
            jnp.float32
        )
        keep_rows = (
            ext_docs[lead_rows - tap_index : lead_rows - tap_index + half_rows] == own_docs
        )[:, None]
        accum = accum + jnp.where(keep_rows, conv_all[tap_index][None, :] * shifted, 0.0)
    return jax.nn.silu(accum).astype(jnp.bfloat16)


def link_states(earlier, later):
    return (earlier[0] * later[0], later[0][..., None, None] * earlier[1] + later[1])


def shards(
    queries,
    key_rows,
    value_rows,
    out_weight,
    ssm_input,
    bc_input,
    conv_input,
    conv_bc,
    step_size,
    decay_rate,
    skip_gain,
    doc_ids,
):
    seq_count = lax.axis_size("seq")
    seq_index = lax.axis_index("seq")
    rows_dev = queries.shape[0]
    half_rows = rows_dev // 2
    doc_all = lax.all_gather(doc_ids, "seq", axis=0, tiled=True)
    offsets = jnp.arange(half_rows, dtype=jnp.int32)
    front_place = seq_index * half_rows + offsets
    back_place = (2 * seq_count - 1 - seq_index) * half_rows + offsets
    query_place = jnp.concatenate([front_place, back_place])
    query_doc = jnp.take(doc_all, query_place)
    head_size = HEAD_DIM
    kv_local = key_rows.shape[1] // head_size
    group_size = queries.shape[1] // key_rows.shape[1]
    query_group = queries.reshape(rows_dev, kv_local, group_size, head_size)
    attention_score_scale = 1.0 / math.sqrt(head_size)

    def attend_block(state_carry, key_block, value_block, key_place):
        block_rows = key_block.shape[0]
        key_doc = jnp.take(doc_all, key_place)
        allowed = (key_place[None, :] <= query_place[:, None]) & (
            key_doc[None, :] == query_doc[:, None]
        )
        row_top, weight_sum, mixture_total_sum = state_carry
        key_heads = key_block.reshape(block_rows, kv_local, head_size)
        value_heads = value_block.reshape(block_rows, kv_local, head_size)
        logit_scores = (
            jnp.einsum("qhgd,khd->hgqk", query_group, key_heads, preferred_element_type=jnp.float32)
            * attention_score_scale
        )
        masked = jnp.where(allowed, logit_scores, NEG_BIG)
        new_top = jnp.maximum(row_top, jnp.max(masked, axis=-1))
        weights = jnp.where(allowed, jnp.exp(masked - new_top[..., None]), 0.0)
        shrink = jnp.exp(row_top - new_top)
        new_sum = weight_sum * shrink + jnp.sum(weights, axis=-1)
        new_mixed = mixture_total_sum * shrink[..., None] + jnp.einsum(
            "hgqk,khd->hgqd",
            weights.astype(jnp.bfloat16),
            value_heads,
            preferred_element_type=jnp.float32,
        )
        return (new_top, new_sum, new_mixed)

    start_attend = (
        jnp.full((kv_local, group_size, rows_dev), NEG_BIG, jnp.float32),
        jnp.zeros((kv_local, group_size, rows_dev), jnp.float32),
        jnp.zeros((kv_local, group_size, rows_dev, head_size), jnp.float32),
    )
    key_tile = lax.all_gather(key_rows, "seq", axis=0, tiled=True)
    value_tile = lax.all_gather(value_rows, "seq", axis=0, tiled=True)
    tile_rows = key_tile.shape[0]
    block_rows = 512
    block_count = tile_rows // block_rows
    key_place = layout_place(jnp.arange(tile_rows, dtype=jnp.int32), rows_dev, seq_count)

    def add_block_step(inner_carry, block_part):
        return (attend_block(inner_carry, block_part[0], block_part[1], block_part[2]), None)

    result_carry, unused_out = lax.scan(
        add_block_step,
        start_attend,
        (
            key_tile.reshape(block_count, block_rows, -1),
            value_tile.reshape(block_count, block_rows, -1),
            key_place.reshape(block_count, block_rows),
        ),
    )
    row_top, weight_sum, mixture_total_sum = result_carry
    context = (mixture_total_sum / weight_sum[..., None]).astype(jnp.bfloat16)
    context = jnp.transpose(context, (2, 0, 1, 3)).reshape(rows_dev, queries.shape[1])
    attn_out = lax.psum_scatter(
        jnp.dot(context, out_weight, preferred_element_type=jnp.float32).astype(jnp.bfloat16),
        "head",
        scatter_dimension=0,
        tiled=True,
    )
    x_width = ssm_input.shape[1]
    channels = jnp.concatenate([ssm_input, bc_input.reshape(rows_dev, -1)], axis=1)
    conv_all = jnp.concatenate([conv_input, conv_bc.reshape(conv_input.shape[0], -1)], axis=1)
    lead_rows = conv_all.shape[0] - 1
    front_rows = channels[:half_rows]
    back_rows = channels[half_rows:]
    edge_rows = jnp.concatenate(
        [back_rows[half_rows - lead_rows :], front_rows[half_rows - lead_rows :]], axis=0
    )
    padded = padded_2(edge_rows, (("seq", 0),), lead_rows)
    is_last = seq_index == seq_count - 1
    before_front = padded[:lead_rows]
    before_back = jnp.where(is_last, front_rows[half_rows - lead_rows :], padded[3 * lead_rows :])
    lead_ids = jnp.arange(lead_rows, dtype=jnp.int32)
    front_lead = seq_index * half_rows - lead_rows + lead_ids
    front_lead_doc = jnp.where(front_lead >= 0, jnp.take(doc_all, jnp.maximum(front_lead, 0)), -1)
    back_lead = back_place[0] - lead_rows + lead_ids
    back_lead_doc = jnp.take(doc_all, back_lead)
    front_docs = jnp.take(doc_all, front_place)
    back_docs = jnp.take(doc_all, back_place)
    front_conv = conv_half(
        jnp.concatenate([before_front, front_rows], axis=0),
        jnp.concatenate([front_lead_doc, front_docs]),
        conv_all,
    )
    back_conv = conv_half(
        jnp.concatenate([before_back, back_rows], axis=0),
        jnp.concatenate([back_lead_doc, back_docs]),
        conv_all,
    )
    group_local = bc_input.shape[2] // STATE
    per_group = decay_rate.shape[0] // group_local
    head_rates = decay_rate.reshape(group_local, per_group)
    front_prev = jnp.where(seq_index > 0, jnp.take(doc_all, jnp.maximum(front_place[0] - 1, 0)), -1)
    back_prev = jnp.take(doc_all, back_place[0] - 1)
    front_local, front_fade, front_state, front_reach, front_c = ssd_half(
        front_conv[:, :x_width],
        front_conv[:, x_width:].reshape(half_rows, 2, -1),
        step_size[:half_rows],
        front_docs,
        front_prev,
        head_rates,
    )
    back_local, back_fade, back_state, back_reach, back_c = ssd_half(
        back_conv[:, :x_width],
        back_conv[:, x_width:].reshape(half_rows, 2, -1),
        step_size[half_rows:],
        back_docs,
        back_prev,
        head_rates,
    )
    identity_pair = (jnp.ones_like(front_fade), jnp.zeros_like(front_state))
    front_prefix = entering((front_fade, front_state), "seq", link_states, identity_pair, False)
    front_in = front_prefix[1]
    after_front = front_fade[..., None, None] * front_in + front_state
    lead_fade = jnp.where(is_last, jnp.zeros_like(back_fade), back_fade)
    lead_state = jnp.where(
        is_last, back_fade[..., None, None] * after_front + back_state, back_state
    )
    back_prefix = entering((lead_fade, lead_state), "seq", link_states, identity_pair, True)
    back_in = back_prefix[0][..., None, None] * after_front + back_prefix[1]
    skip_heads = skip_gain.reshape(group_local, per_group)[None, :, :, None]

    def finish(local_out, reach_in, c_rows, state_in, x_conv):
        carried = jnp.einsum(
            "tgn,gepn->tgep", c_rows.astype(jnp.float32), state_in, precision=lax.Precision.HIGHEST
        )
        x_heads = x_conv.astype(jnp.float32).reshape(local_out.shape)
        mixed_out = local_out + reach_in[..., None] * carried + skip_heads * x_heads
        return mixed_out.reshape(half_rows, -1).astype(jnp.bfloat16)

    front_out = finish(front_local, front_reach, front_c, front_in, front_conv[:, :x_width])
    back_out = finish(back_local, back_reach, back_c, back_in, back_conv[:, :x_width])
    ssm_out = jnp.concatenate([front_out, back_out], axis=0)
    return (attn_out, ssm_out)


def solution(mesh):
    in_specs = (
        P("seq", "head"),
        P("seq", "head"),
        P("seq", "head"),
        P("head", None),
        P("seq", "head"),
        P("seq", None, "head"),
        P(None, "head"),
        P(None, None, "head"),
        P("seq", "head"),
        P("head"),
        P("head"),
        P("seq"),
    )
    out_specs = (P(("seq", "head"), None), P("seq", "head"))
    return jax.shard_map(shards, mesh=mesh, in_specs=in_specs, out_specs=out_specs, check_vma=False)
```

profile of v0, /device:TPU:0, one launch (start us, length us, event | category | flops | bytes accessed | tf_op | source)
XLA Modules:
  0.0 256.9 jit_solution(6416739815655025098)
XLA Ops:
  12.1 11.9 %all-gather.2 = s32[8,1,256]{2,1,0:T(1,128)S(1)} all-gather(s32[1,1,256]{2,1,0:T(1,128)S(1)} %bitcast.263), channel_id=1, replica_groups=mesh['seq'=8,'head'=4] {'seq'}, dimensions={0}, use_global_device_ids=true | all-gather | bytes 9216 | tf_op jit(solution)/shard_map/all_gather | solution.py:167
  32.4 2.2 collective-permute-start
  50.0 11.1 %all_gather.32 = bf16[8,2,16]{2,1,0:T(2,128)(2,1)} all-gather(bf16[1,2,16]{2,1,0:T(2,128)(2,1)S(1)} %copy-done.44), channel_id=1, replica_groups=mesh['seq'=8,'head'=4] {'seq'}, dimensions={0}, use_global_device_ids=true | all-gather | bytes 576 | tf_op jit(solution)/shard_map/all_gather | solution.py:36
  65.0 9.9 %all_gather.35 = bf16[8,2,16]{2,1,0:T(2,128)(2,1)} all-gather(bf16[1,2,16]{2,1,0:T(2,128)(2,1)S(1)} %copy-done.43), channel_id=1, replica_groups=mesh['seq'=8,'head'=4] {'seq'}, dimensions={0}, use_global_device_ids=true | all-gather | bytes 576 | tf_op jit(solution)/shard_map/all_gather | solution.py:36
  78.7 2.0 copy.100
  82.1 3.3 %multiply_convert_fusion = bf16[128,2560]{1,0:T(8,128)(2,1)S(1)} fusion(bf16[128,2560]{1,0:T(8,128)(2,1)} %get-tuple-element.573, bf16[3,2560]{1,0:T(4,128)(2,1)S(1)} %copy-done.29, f32[2560]{0:T(1024)S(1)} %copy-done.24, f32[2560]{0:T(1024)S(1)} %copy-done.26, f32[2560]{0:T(1024)S(1)} %copy-done.28, f32[2560]{0:T(1024)S(1)} %copy-done.22, ...), kind=kLoop, calls=%fused_computation.63 | loop fusion | flops 9175040 | bytes 1367424 | tf_op jit(solution)/shard_map/convert_element_type | solution.py:142
  86.3 2.1 copy.118
  88.7 2.1 convolution_bitcast_fusion.4
  95.3 16.0 %while.62 = (s32[]{:T(128)}, f32[2,16,64,128]{3,2,1,0:T(8,128)S(1)}, s32[]{:T(128)}, bf16[8,2,16]{2,1,0:T(2,128)(2,1)}, bf16[8,2,16,64,128]{4,3,2,1,0:T(8,128)(2,1)}, /*index=5*/s32[]{:T(128)}, s32[]{:T(128)}) while((s32[]{:T(128)}, f32[2,16,64,128]{3,2,1,0:T(8,128)S(1)}, s32[]{:T(128)}, bf16[8,2,16]{2,1,0:T(2,128)(2,1)}, ...), condition=%wide.region_7.10_spmd.clone, body=%wide.region_6.9_spmd.clone.sunk | while | flops 1310756 | bytes 2621865 | solution.py:50
  111.4 2.5 fusion.25
  114.2 14.3 %all-gather.10.cloned.1.call-done = bf16[2048,256]{1,0:T(8,128)(2,1)} async-done(((bf16[256,256]{1,0:T(8,128)(2,1)}), bf16[2048,256]{1,0:T(8,128)(2,1)}) %all-gather.10.cloned.1.call-update) | async-done | bytes 1048592 | tf_op jit(solution)/shard_map/all_gather | solution.py:211
  128.4 69.2 %while.61 = (s32[]{:T(128)}, f32[2,4,256]{2,1,0:T(4,128)S(1)}, f32[2,4,256]{2,1,0:T(4,128)}, f32[2,4,256,128]{3,2,1,0:T(8,128)}, s32[4,512]{1,0:T(4,128)}, /*ind...) while((s32[]{:T(128)}, f32[2,4,256]{2,1,0:T(4,128)S(1)}, ...), condition=%wide.region_3.4_spmd.clone, body=%wide.region_0.3_spmd.clone.sunk | while | flops 551698432 | bytes 18577608 | solution.py:220
  129.1 3.1 %gather_fusion = s32[512]{0:T(512)S(1)} fusion(s32[2048]{0:T(1024)S(1)} %get-tuple-element.791, s32[1024]{0:T(1024)S(1)} %pad_clamp_fusion.7), kind=kCustom, calls=%fused_computation.clone.clone.1 | custom fusion | bytes 6144 | tf_op jit(solution)/shard_map/while/body/eval_jaxpr/jit(_take)/gather | solution.py:181
  134.4 2.9 %fusion.114 = (f32[2,4,256]{2,1,0:T(4,128)S(1)}, f32[2,512,256,4]{2,1,3,0:T(8,128)}) fusion(pred[256,512]{0,1:T(8,128)(4,1)S(1)} %compare_and_fusion.2, bf16[512,2,128,1]{0,2,3,1:T(8,128)(2,1)S(1)} %bitcast.218, bf16[256,2,4,128]{3,0,2,1:T(8,128)(2,1)S(1)} %get-tuple-element.794), kind=kOutput, calls=%fused_computation.8.clone.1 | convolution fusion | flops 271579136 | bytes 5120000 | tf_op jit(solution)/shard_map/while/body/eval_jaxpr/qhgd,khd->hgqk/dot_general | solution.py:189
  137.3 3.4 %fusion.115 = f32[2,4,256]{2,1,0:T(4,128)S(1)} fusion(f32[2,512,256,4]{2,1,3,0:T(8,128)} %get-tuple-element.744, f32[2,4,256]{2,1,0:T(4,128)S(1)} %select_maximum_fusion.2, pred[256,512]{0,1:T(8,128)(4,1)S(1)} %compare_and_fusion.2), kind=kLoop, calls=%fused_computation.10.clone.1 | loop fusion | flops 5240832 | bytes 4341760 | tf_op jit(solution)/shard_map/while/body/eval_jaxpr/reduce_sum | solution.py:196
  140.9 4.7 %fusion.117 = f32[2,4,256,128]{3,2,1,0:T(8,128)} fusion(bf16[512,2,128,1]{0,2,3,1:T(8,128)(2,1)S(1)} %bitcast.219, f32[2,512,256,4]{2,1,3,0:T(8,128)} %get-tuple-element.744, f32[2,4,256]{2,1,0:T(4,128)S(1)} %select_maximum_fusion.2, pred[256,512]{0,1:T(8,128)(4,1)S(1)} %compare_and_fusion.2, f32[2,4,256,128]{3,2,1,0:T(8,128)} %get-tuple-element.775, ...), kind=kOutput, calls=%fused_computation.13.clone.1 | convolution fusion | flops 274464768 | bytes 6701057 | tf_op jit(solution)/shard_map/while/body/eval_jaxpr/hgqk,khd->hgqd/dot_general | solution.py:197
  146.4 3.1 %gather_fusion = s32[512]{0:T(512)S(1)} fusion(s32[2048]{0:T(1024)S(1)} %get-tuple-element.791, s32[1024]{0:T(1024)S(1)} %pad_clamp_fusion.7), kind=kCustom, calls=%fused_computation.clone.clone.1 | custom fusion | bytes 6144 | tf_op jit(solution)/shard_map/while/body/eval_jaxpr/jit(_take)/gather | solution.py:181
  151.6 2.9 %fusion.114 = (f32[2,4,256]{2,1,0:T(4,128)S(1)}, f32[2,512,256,4]{2,1,3,0:T(8,128)}) fusion(pred[256,512]{0,1:T(8,128)(4,1)S(1)} %compare_and_fusion.2, bf16[512,2,128,1]{0,2,3,1:T(8,128)(2,1)S(1)} %bitcast.218, bf16[256,2,4,128]{3,0,2,1:T(8,128)(2,1)S(1)} %get-tuple-element.794), kind=kOutput, calls=%fused_computation.8.clone.1 | convolution fusion | flops 271579136 | bytes 5120000 | tf_op jit(solution)/shard_map/while/body/eval_jaxpr/qhgd,khd->hgqk/dot_general | solution.py:189
  154.6 3.2 %fusion.115 = f32[2,4,256]{2,1,0:T(4,128)S(1)} fusion(f32[2,512,256,4]{2,1,3,0:T(8,128)} %get-tuple-element.744, f32[2,4,256]{2,1,0:T(4,128)S(1)} %select_maximum_fusion.2, pred[256,512]{0,1:T(8,128)(4,1)S(1)} %compare_and_fusion.2), kind=kLoop, calls=%fused_computation.10.clone.1 | loop fusion | flops 5240832 | bytes 4341760 | tf_op jit(solution)/shard_map/while/body/eval_jaxpr/reduce_sum | solution.py:196
  158.0 5.0 %fusion.117 = f32[2,4,256,128]{3,2,1,0:T(8,128)} fusion(bf16[512,2,128,1]{0,2,3,1:T(8,128)(2,1)S(1)} %bitcast.219, f32[2,512,256,4]{2,1,3,0:T(8,128)} %get-tuple-element.744, f32[2,4,256]{2,1,0:T(4,128)S(1)} %select_maximum_fusion.2, pred[256,512]{0,1:T(8,128)(4,1)S(1)} %compare_and_fusion.2, f32[2,4,256,128]{3,2,1,0:T(8,128)} %get-tuple-element.775, ...), kind=kOutput, calls=%fused_computation.13.clone.1 | convolution fusion | flops 274464768 | bytes 6701057 | tf_op jit(solution)/shard_map/while/body/eval_jaxpr/hgqk,khd->hgqd/dot_general | solution.py:197
  163.7 3.1 %gather_fusion = s32[512]{0:T(512)S(1)} fusion(s32[2048]{0:T(1024)S(1)} %get-tuple-element.791, s32[1024]{0:T(1024)S(1)} %pad_clamp_fusion.7), kind=kCustom, calls=%fused_computation.clone.clone.1 | custom fusion | bytes 6144 | tf_op jit(solution)/shard_map/while/body/eval_jaxpr/jit(_take)/gather | solution.py:181
  169.0 2.9 %fusion.114 = (f32[2,4,256]{2,1,0:T(4,128)S(1)}, f32[2,512,256,4]{2,1,3,0:T(8,128)}) fusion(pred[256,512]{0,1:T(8,128)(4,1)S(1)} %compare_and_fusion.2, bf16[512,2,128,1]{0,2,3,1:T(8,128)(2,1)S(1)} %bitcast.218, bf16[256,2,4,128]{3,0,2,1:T(8,128)(2,1)S(1)} %get-tuple-element.794), kind=kOutput, calls=%fused_computation.8.clone.1 | convolution fusion | flops 271579136 | bytes 5120000 | tf_op jit(solution)/shard_map/while/body/eval_jaxpr/qhgd,khd->hgqk/dot_general | solution.py:189
  171.9 3.2 %fusion.115 = f32[2,4,256]{2,1,0:T(4,128)S(1)} fusion(f32[2,512,256,4]{2,1,3,0:T(8,128)} %get-tuple-element.744, f32[2,4,256]{2,1,0:T(4,128)S(1)} %select_maximum_fusion.2, pred[256,512]{0,1:T(8,128)(4,1)S(1)} %compare_and_fusion.2), kind=kLoop, calls=%fused_computation.10.clone.1 | loop fusion | flops 5240832 | bytes 4341760 | tf_op jit(solution)/shard_map/while/body/eval_jaxpr/reduce_sum | solution.py:196
  175.3 5.0 %fusion.117 = f32[2,4,256,128]{3,2,1,0:T(8,128)} fusion(bf16[512,2,128,1]{0,2,3,1:T(8,128)(2,1)S(1)} %bitcast.219, f32[2,512,256,4]{2,1,3,0:T(8,128)} %get-tuple-element.744, f32[2,4,256]{2,1,0:T(4,128)S(1)} %select_maximum_fusion.2, pred[256,512]{0,1:T(8,128)(4,1)S(1)} %compare_and_fusion.2, f32[2,4,256,128]{3,2,1,0:T(8,128)} %get-tuple-element.775, ...), kind=kOutput, calls=%fused_computation.13.clone.1 | convolution fusion | flops 274464768 | bytes 6701057 | tf_op jit(solution)/shard_map/while/body/eval_jaxpr/hgqk,khd->hgqd/dot_general | solution.py:197
  181.0 3.1 %gather_fusion = s32[512]{0:T(512)S(1)} fusion(s32[2048]{0:T(1024)S(1)} %get-tuple-element.791, s32[1024]{0:T(1024)S(1)} %pad_clamp_fusion.7), kind=kCustom, calls=%fused_computation.clone.clone.1 | custom fusion | bytes 6144 | tf_op jit(solution)/shard_map/while/body/eval_jaxpr/jit(_take)/gather | solution.py:181
  186.3 2.9 %fusion.114 = (f32[2,4,256]{2,1,0:T(4,128)S(1)}, f32[2,512,256,4]{2,1,3,0:T(8,128)}) fusion(pred[256,512]{0,1:T(8,128)(4,1)S(1)} %compare_and_fusion.2, bf16[512,2,128,1]{0,2,3,1:T(8,128)(2,1)S(1)} %bitcast.218, bf16[256,2,4,128]{3,0,2,1:T(8,128)(2,1)S(1)} %get-tuple-element.794), kind=kOutput, calls=%fused_computation.8.clone.1 | convolution fusion | flops 271579136 | bytes 5120000 | tf_op jit(solution)/shard_map/while/body/eval_jaxpr/qhgd,khd->hgqk/dot_general | solution.py:189
  189.2 3.2 %fusion.115 = f32[2,4,256]{2,1,0:T(4,128)S(1)} fusion(f32[2,512,256,4]{2,1,3,0:T(8,128)} %get-tuple-element.744, f32[2,4,256]{2,1,0:T(4,128)S(1)} %select_maximum_fusion.2, pred[256,512]{0,1:T(8,128)(4,1)S(1)} %compare_and_fusion.2), kind=kLoop, calls=%fused_computation.10.clone.1 | loop fusion | flops 5240832 | bytes 4341760 | tf_op jit(solution)/shard_map/while/body/eval_jaxpr/reduce_sum | solution.py:196
  192.6 5.0 %fusion.117 = f32[2,4,256,128]{3,2,1,0:T(8,128)} fusion(bf16[512,2,128,1]{0,2,3,1:T(8,128)(2,1)S(1)} %bitcast.219, f32[2,512,256,4]{2,1,3,0:T(8,128)} %get-tuple-element.744, f32[2,4,256]{2,1,0:T(4,128)S(1)} %select_maximum_fusion.2, pred[256,512]{0,1:T(8,128)(4,1)S(1)} %compare_and_fusion.2, f32[2,4,256,128]{3,2,1,0:T(8,128)} %get-tuple-element.775, ...), kind=kOutput, calls=%fused_computation.13.clone.1 | convolution fusion | flops 274464768 | bytes 6701057 | tf_op jit(solution)/shard_map/while/body/eval_jaxpr/hgqk,khd->hgqd/dot_general | solution.py:197
  199.4 7.1 %convolution_convert_fusion = bf16[256,4096]{1,0:T(8,128)(2,1)} fusion(bf16[256,1024]{0,1:T(8,128)(2,1)S(1)} %bitcast.226, bf16[1024,4096]{1,0:T(8,128)(2,1)} %param.25), kind=kOutput, calls=%fused_computation.37 | convolution fusion | flops 2148532224 | bytes 11010048 | tf_op jit(solution)/shard_map/dot_general | solution.py:233
  210.6 21.0 %while.63 = (s32[]{:T(128)}, f32[2,16]{1,0:T(2,128)S(1)}, f32[2,16,64,128]{3,2,1,0:T(8,128)S(1)}, s32[]{:T(128)}, bf16[8,2,16]{2,1,0:T(2,128)(2,1)}, /*index=5*/...) while((s32[]{:T(128)}, f32[2,16]{1,0:T(2,128)S(1)}, ...), condition=%wide.region_10.13_spmd.clone, body=%wide.region_9.12_spmd.clone.sunk | while | flops 1310888 | bytes 2622261 | solution.py:50
  231.6 3.0 %fusion.26 = bf16[128,2,16,64]{0,3,2,1:T(8,128)(2,1)} fusion(f32[128,2,16,64]{0,3,2,1:T(8,128)} %fusion.18, bf16[128,2,128,1]{0,2,3,1:T(8,128)(2,1)S(1)} %bitcast.238, bf16[128,2,16,64]{0,3,2,1:T(8,128)(2,1)} %bitcast.224, f32[2,16,64,128]{3,2,1,0:T(8,128)S(1)} %get-tuple-element.375, f32[2,16]{1,0:T(2,128)S(1)} %get-tuple-element.374, ...), kind=kOutput, calls=%fused_computation.66 | convolution fusion | flops 405274624 | bytes 5325184 | tf_op jit(solution)/shard_map/tgn,gepn->tgep/dot_general | solution.py:302
  237.0 13.4 %reduce-scatter.2.cloned.1.call-done = bf16[64,4096]{1,0:T(8,128)(2,1)} async-done(((bf16[256,4096]{1,0:T(8,128)(2,1)}), bf16[64,4096]{1,0:T(8,128)(2,1)}) %reduce-scatter.2.cloned.1.call-update) | async-done | bytes 524304 | tf_op jit(solution)/shard_map/reduce_scatter | solution.py:232
  (314 shorter events, 97.2 us)
Async XLA Ops:
  7.2 88.1 %all-gather.12.cloned.1.call-start = ((), (), s32[]{:S(2)}) async-start(), calls=%async_computation.4 | async-start | bytes 4718592 | tf_op jit(solution)/shard_map/all_gather | solution.py:36
  8.7 23.1 %collective-permute-start.1 = (bf16[3,2560]{1,0:T(4,128)(2,1)S(1)}, bf16[3,2560]{1,0:T(4,128)(2,1)S(1)}, u32[]{:S(2)}, u32[]{:S(2)}) collective-permute-start(bf16[3,2560]{1,0:T(4,128)(2,1)S(1)} %slice.200), channel_id=1, source_target_pairs={{4,0},{8,4},{12,8},{16,12},{20,16},{24,20},{28,24},{5,1},{9,5},{13... | collective-permute-start | bytes 46088 | tf_op jit(solution)/shard_map/ppermute | solution.py:26
  10.0 17.1 %copy-start.33 = (f32[256,32]{0,1:T(8,128)S(1)}, f32[256,32]{0,1:T(8,128)}, u32[]{:S(2)}) copy-start(f32[256,32]{0,1:T(8,128)} %param.30) | copy-start | bytes 98308
  10.0 17.1 %copy-start.54 = (f32[32]{0:T(128)S(1)}, f32[32]{0:T(128)}, u32[]{:S(2)}) copy-start(f32[32]{0:T(128)} %param.31) | copy-start | bytes 388
  11.0 20.3 %copy-start.34 = (f32[4,2048]{1,0:T(4,128)S(1)}, f32[4,2048]{1,0:T(4,128)}, u32[]{:S(2)}) copy-start(f32[4,2048]{1,0:T(4,128)} %param.28) | copy-start | bytes 98308
  11.0 20.3 %copy-start.39 = (f32[4,2,256]{2,1,0:T(2,128)S(1)}, f32[4,2,256]{2,1,0:T(2,128)}, u32[]{:S(2)}) copy-start(f32[4,2,256]{2,1,0:T(2,128)} %param.29) | copy-start | bytes 24580
  32.4 3.1 %collective-permute-start = (bf16[3,2560]{1,0:T(4,128)(2,1)S(1)}, bf16[3,2560]{1,0:T(4,128)(2,1)S(1)}, u32[]{:S(2)}, u32[]{:S(2)}) collective-permute-start(bf16[3,2560]{1,0:T(4,128)(2,1)S(1)} %get-tuple-element.570), channel_id=1, source_target_pairs={{0,4},{4,8},{8,12},{12,16},{16,20},{20,24},{24,28},{1,5},{5,9},{9,... | collective-permute-start | bytes 46088 | tf_op jit(solution)/shard_map/ppermute | solution.py:24
  36.9 56.8 %copy-start.7 = (bf16[128,1,256]{0,2,1:T(8,128)(2,1)}, bf16[128,1,256]{0,2,1:T(8,128)(2,1)S(1)}, u32[]{:S(2)}) copy-start(bf16[128,1,256]{0,2,1:T(8,128)(2,1)S(1)} %get-tuple-element.576) | copy-start | bytes 196612
  37.2 55.6 %copy-start.1 = (bf16[128,2048]{0,1:T(8,128)(2,1)}, bf16[128,2048]{0,1:T(8,128)(2,1)S(1)}, u32[]{:S(2)}) copy-start(bf16[128,2048]{0,1:T(8,128)(2,1)S(1)} %copy.105) | copy-start | bytes 1572868
  37.2 7.6 %copy-start.31 = (f32[128,2,16]{0,2,1:T(8,128)S(1)}, f32[128,2,16]{0,2,1:T(8,128)}, u32[]{:S(2)}) copy-start(f32[128,2,16]{0,2,1:T(8,128)} %get-tuple-element.597) | copy-start | bytes 49156
  38.7 11.3 %copy-start.44 = (bf16[1,2,16]{2,1,0:T(2,128)(2,1)S(1)}, bf16[1,2,16]{2,1,0:T(2,128)(2,1)}, u32[]{:S(2)}) copy-start(bf16[1,2,16]{2,1,0:T(2,128)(2,1)} %get-tuple-element.578) | copy-start | bytes 196
  38.7 22.4 %copy-start.55 = (f32[32]{0:T(128)S(1)}, f32[32]{0:T(128)}, u32[]{:S(2)}) copy-start(f32[32]{0:T(128)} %param.32) | copy-start | bytes 388
  38.7 23.0 %copy-start.52 = (s32[128]{0:T(128)S(1)}, s32[128]{0:T(128)}, u32[]{:S(2)}) copy-start(s32[128]{0:T(128)} %copy-done.51) | copy-start | bytes 1540
  38.7 75.4 %all-gather.8.cloned.1.call-start = ((), (), s32[]{:S(2)}) async-start(), calls=%async_computation.1 | async-start | bytes 1179648 | tf_op jit(solution)/shard_map/all_gather | solution.py:210
  39.5 88.9 %all-gather.10.cloned.1.call-start = ((), (), s32[]{:S(2)}) async-start(), calls=%async_computation.2 | async-start | bytes 1179648 | tf_op jit(solution)/shard_map/all_gather | solution.py:211
  40.2 170.3 %all-gather.14.cloned.1.call-start = ((), (), s32[]{:S(2)}) async-start(), calls=%async_computation.5 | async-start | bytes 4718592 | tf_op jit(solution)/shard_map/all_gather | solution.py:36
  49.3 15.7 %copy-start.43 = (bf16[1,2,16]{2,1,0:T(2,128)(2,1)S(1)}, bf16[1,2,16]{2,1,0:T(2,128)(2,1)}, u32[]{:S(2)}) copy-start(bf16[1,2,16]{2,1,0:T(2,128)(2,1)} %get-tuple-element.583) | copy-start | bytes 196
  49.3 26.9 %copy-start.47 = (s32[128,1]{0,1:T(1,128)S(1)}, s32[128,1]{0,1:T(1,128)}, u32[]{:S(2)}) copy-start(s32[128,1]{0,1:T(1,128)} %fusion.67) | copy-start | bytes 1540
  49.3 26.9 %copy-start.48 = (s32[128,1]{0,1:T(1,128)S(1)}, s32[128,1]{0,1:T(1,128)}, u32[]{:S(2)}) copy-start(s32[128,1]{0,1:T(1,128)} %fusion.68) | copy-start | bytes 1540
  50.0 28.0 %copy-start.50 = (s32[128]{0:T(128)S(1)}, s32[128]{0:T(128)}, u32[]{:S(2)}) copy-start(s32[128]{0:T(128)} %copy-done.49) | copy-start | bytes 1540
  50.0 28.0 %copy-start.53 = (s32[128]{0:T(128)S(1)}, s32[128]{0:T(128)}, u32[]{:S(2)}) copy-start(s32[128]{0:T(128)} %copy-done.51) | copy-start | bytes 1540
  95.3 16.0 %copy-start.3 = (bf16[128,2048]{0,1:T(8,128)(2,1)S(1)}, bf16[128,2048]{0,1:T(8,128)(2,1)}, u32[]{:S(2)}) copy-start(bf16[128,2048]{0,1:T(8,128)(2,1)} %copy.118) | copy-start | bytes 1572868
  95.3 16.0 %copy-start.30 = (f32[128,2,16]{0,2,1:T(8,128)S(1)}, f32[128,2,16]{0,2,1:T(8,128)}, u32[]{:S(2)}) copy-start(f32[128,2,16]{0,2,1:T(8,128)} %copy.128) | copy-start | bytes 49156
  95.3 16.0 %copy-start.37 = (f32[2,16]{1,0:T(2,128)S(1)}, f32[2,16]{1,0:T(2,128)}, u32[]{:S(2)}) copy-start(f32[2,16]{1,0:T(2,128)} %get-tuple-element.561) | copy-start | bytes 388
  95.3 16.0 %copy-start.40 = (f32[2,16]{1,0:T(2,128)S(1)}, f32[2,16]{1,0:T(2,128)}, u32[]{:S(2)}) copy-start(f32[2,16]{1,0:T(2,128)} %get-tuple-element.562) | copy-start | bytes 388
  95.3 16.0 %copy-start.41 = (f32[2,16]{1,0:T(2,128)S(1)}, f32[2,16]{1,0:T(2,128)}, u32[]{:S(2)}) copy-start(f32[2,16]{1,0:T(2,128)} %get-tuple-element.563) | copy-start | bytes 388
  113.9 136.5 %reduce-scatter.2.cloned.1.call-start = ((), (), s32[]{:S(2)}) async-start(), calls=%async_computation.3 | async-start | bytes 2621440 | tf_op jit(solution)/shard_map/reduce_scatter | solution.py:232
  157.8 5.2 %copy-start.10 = (f32[2,4,256]{2,1,0:T(4,128)}, f32[2,4,256]{2,1,0:T(4,128)S(1)}, u32[]{:S(2)}) copy-start(f32[2,4,256]{2,1,0:T(4,128)S(1)} %get-tuple-element.787) | copy-start | bytes 24580 | tf_op jit(solution)/shard_map/while
  210.5 21.0 %copy-start = (f32[2,16,64,128]{3,2,1,0:T(8,128)S(1)}, f32[2,16,64,128]{3,2,1,0:T(8,128)}, u32[]{:S(2)}) copy-start(f32[2,16,64,128]{3,2,1,0:T(8,128)} %get-tuple-element.603) | copy-start | bytes 3145732
  210.6 21.0 %copy-start.6 = (bf16[128,1,256]{0,2,1:T(8,128)(2,1)S(1)}, bf16[128,1,256]{0,2,1:T(8,128)(2,1)}, u32[]{:S(2)}) copy-start(bf16[128,1,256]{0,2,1:T(8,128)(2,1)} %copy-done.5) | copy-start | bytes 196612
  210.6 21.0 %copy-start.14 = (f32[128,2,16]{0,2,1:T(8,128)S(1)}, f32[128,2,16]{0,2,1:T(8,128)}, u32[]{:S(2)}) copy-start(f32[128,2,16]{0,2,1:T(8,128)} %copy.125) | copy-start | bytes 49156
  210.6 21.0 %copy-start.38 = (f32[2,16]{1,0:T(2,128)S(1)}, f32[2,16]{1,0:T(2,128)}, u32[]{:S(2)}) copy-start(f32[2,16]{1,0:T(2,128)} %get-tuple-element.561) | copy-start | bytes 388
  (37 other events, 92.8 us)
Sparse Core Ops, SparseCore 0:
  38.9 38.9 all-gather.11
  79.8 23.3 all-gather.7
  105.0 23.3 all-gather.9
  130.2 36.5 all-gather.13
  206.6 43.7 reduce-scatter.1
where the time goes:
time: 259 us; the launch traced here: 257 us
  other arithmetic  73.7 us (28%)
  matrix products  54.2 us (21%)
  local copies, waits for them, and re-layouts  44.8 us (17%)
  blocking collectives  32.8 us (13%)
  waiting for transfers between devices  29.7 us (11%)
  between operations  17.4 us (7%)
  starting transfers between devices  3.91 us (2%)
    select_n x24, other arithmetic, hop(): return jax.tree.map(lambda a, b: jnp.where(reached, a, b), new, before)  26.4 us
    all_gather x2, blocking collectives, entering(): lax.all_gather(part.astype(kind), axis)  21 us
    dot_general x4, matrix products, attend_block(): jnp.einsum('hgqk,khd->hgqd', weights.astype(jnp.bfloat16), value_heads, p...  19.7 us
    all_gather x1, waiting for transfers between devices, shards(): value_tile = lax.all_gather(value_rows, 'seq', axis=0, tiled=True)  14.3 us
    reduce_scatter x1, waiting for transfers between devices, shards(): lax.psum_scatter(jnp.dot(context, out_weight, preferred_element_type=jnp....  13.4 us
    reduce_sum x4, other arithmetic, attend_block(): new_sum = weight_sum * shrink + jnp.sum(weights, axis=-1)  13.1 us
    gather x4, local copies, waits for them, and re-layouts, attend_block(): key_doc = jnp.take(doc_all, key_place)  12.6 us
    all_gather x1, blocking collectives, shards(): doc_all = lax.all_gather(doc_ids, 'seq', axis=0, tiled=True)  11.9 us
  transfers between devices with their start and end apart: 7, of which 3 were waited for; matrix products, arithmetic and copies ran while one was open for 65% of the time, Pallas kernels for 0%

commit v1 on v0

v1 whole, which is shorter than its diff:
```python
import functools
import math

import jax
import jax.numpy as jnp
from jax import lax
from jax.experimental import pallas as pl
from jax.experimental.pallas import tpu as pltpu
from jax.sharding import PartitionSpec as P

HEAD_DIM = 128
STATE = 128
SB = 128
LEAD = 8

NEG_BIG = -1e30
BF = jnp.bfloat16
F32 = jnp.float32
HI = lax.Precision.HIGHEST


def anywhere():
    return pl.BlockSpec(memory_space=pl.ANY)


def vmem():
    return pl.BlockSpec(memory_space=pltpu.VMEM)


def smem():
    return pl.BlockSpec(memory_space=pltpu.SMEM)


def swap(x, bit):
    count = lax.axis_size("seq")
    return lax.ppermute(x, "seq", [(i, i ^ bit) for i in range(count)])


def chip_bits(count):
    bits, bit = [], 2
    while bit < count:
        bits.append(bit)
        bit *= 2
    return bits


def two_way_gather(front, back, whole):
    count = lax.axis_size("seq")
    bits = chip_bits(count)
    pieces = [(0, None, whole)]
    fronts, backs = {0: front}, {0: back}
    for bit in bits:
        got = swap(whole, bit)
        pieces.append((bit, None, got))
        half_rows = got.shape[0] // 2
        fronts[bit], backs[bit] = got[:half_rows], got[half_rows:]
    for pattern in range(2, count, 2):
        if pattern in bits:
            continue
        high = max(bit for bit in bits if pattern & bit)
        low = min(bit for bit in bits if pattern & bit)
        fronts[pattern] = swap(fronts[pattern ^ high], high)
        pieces.append((pattern, 0, fronts[pattern]))
    for pattern in range(2, count, 2):
        if pattern in bits:
            continue
        low = min(bit for bit in bits if pattern & bit)
        backs[pattern] = swap(backs[pattern ^ low], low)
        pieces.append((pattern, 1, backs[pattern]))
    return pieces


def attend_kernel(
    places, half, count, is_back, ids_ref, docs_ref, docs_s, q_ref, w_ref, *rest
):
    total = len(places)
    pieces = rest[:total]
    send_ref, keep_ref, kvs, ws, scores, top, acc, ctx, kv_sem, w_sem = rest[total:]
    me = ids_ref[0]
    odd = ids_ref[1]
    rows = q_ref.shape[0]
    width = pieces[0].shape[-1]
    kv_heads = width // (2 * HEAD_DIM)
    group = q_ref.shape[1] // (kv_heads * HEAD_DIM)
    w_copy = pltpu.make_async_copy(w_ref, ws, w_sem)
    w_copy.start()
    copies = []
    for at, (pattern, part) in enumerate(places):
        owner = lax.bitwise_xor(me, pattern)
        if part is None:
            halves = ((0, 0, rows), (1, rows, rows)) if is_back else ((0, 0, rows),)
        else:
            halves = ((part, 0, rows),) if (part == 0 or is_back) else ()
        for which, first, size in halves:
            block = owner if which == 0 else 2 * count - 1 - owner
            copy = pltpu.make_async_copy(
                pieces[at].at[pl.ds(first, size)],
                kvs.at[pl.ds(pl.multiple_of(block * rows, rows), rows)],
                kv_sem.at[len(copies)],
            )
            copy.start()
            copies.append(copy)
    block = 2 * count - 1 - me if is_back else me

    def doc_at(where, lane):
        slot = lax.bitwise_xor(lax.shift_right_logical(where, 1), me)
        return docs_s[slot, lax.rem(where, 2) * rows + lane]

    first_doc = doc_at(block, 0)

    def count_step(at, skipped):
        return skipped + jnp.where(doc_at(at, rows - 1) < first_doc, 1, 0)

    start = lax.fori_loop(0, block, count_step, 0)
    tile_rows = 2 * rows
    first_tile = lax.shift_right_logical(start, 1)
    last_tile = lax.shift_right_logical(block, 1) + 1
    own = docs_ref[pl.ds(lax.bitwise_xor(lax.shift_right_logical(block, 1), me), 1), :]
    own = jnp.where(lax.rem(block, 2) == 1, own[:, rows:], own[:, :rows])
    own_col = jnp.transpose(jnp.broadcast_to(own, (rows, rows)))[:, :1]
    q_place = block * rows + lax.broadcasted_iota(jnp.int32, (rows, tile_rows), 0)
    k_place = lax.broadcasted_iota(jnp.int32, (rows, tile_rows), 1)
    for copy in copies:
        copy.wait()
    scale = math.log2(math.e) / math.sqrt(HEAD_DIM)
    for kv in range(kv_heads):
        heads = [kv * group + e for e in range(group)]
        q = jnp.concatenate(
            [q_ref[:, h * HEAD_DIM : (h + 1) * HEAD_DIM] for h in heads], axis=0
        )
        top[...] = jnp.full(top.shape, NEG_BIG, F32)
        acc[...] = jnp.zeros(acc.shape, F32)

        def score_step(tile, carry, q=q, kv=kv):
            at = pl.multiple_of(tile * tile_rows, tile_rows)
            keys = kvs[pl.ds(at, tile_rows), kv * HEAD_DIM : (kv + 1) * HEAD_DIM]
            docs = docs_ref[pl.ds(lax.bitwise_xor(tile, me), 1), :]
            allowed = (k_place + at <= q_place) & (docs == own_col)
            found = lax.dot_general(q, keys, (((1,), (1,)), ((), ())), preferred_element_type=F32)
            found = jnp.where(
                allowed[None], found.reshape(group, rows, tile_rows), NEG_BIG
            ).reshape(group * rows, tile_rows)
            scores[tile] = found
            top[...] = jnp.maximum(
                top[...], jnp.maximum(found[:, :HEAD_DIM], found[:, HEAD_DIM:])
            )
            return carry

        lax.fori_loop(first_tile, last_tile, score_step, 0)
        row_top = jnp.max(top[...], axis=1, keepdims=True)

        def mix_step(tile, carry, row_top=row_top, kv=kv):
            at = pl.multiple_of(tile * tile_rows, tile_rows)
            first = (kv_heads + kv) * HEAD_DIM
            values = kvs[pl.ds(at, tile_rows), first : first + HEAD_DIM]
            values = jnp.concatenate([values, jnp.ones_like(values)], axis=1)
            weights = jnp.exp2((scores[tile] - row_top) * scale).astype(BF)
            acc[...] += jnp.dot(weights, values, preferred_element_type=F32)
            return carry

        lax.fori_loop(first_tile, last_tile, mix_step, 0)
        mixed = (acc[:, :HEAD_DIM] / acc[:, HEAD_DIM:]).astype(BF)
        for e, h in enumerate(heads):
            ctx[:, h * HEAD_DIM : (h + 1) * HEAD_DIM] = mixed[e * rows : (e + 1) * rows]
    w_copy.wait()
    part_rows = rows // 2

    def project(at, carry):
        lanes = pl.ds(pl.multiple_of(at * 512, 512), 512)
        made = jnp.dot(ctx[...], ws[:, lanes], preferred_element_type=F32).astype(BF)
        lower, upper = made[:part_rows], made[part_rows:]

        @pl.when(odd == 0)
        def _():
            keep_ref[:, lanes] = lower
            send_ref[:, lanes] = upper

        @pl.when(odd == 1)
        def _():
            keep_ref[:, lanes] = upper
            send_ref[:, lanes] = lower

        return carry

    lax.fori_loop(0, w_ref.shape[1] // 512, project, 0)


def attend(ids, docs, queries, out_weight, pieces, is_back):
    count = docs.shape[0]
    rows = queries.shape[0] // 2
    places = [(pattern, part) for pattern, part, _ in pieces]
    arrays = [array for _, _, array in pieces]
    kv_width = arrays[0].shape[1]
    kv_heads = kv_width // (2 * HEAD_DIM)
    group = queries.shape[1] // (kv_heads * HEAD_DIM)
    features, columns = out_weight.shape
    half = 1 if is_back else 0
    return pl.pallas_call(
        functools.partial(attend_kernel, places, half, count, is_back),
        grid=(1,),
        in_specs=[
            smem(),
            vmem(),
            smem(),
            pl.BlockSpec((rows, queries.shape[1]), lambda t: (half, 0)),
            anywhere(),
        ]
        + [anywhere()] * len(arrays),
        out_specs=[vmem(), vmem()],
        out_shape=[jax.ShapeDtypeStruct((rows // 2, columns), BF)] * 2,
        scratch_shapes=[
            pltpu.VMEM((2 * count * rows, kv_width), BF),
            pltpu.VMEM((features, columns), BF),
            pltpu.VMEM((count, group * rows, 2 * rows), F32),
            pltpu.VMEM((group * rows, HEAD_DIM), F32),
            pltpu.VMEM((group * rows, 2 * HEAD_DIM), F32),
            pltpu.VMEM((rows, queries.shape[1]), BF),
            pltpu.SemaphoreType.DMA((2 * count,)),
            pltpu.SemaphoreType.DMA,
        ],
        cost_estimate=pl.CostEstimate(
            flops=2 * rows * features * columns, bytes_accessed=12 << 20, transcendentals=rows * 8192
        ),
        name="attend_back" if is_back else "attend_front",
    )(ids, docs, docs, queries, out_weight, *arrays)


def spread(values, expand):
    high = values.astype(BF)
    low = (values - high.astype(F32)).astype(BF)
    return jnp.dot(jnp.concatenate([high, low], axis=1), expand, preferred_element_type=F32)


def local_kernel(
    count, ids_ref, docs_ref, x_ref, bc_ref, lead_ref, tx_ref, tbc_ref, step_ref, rate_ref, expand_ref,
    xc_ref, xt_ref, mix_ref, reach_ref, keep_ref, send_ref, ext,
):
    half = pl.program_id(0)
    me = ids_ref[0]
    core = lax.rem(me, 2)
    rows, x_width = x_ref.shape
    bc_width = bc_ref.shape[1]
    groups = bc_width // (2 * STATE)
    x_group = x_width // groups
    block = jnp.where(half == 0, me, 2 * count - 1 - me)

    def doc_row(where):
        slot = lax.bitwise_xor(lax.shift_right_logical(where, 1), me)
        got = docs_ref[pl.ds(slot, 1), :]
        return jnp.where(lax.rem(where, 2) == 1, got[:, rows:], got[:, :rows])

    own = doc_row(block)
    before = jnp.where(block > 0, doc_row(jnp.maximum(block - 1, 0)), -1)
    lane = lax.broadcasted_iota(jnp.int32, (1, rows), 1)
    own_b = jnp.broadcast_to(own, (8, rows))
    before_b = jnp.broadcast_to(before, (8, rows))
    lane_b = jnp.broadcast_to(lane, (8, rows))
    lines = []
    for k in range(1, 4):
        moved = jnp.where(lane_b < k, pltpu.roll(before_b, k, 1), pltpu.roll(own_b, k, 1))
        lines.append((moved == own_b)[:1].astype(F32))
    last_doc = before[:, rows - 1 :]
    end_doc = own[:, rows - 1 :]
    lines.append((own == end_doc).astype(F32))
    lines.append((own == last_doc).astype(F32))
    lines.append(own.astype(F32))
    lines.append(jnp.zeros((2, rows), F32))
    table = jnp.transpose(jnp.concatenate(lines, axis=0))
    same = [table[:, k : k + 1] for k in range(3)]
    ending, alive, own_col = table[:, 3:4], table[:, 4:5], table[:, 5:6]

    def conv(source, taps, lead, width):
        ext[:LEAD, :width] = lead.astype(F32)
        ext[LEAD:, :width] = source.astype(F32)
        total = ext[LEAD:, :width] * taps[0:1]
        for k in range(1, 4):
            total += same[k - 1] * (ext[LEAD - k : LEAD - k + rows, :width] * taps[k : k + 1])
        return (total * (0.5 * jnp.tanh(0.5 * total) + 0.5)).astype(BF)

    bc = conv(bc_ref[...], tbc_ref[...], lead_ref[0, :, x_width:], bc_width)
    row_id = lax.broadcasted_iota(jnp.int32, (rows, rows), 0)
    col_id = lax.broadcasted_iota(jnp.int32, (rows, rows), 1)
    lower = row_id >= col_id
    steps = step_ref[...]
    logs = jnp.dot(
        lower.astype(F32), -rate_ref[...] * steps, preferred_element_type=F32, precision=HI
    )
    grow = jnp.exp(-logs) * steps
    reach = jnp.exp(logs)
    reach_ref[...] = reach
    expand = expand_ref[...]
    fade_end = spread(reach[rows - 8 :], expand)[7:8]
    carries = jnp.max(jnp.where(end_doc == last_doc, 1.0, 0.0))
    fade = fade_end * carries
    fade_high = fade.astype(BF)
    fade_low = (fade - fade_high.astype(F32)).astype(BF)
    allowed = lower & (own_col == own.astype(F32))
    for g in range(groups):
        lanes = slice(g * x_group, (g + 1) * x_group)
        xc = conv(x_ref[:, lanes], tx_ref[:, lanes], lead_ref[0, :, lanes], x_group)
        xc_ref[:, lanes] = xc
        xt = (xc.astype(F32) * spread(grow, expand[:, lanes])).astype(BF)
        xt_ref[:, lanes] = xt
        b = bc[:, g * STATE : (g + 1) * STATE]
        c = bc[:, (groups + g) * STATE : (groups + g + 1) * STATE]
        cb = lax.dot_general(c, b, (((1,), (1,)), ((), ())), preferred_element_type=F32)
        mix_ref[:, g * 2 * rows : g * 2 * rows + rows] = jnp.where(allowed, cb, 0.0).astype(BF)
        mix_ref[:, g * 2 * rows + rows : (g + 1) * 2 * rows] = (c.astype(F32) * alive).astype(BF)
        b_t = jnp.transpose(b.astype(F32) * ending).astype(BF)
        state = jnp.dot(b_t, xt, preferred_element_type=F32) * fade_end[:, lanes]
        packed = jnp.concatenate(
            [
                state.astype(BF),
                jnp.broadcast_to(fade_high[:, lanes], (8, x_group)),
                jnp.broadcast_to(fade_low[:, lanes], (8, x_group)),
            ],
            axis=0,
        )

        @pl.when(core == g)
        def _(packed=packed):
            keep_ref[0] = packed

        @pl.when(core != g)
        def _(packed=packed):
            send_ref[0] = packed


def unpack(packed):
    state = packed[:STATE].astype(F32)
    fade = packed[STATE : STATE + 1].astype(F32) + packed[STATE + 8 : STATE + 9].astype(F32)
    return fade, state


def pack(fade, state):
    high = fade.astype(BF)
    low = (fade - high.astype(F32)).astype(BF)
    shape = (8, state.shape[1])
    return jnp.concatenate(
        [state.astype(BF), jnp.broadcast_to(high, shape), jnp.broadcast_to(low, shape)], axis=0
    )


def join_kernel(ids_ref, mine_ref, other_ref, out_ref):
    core = lax.rem(ids_ref[0], 2)
    for half in range(2):
        first_is_mine = core == half

        def joined(first, second):
            fade_a, state_a = unpack(first)
            fade_b, state_b = unpack(second)
            return pack(fade_a * fade_b, fade_b * state_a + state_b)

        @pl.when(first_is_mine)
        def _(half=half):
            out_ref[half] = joined(mine_ref[half], other_ref[half])

        @pl.when(jnp.logical_not(first_is_mine))
        def _(half=half):
            out_ref[half] = joined(other_ref[half], mine_ref[half])


def enter_kernel(places, count, ids_ref, mine_ref, other_ref, *rest):
    total = len(places)
    pieces = rest[:total]
    keep_ref, send_ref, fronts, backs, sems, run = rest[total:]
    me = ids_ref[0]
    core = lax.rem(me, 2)
    chip = lax.shift_right_logical(me, 1)
    chips = count // 2
    copies = []
    for at, (pattern, part) in enumerate(places):
        slot = lax.bitwise_xor(chip, pattern // 2)
        for which in (0, 1) if part is None else (part,):
            source = pieces[at].at[which if part is None else 0]
            target = (fronts if which == 0 else backs).at[slot]
            copy = pltpu.make_async_copy(source, target, sems.at[len(copies)])
            copy.start()
            copies.append(copy)
    for copy in copies:
        copy.wait()
    run[...] = jnp.zeros(run.shape, F32)

    def put(half):
        entering = run[...]
        mine_first = core == half

        def after(packed):
            fade, state = unpack(packed)
            return (fade * entering + state).astype(BF)

        @pl.when(mine_first)
        def _():
            keep_ref[half] = entering.astype(BF)
            send_ref[half] = after(mine_ref[half])

        @pl.when(jnp.logical_not(mine_first))
        def _():
            send_ref[half] = entering.astype(BF)
            keep_ref[half] = after(other_ref[half])

    def front_step(at, carry):
        @pl.when(at == chip)
        def _():
            put(0)

        fade, state = unpack(fronts[at])
        run[...] = fade * run[...] + state
        return carry

    lax.fori_loop(0, chips, front_step, 0)

    def back_step(k, carry):
        at = chips - 1 - k

        @pl.when(at == chip)
        def _():
            put(1)

        fade, state = unpack(backs[at])
        run[...] = fade * run[...] + state
        return carry

    lax.fori_loop(0, chips - chip, back_step, 0)


def finish_kernel(
    ids_ref, xc_ref, xt_ref, mix_ref, reach_ref, skip_ref, expand_ref, mine_ref, other_ref, out_ref, both
):
    core = lax.rem(ids_ref[0], 2)
    rows, x_width = xc_ref.shape
    groups = mix_ref.shape[1] // (2 * rows)
    x_group = x_width // groups
    for g in range(groups):
        lanes = slice(g * x_group, (g + 1) * x_group)
        expand = expand_ref[:, lanes]
        both[:rows] = xt_ref[:, lanes]

        @pl.when(core == g)
        def _():
            both[rows:] = mine_ref[0]

        @pl.when(core != g)
        def _():
            both[rows:] = other_ref[0]

        mix = mix_ref[:, g * 2 * rows : (g + 1) * 2 * rows]
        made = jnp.dot(mix, both[...], preferred_element_type=F32)
        made = made * spread(reach_ref[...], expand)
        skip = spread(skip_ref[...], expand)[:1]
        out_ref[:, lanes] = (made + skip * xc_ref[:, lanes].astype(F32)).astype(BF)


def shards(
    queries, key_rows, value_rows, out_weight, ssm_input, bc_input, conv_input, conv_bc, step_size,
    decay_rate, skip_gain, doc_ids,
):
    count = lax.axis_size("seq")
    me = lax.axis_index("seq")
    z = lax.axis_index("head")
    rows_dev = queries.shape[0]
    rows = rows_dev // 2
    ids = jnp.stack([me, lax.rem(z, 2)]).astype(jnp.int32)

    docs = doc_ids.reshape(1, rows_dev)
    bit = 1
    while bit < count:
        docs = jnp.concatenate([docs, swap(docs, bit)], axis=0)
        bit *= 2

    x_width = ssm_input.shape[1]
    bc = bc_input.reshape(rows_dev, -1)
    bc_width = bc.shape[1]
    taps = conv_input.shape[0]
    edge_front = jnp.concatenate([ssm_input[rows - LEAD : rows], bc[rows - LEAD : rows]], axis=1)
    edge_back = jnp.concatenate([ssm_input[rows_dev - LEAD :], bc[rows_dev - LEAD :]], axis=1)
    lead_front = lax.ppermute(edge_front, "seq", [(i, i + 1) for i in range(count - 1)])
    lead_back = lax.ppermute(edge_back, "seq", [(i + 1, i) for i in range(count - 1)])
    lead_back = jnp.where(me == count - 1, edge_front, lead_back)
    lead = jnp.stack([lead_front, lead_back])

    kv = jnp.concatenate([key_rows, value_rows], axis=1)
    pieces = two_way_gather(kv[:rows], kv[rows:], kv)
    pieces = pieces + [(pattern ^ 1, part, swap(array, 1)) for pattern, part, array in pieces]

    groups = bc_width // (2 * STATE)
    heads = decay_rate.shape[0]
    x_group = x_width // groups
    expand = jnp.repeat(jnp.eye(heads, dtype=BF), x_width // heads, axis=1)
    expand = jnp.concatenate([expand, expand], axis=0)
    pack_rows = STATE + 16
    full = lambda shape: pl.BlockSpec(shape, lambda h: (0,) * len(shape))
    half = lambda width: pl.BlockSpec((rows, width), lambda h: (h, 0))
    packed_spec = pl.BlockSpec((1, pack_rows, x_group), lambda h: (h, 0, 0))
    xc, xt, mix, reach, keep, send = pl.pallas_call(
        functools.partial(local_kernel, count),
        grid=(2,),
        in_specs=[
            smem(),
            full((count, rows_dev)),
            half(x_width),
            half(bc_width),
            pl.BlockSpec((1, LEAD, x_width + bc_width), lambda h: (h, 0, 0)),
            full((taps, x_width)),
            full((taps, bc_width)),
            half(heads),
            full((1, heads)),
            full((2 * heads, x_width)),
        ],
        out_specs=[half(x_width), half(x_width), half(groups * 2 * rows), half(heads), packed_spec, packed_spec],
        out_shape=[
            jax.ShapeDtypeStruct((rows_dev, x_width), BF),
            jax.ShapeDtypeStruct((rows_dev, x_width), BF),
            jax.ShapeDtypeStruct((rows_dev, groups * 2 * rows), BF),
            jax.ShapeDtypeStruct((rows_dev, heads), F32),
            jax.ShapeDtypeStruct((2, pack_rows, x_group), BF),
            jax.ShapeDtypeStruct((2, pack_rows, x_group), BF),
        ],
        scratch_shapes=[pltpu.VMEM((rows + LEAD, x_group), F32)],
        cost_estimate=pl.CostEstimate(flops=400_000_000, bytes_accessed=6 << 20, transcendentals=700_000),
        name="local_states",
    )(
        ids, docs, ssm_input, bc, lead, conv_input, conv_bc.reshape(taps, -1), step_size,
        decay_rate.reshape(1, heads), expand,
    )

    other = swap(send, 1)
    chip = pl.pallas_call(
        join_kernel,
        in_specs=[smem(), vmem(), vmem()],
        out_specs=vmem(),
        out_shape=jax.ShapeDtypeStruct(keep.shape, BF),
        name="join_states",
    )(ids, keep, other)
    chip_pieces = two_way_gather(chip[:1], chip[1:], chip)
    chips = count // 2
    state_shape = jax.ShapeDtypeStruct((2, STATE, x_group), BF)
    enter_mine, enter_other = pl.pallas_call(
        functools.partial(enter_kernel, [(p, part) for p, part, _ in chip_pieces], count),
        in_specs=[smem(), vmem(), vmem()] + [anywhere()] * len(chip_pieces),
        out_specs=[vmem(), vmem()],
        out_shape=[state_shape, state_shape],
        scratch_shapes=[
            pltpu.VMEM((chips, pack_rows, x_group), BF),
            pltpu.VMEM((chips, pack_rows, x_group), BF),
            pltpu.SemaphoreType.DMA((2 * chips,)),
            pltpu.VMEM((STATE, x_group), F32),
        ],
        name="enter_states",
    )(ids, keep, other, *[array for _, _, array in chip_pieces])
    enter_got = swap(enter_other, 1)

    pair = [(i, i ^ 1) for i in range(4)]
    front_send, front_keep = attend(ids, docs, queries, out_weight, pieces, False)
    front_sum = front_keep + lax.ppermute(front_send, "head", pair)
    front_got = lax.ppermute(front_sum, "head", [(2, 0), (3, 1)])
    back_send, back_keep = attend(ids, docs, queries, out_weight, pieces, True)
    back_sum = back_keep + lax.ppermute(back_send, "head", pair)
    back_got = lax.ppermute(back_sum, "head", [(0, 2), (1, 3)])
    attn_out = jnp.where(z < 2, front_sum + front_got, back_sum + back_got)

    state_spec = pl.BlockSpec((1, STATE, x_group), lambda h: (h, 0, 0))
    skip = jnp.broadcast_to(skip_gain.reshape(1, heads), (8, heads))
    ssm_out = pl.pallas_call(
        finish_kernel,
        grid=(2,),
        in_specs=[
            smem(),
            half(x_width),
            half(x_width),
            half(groups * 2 * rows),
            half(heads),
            full((8, heads)),
            full((2 * heads, x_width)),
            state_spec,
            state_spec,
        ],
        out_specs=half(x_width),
        out_shape=jax.ShapeDtypeStruct((rows_dev, x_width), BF),
        scratch_shapes=[pltpu.VMEM((2 * rows, x_group), BF)],
        cost_estimate=pl.CostEstimate(flops=300_000_000, bytes_accessed=5 << 20, transcendentals=0),
        name="finish",
    )(ids, xc, xt, mix, reach, skip, expand, enter_mine, enter_got)
    return (attn_out, ssm_out)


def solution(mesh):
    in_specs = (
        P("seq", "head"),
        P("seq", "head"),
        P("seq", "head"),
        P("head", None),
        P("seq", "head"),
        P("seq", None, "head"),
        P(None, "head"),
        P(None, None, "head"),
        P("seq", "head"),
        P("head"),
        P("head"),
        P("seq"),
    )
    out_specs = (P(("seq", "head"), None), P("seq", "head"))
    return jax.shard_map(shards, mesh=mesh, in_specs=in_specs, out_specs=out_specs, check_vma=False)
```

time: 259 us -> 113 us (0.44)
  the two profiles are of different devices: /device:TPU:0 before, /device:TPU:26 now
where the time goes in v1:
time: 113 us; the launch traced here: 112 us
  Pallas kernels  40.7 us (36%)
  waiting for transfers between devices  27.8 us (25%)
  starting transfers between devices  23 us (20%)
  local copies, waits for them, and re-layouts  13 us (12%)
  other arithmetic  6.37 us (6%)
    pallas_call x2, Pallas kernels, attend(): pl.pallas_call(functools.partial(attend_kernel, places, half, count, is_b...  22.7 us
    ppermute x18, waiting for transfers between devices, swap(): return lax.ppermute(x, 'seq', [(i, i ^ bit) for i in range(count)])  12.8 us
    ppermute x18, starting transfers between devices, swap(): return lax.ppermute(x, 'seq', [(i, i ^ bit) for i in range(count)])  12.3 us
    unnamed x42, local copies, waits for them, and re-layouts  8.54 us
    pallas_call x1, Pallas kernels, shards(): pl.pallas_call(functools.partial(local_kernel, count), grid=(2,), in_spec...  6.94 us
    ppermute x1, waiting for transfers between devices, shards(): back_got = lax.ppermute(back_sum, 'head', [(0, 2), (1, 3)])  6.88 us
    ppermute x1, waiting for transfers between devices, shards(): back_sum = back_keep + lax.ppermute(back_send, 'head', pair)  6.02 us
    pallas_call x1, Pallas kernels, shards(): pl.pallas_call(functools.partial(enter_kernel, [(p, part) for p, part, _...  4.55 us
  transfers between devices with their start and end apart: 24, of which 8 were waited for; matrix products, arithmetic and copies ran while one was open for 13% of the time, Pallas kernels for 33%

profile of v1, /device:TPU:26, one launch (start us, length us, event | category | flops | bytes accessed | tf_op | source)
XLA Modules:
  0.0 111.8 jit_solution(10881425094838843929)
XLA Ops:
  0.6 0.9 constant_dynamic-update-slice_fusion.1
  1.5 0.9 constant_dynamic-update-slice_fusion.rest_0_
  3.1 1.5 %collective-permute-start.4 = (bf16[256,512]{1,0:T(8,128)(2,1)S(1)}, bf16[256,512]{1,0:T(8,128)(2,1)S(1)}, u32[]{:S(2)}, u32[]{:S(2)}) collective-permute-start(bf16[256,512]{1,0:T(8,128)(2,1)S(1)} %constant_dynamic-update-slice_fusion.rest_0_), channel_id=1, source_target_pairs={{0,16},{4,20},{8,24},{12,28},{16,0},{20,4},{24,8},{28,12},{1,17},{... | collective-permute-start | bytes 786440 | tf_op jit(solution)/shard_map/ppermute | solution.py:36
  6.6 3.0 %collective-permute-start.17 = (bf16[8,2560]{1,0:T(8,128)(2,1)S(1)}, bf16[8,2560]{1,0:T(8,128)(2,1)S(1)}, u32[]{:S(2)}, u32[]{:S(2)}) collective-permute-start(bf16[8,2560]{1,0:T(8,128)(2,1)S(1)} %pad_maximum_fusion.2), channel_id=1, source_target_pairs={{4,0},{8,4},{12,8},{16,12},{20,16},{24,20},{28,24},{5,1},{9,5},{13... | collective-permute-start | bytes 122888 | tf_op jit(solution)/shard_map/ppermute | solution.py:478
  11.6 1.7 %copy.15 = bf16[32,8,2,256]{3,1,2,0:T(8,128)(2,1)} copy(bf16[32,8,2,256]{3,2,1,0:T(2,128)(2,1)} %bitcast.18) | data formatting | bytes 524288
  13.3 1.5 %copy.14.step_ref = f32[256,32]{1,0:T(8,128)} copy(f32[256,32]{0,1:T(8,128)} %param.20) | data formatting | bytes 65536 | tf_op args[8]
  14.8 1.3 %copy.18 = f32[1,4,2,256]{3,1,2,0:T(4,128)} copy(f32[1,4,2,256]{3,2,1,0:T(2,128)} %bitcast.27) | data formatting | bytes 16384
  16.8 2.0 %collective-permute-start.2 = (s32[4,256]{1,0:T(4,128)S(1)}, s32[4,256]{1,0:T(4,128)S(1)}, u32[]{:S(2)}, u32[]{:S(2)}) collective-permute-start(s32[4,256]{1,0:T(4,128)S(1)} %pad_add_fusion.1), channel_id=1, source_target_pairs={{0,16},{4,20},{8,24},{12,28},{16,0},{20,4},{24,8},{28,12},{1,17},{... | collective-permute-start | bytes 12296 | tf_op jit(solution)/shard_map/ppermute | solution.py:36
  18.8 1.9 %collective-permute-start.16 = (bf16[8,2560]{1,0:T(8,128)(2,1)S(1)}, bf16[8,2560]{1,0:T(8,128)(2,1)S(1)}, u32[]{:S(2)}, u32[]{:S(2)}) collective-permute-start(bf16[8,2560]{1,0:T(8,128)(2,1)S(1)} %get-tuple-element.30), channel_id=1, source_target_pairs={{0,4},{4,8},{8,12},{12,16},{16,20},{20,24},{24,28},{1,5},{5,9},{9,... | collective-permute-start | bytes 122888 | tf_op jit(solution)/shard_map/ppermute | solution.py:477
  20.7 1.3 %pad_add_fusion.docs_ref.docs_s = s32[8,256]{1,0:T(8,128)} fusion(s32[4,256]{1,0:T(4,128)S(1)} %collective-permute-done.2, s32[2,256]{1,0:T(2,128)S(1)} %collective-permute-done.1, s32[1,256]{1,0:T(1,128)S(1)} %collective-permute-done, s32[1,256]{1,0:T(1,128)} %bitcast.26), kind=kLoop, calls=%fused_computation.11 | loop fusion | flops 6144 | bytes 16384 | tf_op jit(solution)/shard_map/concatenate | solution.py:468
  22.0 2.1 %collective-permute-done.16 = bf16[8,2560]{1,0:T(8,128)(2,1)S(1)} collective-permute-done((bf16[8,2560]{1,0:T(8,128)(2,1)S(1)}, bf16[8,2560]{1,0:T(8,128)(2,1)S(1)}, u32[]{:S(2)}, u32[]{:S(2)}) %collective-permute-start.16) | collective-permute-done | bytes 40992 | tf_op jit(solution)/shard_map/ppermute | solution.py:477
  24.9 3.0 %collective-permute-start.6 = (bf16[128,512]{1,0:T(8,128)(2,1)S(1)}, bf16[128,512]{1,0:T(8,128)(2,1)S(1)}, u32[]{:S(2)}, u32[]{:S(2)}) collective-permute-start(bf16[128,512]{1,0:T(8,128)(2,1)S(1)} %slice.41), channel_id=1, source_target_pairs={{0,8},{4,12},{8,0},{12,4},{16,24},{20,28},{24,16},{28,20},{1,9},{5... | collective-permute-start | bytes 393224 | tf_op jit(solution)/shard_map/ppermute | solution.py:36
  28.4 6.9 %local_states.1 = (bf16[256,2048]{1,0:T(8,128)(2,1)}, bf16[256,2048]{1,0:T(8,128)(2,1)}, bf16[256,512]{1,0:T(8,128)(2,1)}, f32[256,32]{1,0:T(8,128)}, bf16[2,144...) custom-call(s32[2]{0:T(128)} %pad_add_fusion.3.ids_ref, s32[8,256]{1,0:T(8,128)} %pad_add_fusion.docs_ref.docs_s, ...), custom_call_target="tpu_custom_call" | custom-call | flops 400000000 | bytes 6291456 | tf_op jit(solution)/shard_map/local_states/pallas_call | solution.py:495
  36.0 1.8 %collective-permute-done.10.rest_8_ = bf16[128,512]{1,0:T(8,128)(2,1)S(1)} collective-permute-done((bf16[128,512]{1,0:T(8,128)(2,1)S(1)}, bf16[128,512]{1,0:T(8,128)(2,1)S(1)}, u32[]{:S(2)}, u32[]{:S(2)}) %collective-permute-start.10) | collective-permute-done | bytes 131104 | tf_op jit(solution)/shard_map/ppermute | solution.py:36
  39.5 10.7 %attend_front.1 = (bf16[64,4096]{1,0:T(8,128)(2,1)}, bf16[64,4096]{1,0:T(8,128)(2,1)}) custom-call(s32[2]{0:T(128)} %pad_add_fusion.3.ids_ref, s32[8,256]{1,0:T(8,128)} %pad_add_fusion.docs_ref.docs_s, s32[8,256]{1,0:T(8,128)} %pad_add_fusion.docs_ref.docs_s, bf16[256,1024]{1,0:T(8,128)(2,1)} %q_ref.3, bf16[1024,4096]{1,0:T(8,128)(2,1)} %w_ref.3, ...), custom_call_target="tpu_custom_call" | custom-call | flops 1073741824 | bytes 12582912 | tf_op jit(solution)/shard_map/attend_front/pallas_call | solution.py:198
  50.7 12.0 %attend_back.1 = (bf16[64,4096]{1,0:T(8,128)(2,1)}, bf16[64,4096]{1,0:T(8,128)(2,1)}) custom-call(s32[2]{0:T(128)} %pad_add_fusion.3.ids_ref, s32[8,256]{1,0:T(8,128)} %pad_add_fusion.docs_ref.docs_s, s32[8,256]{1,0:T(8,128)} %pad_add_fusion.docs_ref.docs_s, bf16[256,1024]{1,0:T(8,128)(2,1)} %q_ref.3, bf16[1024,4096]{1,0:T(8,128)(2,1)} %w_ref.3, ...), custom_call_target="tpu_custom_call" | custom-call | flops 1073741824 | bytes 12582912 | tf_op jit(solution)/shard_map/attend_back/pallas_call | solution.py:198
  62.7 1.7 %collective-permute-start.14 = (bf16[64,4096]{1,0:T(8,128)(2,1)}, bf16[64,4096]{1,0:T(8,128)(2,1)}, u32[]{:S(2)}, u32[]{:S(2)}) collective-permute-start(bf16[64,4096]{1,0:T(8,128)(2,1)} %get-tuple-element.17), channel_id=1, source_target_pairs={{0,1},{1,0},{2,3},{3,2},{4,5},{5,4},{6,7},{7,6},{8,9},{9,8},{10,11... | collective-permute-start | bytes 1572872 | tf_op jit(solution)/shard_map/ppermute | solution.py:558
  64.4 0.8 copy-done
  65.2 2.3 %join_states.1.rest_0_ = bf16[2,144,1024]{2,1,0:T(8,128)(2,1)} custom-call(s32[2]{0:T(128)} %pad_add_fusion.3.ids_ref, bf16[2,144,1024]{2,1,0:T(8,128)(2,1)} %get-tuple-element.22.mine_ref, bf16[2,144,1024]{2,1,0:T(8,128)(2,1)} %copy-done), custom_call_target="tpu_custom_call" | custom-call | tf_op jit(solution)/shard_map/join_states/pallas_call | solution.py:528
  67.5 1.1 collective-permute-start.20
  68.7 2.3 %collective-permute-start.13 = (bf16[64,4096]{1,0:T(8,128)(2,1)S(1)}, bf16[64,4096]{1,0:T(8,128)(2,1)S(1)}, u32[]{:S(2)}, u32[]{:S(2)}) collective-permute-start(bf16[64,4096]{1,0:T(8,128)(2,1)S(1)} %add.12), channel_id=1, source_target_pairs={{2,0},{3,1},{6,4},{7,5},{10,8},{11,9},{14,12},{15,13},{18,16},{19,... | collective-permute-start | bytes 1572872 | tf_op jit(solution)/shard_map/ppermute | solution.py:556
  71.0 6.0 %collective-permute-done.14 = bf16[64,4096]{1,0:T(8,128)(2,1)} collective-permute-done((bf16[64,4096]{1,0:T(8,128)(2,1)}, bf16[64,4096]{1,0:T(8,128)(2,1)}, u32[]{:S(2)}, u32[]{:S(2)}) %collective-permute-start.14) | collective-permute-done | bytes 524320 | tf_op jit(solution)/shard_map/ppermute | solution.py:558
  77.0 1.3 %add.14 = bf16[64,4096]{1,0:T(8,128)(2,1)S(1)} add(bf16[64,4096]{1,0:T(8,128)(2,1)} %get-tuple-element.16, bf16[64,4096]{1,0:T(8,128)(2,1)} %collective-permute-done.14) | non-fusion elementwise | flops 262144 | bytes 1572864 | tf_op jit(solution)/shard_map/add | solution.py:558
  78.3 1.3 %collective-permute-start.15 = (bf16[64,4096]{1,0:T(8,128)(2,1)S(1)}, bf16[64,4096]{1,0:T(8,128)(2,1)S(1)}, u32[]{:S(2)}, u32[]{:S(2)}) collective-permute-start(bf16[64,4096]{1,0:T(8,128)(2,1)S(1)} %add.14), channel_id=1, source_target_pairs={{0,2},{1,3},{4,6},{5,7},{8,10},{9,11},{12,14},{13,15},{16,18},{17,... | collective-permute-start | bytes 1572872 | tf_op jit(solution)/shard_map/ppermute | solution.py:559
  79.6 2.9 %collective-permute-done.19.rest_1_ = bf16[2,144,1024]{2,1,0:T(8,128)(2,1)S(1)} collective-permute-done((bf16[2,144,1024]{2,1,0:T(8,128)(2,1)}, bf16[2,144,1024]{2,1,0:T(8,128)(2,1)S(1)}, u32[]{:S(2)}, u32[]{:S(2)}) %collective-permute-start.19) | collective-permute-done | bytes 589856 | tf_op jit(solution)/shard_map/ppermute | solution.py:36
  84.1 2.1 %collective-permute-start.22 = (bf16[1,144,1024]{2,1,0:T(8,128)(2,1)}, bf16[1,144,1024]{2,1,0:T(8,128)(2,1)}, u32[]{:S(2)}, u32[]{:S(2)}) collective-permute-start(bf16[1,144,1024]{2,1,0:T(8,128)(2,1)} %slice.43), channel_id=1, source_target_pairs={{0,8},{4,12},{8,0},{12,4},{16,24},{20,28},{24,16},{28,20},{1,9},{5... | collective-permute-start | bytes 884744 | tf_op jit(solution)/shard_map/ppermute | solution.py:36
  86.2 6.1 %collective-permute-done.21.rest_3_ = bf16[1,144,1024]{2,1,0:T(8,128)(2,1)} collective-permute-done((bf16[1,144,1024]{2,1,0:T(8,128)(2,1)}, bf16[1,144,1024]{2,1,0:T(8,128)(2,1)}, u32[]{:S(2)}, u32[]{:S(2)}) %collective-permute-start.21) | collective-permute-done | bytes 294944 | tf_op jit(solution)/shard_map/ppermute | solution.py:36
  92.3 1.8 %collective-permute-done.22.rest_4_ = bf16[1,144,1024]{2,1,0:T(8,128)(2,1)} collective-permute-done((bf16[1,144,1024]{2,1,0:T(8,128)(2,1)}, bf16[1,144,1024]{2,1,0:T(8,128)(2,1)}, u32[]{:S(2)}, u32[]{:S(2)}) %collective-permute-start.22) | collective-permute-done | bytes 294944 | tf_op jit(solution)/shard_map/ppermute | solution.py:36
  94.1 4.6 %enter_states.1 = (bf16[2,128,1024]{2,1,0:T(8,128)(2,1)}, bf16[2,128,1024]{2,1,0:T(8,128)(2,1)}) custom-call(s32[2]{0:T(128)} %pad_add_fusion.3.ids_ref, bf16[2,144,1024]{2,1,0:T(8,128)(2,1)} %get-tuple-element.22.mine_ref, bf16[2,144,1024]{2,1,0:T(8,128)(2,1)} %copy-done, bf16[2,144,1024]{2,1,0:T(8,128)(2,1)} %join_states.1.rest_0_, ...), custom_call_target="tpu_custom_call" | custom-call | tf_op jit(solution)/shard_map/enter_states/pallas_call | solution.py:538
  99.0 6.9 %collective-permute-done.15 = bf16[64,4096]{1,0:T(8,128)(2,1)S(1)} collective-permute-done((bf16[64,4096]{1,0:T(8,128)(2,1)S(1)}, bf16[64,4096]{1,0:T(8,128)(2,1)S(1)}, u32[]{:S(2)}, u32[]{:S(2)}) %collective-permute-start.15) | collective-permute-done | bytes 524320 | tf_op jit(solution)/shard_map/ppermute | solution.py:559
  105.9 0.9 add_select_fusion
  107.6 4.2 %finish.1 = bf16[256,2048]{1,0:T(8,128)(2,1)} custom-call(s32[2]{0:T(128)} %pad_add_fusion.3.ids_ref, bf16[256,2048]{1,0:T(8,128)(2,1)} %get-tuple-element.18.xc_ref, bf16[256,2048]{1,0:T(8,128)(2,1)} %get-tuple-element.19.xt_ref, bf16[256,512]{1,0:T(8,128)(2,1)} %get-tuple-element.20.mix_ref, f32[256,32]{1,0:T(8,128)} %get-tuple-element.21.reach_ref, ...), custom_call_target="tpu_custom_call" | custom-call | flops 300000000 | bytes 5242880 | tf_op jit(solution)/shard_map/finish/pallas_call | solution.py:564
  (85 shorter events, 12.1 us)
Async XLA Ops:
  2.5 35.6 %copy-start.4 = (bf16[256,512]{1,0:T(8,128)(2,1)}, bf16[256,512]{1,0:T(8,128)(2,1)S(1)}, u32[]{:S(2)}) copy-start(bf16[256,512]{1,0:T(8,128)(2,1)S(1)} %constant_dynamic-update-slice_fusion.rest_0_) | copy-start | bytes 786436
  2.5 22.3 %collective-permute-start.3 = (bf16[256,512]{1,0:T(8,128)(2,1)S(1)}, bf16[256,512]{1,0:T(8,128)(2,1)S(1)}, u32[]{:S(2)}, u32[]{:S(2)}) collective-permute-start(bf16[256,512]{1,0:T(8,128)(2,1)S(1)} %constant_dynamic-update-slice_fusion.rest_0_), channel_id=1, source_target_pairs={{0,8},{4,12},{8,0},{12,4},{16,24},{20,28},{24,16},{28,20},{1,9},{5... | collective-permute-start | bytes 786440 | tf_op jit(solution)/shard_map/ppermute | solution.py:36
  3.1 21.8 %collective-permute-start.4 = (bf16[256,512]{1,0:T(8,128)(2,1)S(1)}, bf16[256,512]{1,0:T(8,128)(2,1)S(1)}, u32[]{:S(2)}, u32[]{:S(2)}) collective-permute-start(bf16[256,512]{1,0:T(8,128)(2,1)S(1)} %constant_dynamic-update-slice_fusion.rest_0_), channel_id=1, source_target_pairs={{0,16},{4,20},{8,24},{12,28},{16,0},{20,4},{24,8},{28,12},{1,17},{... | collective-permute-start | bytes 786440 | tf_op jit(solution)/shard_map/ppermute | solution.py:36
  4.6 30.7 %collective-permute-start.7 = (bf16[256,512]{1,0:T(8,128)(2,1)S(1)}, bf16[256,512]{1,0:T(8,128)(2,1)S(1)}, u32[]{:S(2)}, u32[]{:S(2)}) collective-permute-start(bf16[256,512]{1,0:T(8,128)(2,1)S(1)} %constant_dynamic-update-slice_fusion.rest_0_), channel_id=1, source_target_pairs={{0,4},{4,0},{8,12},{12,8},{16,20},{20,16},{24,28},{28,24},{1,5},{5... | collective-permute-start | bytes 786440 | tf_op jit(solution)/shard_map/ppermute | solution.py:36
  4.6 5.6 %collective-permute-start = (s32[1,256]{1,0:T(1,128)}, s32[1,256]{1,0:T(1,128)S(1)}, u32[]{:S(2)}, u32[]{:S(2)}) collective-permute-start(s32[1,256]{1,0:T(1,128)} %bitcast.23), channel_id=1, source_target_pairs={{0,4},{4,0},{8,12},{12,8},{16,20},{20,16},{24,28},{28,24},{1,5},{5... | collective-permute-start | bytes 3080 | tf_op jit(solution)/shard_map/ppermute | solution.py:36
  6.6 12.1 %collective-permute-start.17 = (bf16[8,2560]{1,0:T(8,128)(2,1)S(1)}, bf16[8,2560]{1,0:T(8,128)(2,1)S(1)}, u32[]{:S(2)}, u32[]{:S(2)}) collective-permute-start(bf16[8,2560]{1,0:T(8,128)(2,1)S(1)} %pad_maximum_fusion.2), channel_id=1, source_target_pairs={{4,0},{8,4},{12,8},{16,12},{20,16},{24,20},{28,24},{5,1},{9,5},{13... | collective-permute-start | bytes 122888 | tf_op jit(solution)/shard_map/ppermute | solution.py:478
  10.2 18.2 %copy-start.3 = (bf16[64,2048]{1,0:T(8,128)(2,1)}, bf16[64,2048]{1,0:T(8,128)(2,1)S(1)}, u32[]{:S(2)}) copy-start(bf16[64,2048]{1,0:T(8,128)(2,1)S(1)} %constant_dynamic-update-slice_fusion.2.expand_ref) | copy-start | bytes 786436
  10.9 5.2 %collective-permute-start.1 = (s32[2,256]{1,0:T(2,128)S(1)}, s32[2,256]{1,0:T(2,128)S(1)}, u32[]{:S(2)}, u32[]{:S(2)}) collective-permute-start(s32[2,256]{1,0:T(2,128)S(1)} %pad_add_fusion.2), channel_id=1, source_target_pairs={{0,8},{4,12},{8,0},{12,4},{16,24},{20,28},{24,16},{28,20},{1,9},{5... | collective-permute-start | bytes 6152 | tf_op jit(solution)/shard_map/ppermute | solution.py:36
  16.8 3.9 %collective-permute-start.2 = (s32[4,256]{1,0:T(4,128)S(1)}, s32[4,256]{1,0:T(4,128)S(1)}, u32[]{:S(2)}, u32[]{:S(2)}) collective-permute-start(s32[4,256]{1,0:T(4,128)S(1)} %pad_add_fusion.1), channel_id=1, source_target_pairs={{0,16},{4,20},{8,24},{12,28},{16,0},{20,4},{24,8},{28,12},{1,17},{... | collective-permute-start | bytes 12296 | tf_op jit(solution)/shard_map/ppermute | solution.py:36
  18.8 5.3 %collective-permute-start.16 = (bf16[8,2560]{1,0:T(8,128)(2,1)S(1)}, bf16[8,2560]{1,0:T(8,128)(2,1)S(1)}, u32[]{:S(2)}, u32[]{:S(2)}) collective-permute-start(bf16[8,2560]{1,0:T(8,128)(2,1)S(1)} %get-tuple-element.30), channel_id=1, source_target_pairs={{0,4},{4,8},{8,12},{12,16},{16,20},{20,24},{24,28},{1,5},{5,9},{9,... | collective-permute-start | bytes 122888 | tf_op jit(solution)/shard_map/ppermute | solution.py:477
  24.8 13.3 %copy-start.1 = (bf16[256,512]{1,0:T(8,128)(2,1)}, bf16[256,512]{1,0:T(8,128)(2,1)S(1)}, u32[]{:S(2)}) copy-start(bf16[256,512]{1,0:T(8,128)(2,1)S(1)} %collective-permute-done.3.rest_1_) | copy-start | bytes 786436
  24.8 10.7 %collective-permute-start.5 = (bf16[128,512]{1,0:T(8,128)(2,1)S(1)}, bf16[128,512]{1,0:T(8,128)(2,1)S(1)}, u32[]{:S(2)}, u32[]{:S(2)}) collective-permute-start(bf16[128,512]{1,0:T(8,128)(2,1)S(1)} %slice.40), channel_id=1, source_target_pairs={{0,16},{4,20},{8,24},{12,28},{16,0},{20,4},{24,8},{28,12},{1,17},{... | collective-permute-start | bytes 393224 | tf_op jit(solution)/shard_map/ppermute | solution.py:36
  24.9 13.2 %copy-start.2 = (bf16[256,512]{1,0:T(8,128)(2,1)}, bf16[256,512]{1,0:T(8,128)(2,1)S(1)}, u32[]{:S(2)}) copy-start(bf16[256,512]{1,0:T(8,128)(2,1)S(1)} %collective-permute-done.4.rest_2_) | copy-start | bytes 786436
  24.9 11.0 %collective-permute-start.6 = (bf16[128,512]{1,0:T(8,128)(2,1)S(1)}, bf16[128,512]{1,0:T(8,128)(2,1)S(1)}, u32[]{:S(2)}, u32[]{:S(2)}) collective-permute-start(bf16[128,512]{1,0:T(8,128)(2,1)S(1)} %slice.41), channel_id=1, source_target_pairs={{0,8},{4,12},{8,0},{12,4},{16,24},{20,28},{24,16},{28,20},{1,9},{5... | collective-permute-start | bytes 393224 | tf_op jit(solution)/shard_map/ppermute | solution.py:36
  27.9 10.1 %collective-permute-start.8 = (bf16[256,512]{1,0:T(8,128)(2,1)S(1)}, bf16[256,512]{1,0:T(8,128)(2,1)S(1)}, u32[]{:S(2)}, u32[]{:S(2)}) collective-permute-start(bf16[256,512]{1,0:T(8,128)(2,1)S(1)} %collective-permute-done.3.rest_1_), channel_id=1, source_target_pairs={{0,4},{4,0},{8,12},{12,8},{16,20},{20,16},{24,28},{28,24},{1,5},{5... | collective-permute-start | bytes 786440 | tf_op jit(solution)/shard_map/ppermute | solution.py:36
  27.9 10.1 %collective-permute-start.9 = (bf16[256,512]{1,0:T(8,128)(2,1)S(1)}, bf16[256,512]{1,0:T(8,128)(2,1)S(1)}, u32[]{:S(2)}, u32[]{:S(2)}) collective-permute-start(bf16[256,512]{1,0:T(8,128)(2,1)S(1)} %collective-permute-done.4.rest_2_), channel_id=1, source_target_pairs={{0,4},{4,0},{8,12},{12,8},{16,20},{20,16},{24,28},{28,24},{1,5},{5... | collective-permute-start | bytes 786440 | tf_op jit(solution)/shard_map/ppermute | solution.py:36
  35.4 29.0 %collective-permute-start.18 = (bf16[2,144,1024]{2,1,0:T(8,128)(2,1)}, bf16[2,144,1024]{2,1,0:T(8,128)(2,1)S(1)}, u32[]{:S(2)}, u32[]{:S(2)}) collective-permute-start(bf16[2,144,1024]{2,1,0:T(8,128)(2,1)} %get-tuple-element.23), channel_id=1, source_target_pairs={{0,4},{4,0},{8,12},{12,8},{16,20},{20,16},{24,28},{28,24},{1,5},{5... | collective-permute-start | bytes 1769480 | tf_op jit(solution)/shard_map/ppermute | solution.py:36
  35.5 2.4 %collective-permute-start.10 = (bf16[128,512]{1,0:T(8,128)(2,1)S(1)}, bf16[128,512]{1,0:T(8,128)(2,1)S(1)}, u32[]{:S(2)}, u32[]{:S(2)}) collective-permute-start(bf16[128,512]{1,0:T(8,128)(2,1)S(1)} %collective-permute-done.5.rest_3_), channel_id=1, source_target_pairs={{0,4},{4,0},{8,12},{12,8},{16,20},{20,16},{24,28},{28,24},{1,5},{5... | collective-permute-start | bytes 393224 | tf_op jit(solution)/shard_map/ppermute | solution.py:36
  35.9 2.1 %collective-permute-start.11 = (bf16[128,512]{1,0:T(8,128)(2,1)S(1)}, bf16[128,512]{1,0:T(8,128)(2,1)S(1)}, u32[]{:S(2)}, u32[]{:S(2)}) collective-permute-start(bf16[128,512]{1,0:T(8,128)(2,1)S(1)} %collective-permute-done.6.rest_4_), channel_id=1, source_target_pairs={{0,4},{4,0},{8,12},{12,8},{16,20},{20,16},{24,28},{28,24},{1,5},{5... | collective-permute-start | bytes 393224 | tf_op jit(solution)/shard_map/ppermute | solution.py:36
  50.2 18.4 %copy-start.14 = (bf16[64,4096]{1,0:T(8,128)(2,1)S(1)}, bf16[64,4096]{1,0:T(8,128)(2,1)}, u32[]{:S(2)}) copy-start(bf16[64,4096]{1,0:T(8,128)(2,1)} %get-tuple-element.14) | copy-start | bytes 1572868
  50.2 18.4 %collective-permute-start.12 = (bf16[64,4096]{1,0:T(8,128)(2,1)}, bf16[64,4096]{1,0:T(8,128)(2,1)S(1)}, u32[]{:S(2)}, u32[]{:S(2)}) collective-permute-start(bf16[64,4096]{1,0:T(8,128)(2,1)} %get-tuple-element.15), channel_id=1, source_target_pairs={{0,1},{1,0},{2,3},{3,2},{4,5},{5,4},{6,7},{7,6},{8,9},{9,8},{10,11... | collective-permute-start | bytes 1572872 | tf_op jit(solution)/shard_map/ppermute | solution.py:555
  62.7 44.1 %copy-start.16 = (f32[32]{0:T(128)S(1)}, f32[32]{0:T(128)}, u32[]{:S(2)}) copy-start(f32[32]{0:T(128)} %param.22) | copy-start | bytes 388
  62.7 14.3 %collective-permute-start.14 = (bf16[64,4096]{1,0:T(8,128)(2,1)}, bf16[64,4096]{1,0:T(8,128)(2,1)}, u32[]{:S(2)}, u32[]{:S(2)}) collective-permute-start(bf16[64,4096]{1,0:T(8,128)(2,1)} %get-tuple-element.17), channel_id=1, source_target_pairs={{0,1},{1,0},{2,3},{3,2},{4,5},{5,4},{6,7},{7,6},{8,9},{9,8},{10,11... | collective-permute-start | bytes 1572872 | tf_op jit(solution)/shard_map/ppermute | solution.py:558
  67.5 15.0 %collective-permute-start.19 = (bf16[2,144,1024]{2,1,0:T(8,128)(2,1)}, bf16[2,144,1024]{2,1,0:T(8,128)(2,1)S(1)}, u32[]{:S(2)}, u32[]{:S(2)}) collective-permute-start(bf16[2,144,1024]{2,1,0:T(8,128)(2,1)} %join_states.1.rest_0_), channel_id=1, source_target_pairs={{0,8},{4,12},{8,0},{12,4},{16,24},{20,28},{24,16},{28,20},{1,9},{5... | collective-permute-start | bytes 1769480 | tf_op jit(solution)/shard_map/ppermute | solution.py:36
  67.5 15.8 %collective-permute-start.20 = (bf16[2,144,1024]{2,1,0:T(8,128)(2,1)}, bf16[2,144,1024]{2,1,0:T(8,128)(2,1)S(1)}, u32[]{:S(2)}, u32[]{:S(2)}) collective-permute-start(bf16[2,144,1024]{2,1,0:T(8,128)(2,1)} %join_states.1.rest_0_), channel_id=1, source_target_pairs={{0,16},{4,20},{8,24},{12,28},{16,0},{20,4},{24,8},{28,12},{1,17},{... | collective-permute-start | bytes 1769480 | tf_op jit(solution)/shard_map/ppermute | solution.py:36
  68.7 30.3 %collective-permute-start.13 = (bf16[64,4096]{1,0:T(8,128)(2,1)S(1)}, bf16[64,4096]{1,0:T(8,128)(2,1)S(1)}, u32[]{:S(2)}, u32[]{:S(2)}) collective-permute-start(bf16[64,4096]{1,0:T(8,128)(2,1)S(1)} %add.12), channel_id=1, source_target_pairs={{2,0},{3,1},{6,4},{7,5},{10,8},{11,9},{14,12},{15,13},{18,16},{19,... | collective-permute-start | bytes 1572872 | tf_op jit(solution)/shard_map/ppermute | solution.py:556
  78.3 27.6 %collective-permute-start.15 = (bf16[64,4096]{1,0:T(8,128)(2,1)S(1)}, bf16[64,4096]{1,0:T(8,128)(2,1)S(1)}, u32[]{:S(2)}, u32[]{:S(2)}) collective-permute-start(bf16[64,4096]{1,0:T(8,128)(2,1)S(1)} %add.14), channel_id=1, source_target_pairs={{0,2},{1,3},{4,6},{5,7},{8,10},{9,11},{12,14},{13,15},{16,18},{17,... | collective-permute-start | bytes 1572872 | tf_op jit(solution)/shard_map/ppermute | solution.py:559
  82.5 11.6 %copy-start.5 = (bf16[2,144,1024]{2,1,0:T(8,128)(2,1)}, bf16[2,144,1024]{2,1,0:T(8,128)(2,1)S(1)}, u32[]{:S(2)}) copy-start(bf16[2,144,1024]{2,1,0:T(8,128)(2,1)S(1)} %collective-permute-done.19.rest_1_) | copy-start | bytes 1769476
  83.3 9.0 %collective-permute-start.21 = (bf16[1,144,1024]{2,1,0:T(8,128)(2,1)}, bf16[1,144,1024]{2,1,0:T(8,128)(2,1)}, u32[]{:S(2)}, u32[]{:S(2)}) collective-permute-start(bf16[1,144,1024]{2,1,0:T(8,128)(2,1)} %slice.42), channel_id=1, source_target_pairs={{0,16},{4,20},{8,24},{12,28},{16,0},{20,4},{24,8},{28,12},{1,17},{... | collective-permute-start | bytes 884744 | tf_op jit(solution)/shard_map/ppermute | solution.py:36
  83.3 10.8 %copy-start.6 = (bf16[2,144,1024]{2,1,0:T(8,128)(2,1)}, bf16[2,144,1024]{2,1,0:T(8,128)(2,1)S(1)}, u32[]{:S(2)}) copy-start(bf16[2,144,1024]{2,1,0:T(8,128)(2,1)S(1)} %collective-permute-done.20.rest_2_) | copy-start | bytes 1769476
  84.1 10.0 %collective-permute-start.22 = (bf16[1,144,1024]{2,1,0:T(8,128)(2,1)}, bf16[1,144,1024]{2,1,0:T(8,128)(2,1)}, u32[]{:S(2)}, u32[]{:S(2)}) collective-permute-start(bf16[1,144,1024]{2,1,0:T(8,128)(2,1)} %slice.43), channel_id=1, source_target_pairs={{0,8},{4,12},{8,0},{12,4},{16,24},{20,28},{24,16},{28,20},{1,9},{5... | collective-permute-start | bytes 884744 | tf_op jit(solution)/shard_map/ppermute | solution.py:36
  98.7 8.1 %collective-permute-start.23 = (bf16[2,128,1024]{2,1,0:T(8,128)(2,1)}, bf16[2,128,1024]{2,1,0:T(8,128)(2,1)S(1)}, u32[]{:S(2)}, u32[]{:S(2)}) collective-permute-start(bf16[2,128,1024]{2,1,0:T(8,128)(2,1)} %get-tuple-element.25), channel_id=1, source_target_pairs={{0,4},{4,0},{8,12},{12,8},{16,20},{20,16},{24,28},{28,24},{1,5},{5... | collective-permute-start | bytes 1572872 | tf_op jit(solution)/shard_map/ppermute | solution.py:36
  (9 other events, 11.8 us)

commit v2 on v1

v2 whole, which is shorter than its diff:
```python
import functools
import math

import jax
import jax.numpy as jnp
import numpy as np
from jax import lax
from jax.experimental import pallas as pl
from jax.experimental.pallas import tpu as pltpu
from jax.sharding import PartitionSpec as P

HEAD_DIM = 128
STATE = 128
SB = 128
LEAD = 8
EDGE = 16
CHUNK = 512

NEG_BIG = -1e30
BF = jnp.bfloat16
F32 = jnp.float32
HI = lax.Precision.HIGHEST


def anywhere():
    return pl.BlockSpec(memory_space=pl.ANY)


def vmem():
    return pl.BlockSpec(memory_space=pltpu.VMEM)


def params(mebibytes):
    return pltpu.CompilerParams(vmem_limit_bytes=mebibytes << 20)


def takes(microseconds):
    return pl.CostEstimate(
        flops=int(microseconds * 1e10), bytes_accessed=int(microseconds * 3.7e6), transcendentals=0
    )


def in_hbm(x):
    return pltpu.with_memory_space_constraint(x, pltpu.HBM)


def swap(x, bit):
    count = lax.axis_size("seq")
    return lax.ppermute(x, "seq", [(i, i ^ bit) for i in range(count)])


def chip_gather(whole):
    count = lax.axis_size("seq")
    return [(0, whole)] + [(pattern, swap(whole, pattern)) for pattern in range(2, count, 2)]


def assemble(places, count, pieces, kvs, docs_ref, lead_ref):
    me = lax.axis_index("seq")
    rows = kvs.shape[0] // (2 * count)
    for piece, pattern in zip(pieces, places):
        owner = lax.bitwise_xor(me, pattern)
        back = 2 * count - 1 - owner
        kvs[pl.ds(pl.multiple_of(owner * rows, rows), rows), :] = piece[:rows]
        kvs[pl.ds(pl.multiple_of(back * rows, rows), rows), :] = piece[rows + EDGE : 2 * rows + EDGE]
        front_edge = piece[rows : rows + EDGE]
        docs_ref[pl.ds(owner, 1), :] = front_edge[:, : 2 * rows].astype(F32)[EDGE - 1 :]

        @pl.when(owner == me - 1)
        def _(front_edge=front_edge):
            lead_ref[0] = front_edge

        @pl.when(owner == me + 1)
        def _(piece=piece):
            lead_ref[1] = piece[2 * rows + EDGE :]

    own_edge = pieces[0][rows : rows + EDGE]

    @pl.when(me == 0)
    def _():
        lead_ref[0] = own_edge

    @pl.when(me == count - 1)
    def _():
        lead_ref[1] = own_edge


def attend_kernel(places, count, part, q_ref, w_ref, *rest):
    if part == 0:
        total = len(places)
        send_ref, keep_ref, kvs, docs_all, lead_ref, scores, top, acc, ctx = rest[total:]
        assemble(places, count, rest[:total], kvs, docs_all, lead_ref)
    else:
        kvs, docs_all, _, send_ref, keep_ref, scores, top, acc, ctx = rest
    me = lax.axis_index("seq")
    odd = lax.rem(lax.axis_index("head"), 2)
    rows = q_ref.shape[0] // 2
    chunk = rows // 2
    own_rows = chunk // 2
    kv_heads = kvs.shape[1] // (2 * HEAD_DIM)
    group = q_ref.shape[1] // (kv_heads * HEAD_DIM)
    tile_rows = 2 * rows
    scale = math.log2(math.e) / math.sqrt(HEAD_DIM)
    lane = lax.broadcasted_iota(jnp.int32, docs_all.shape, 1)
    is_end = lax.rem(lane, rows) == rows - 1
    k_place = lax.broadcasted_iota(jnp.int32, (chunk, tile_rows), 1)
    q_local = lax.broadcasted_iota(jnp.int32, (chunk, tile_rows), 0)
    q_local = q_local + part * own_rows + jnp.where(q_local >= own_rows, own_rows, 0)
    for side in range(2):
        block = 2 * count - 1 - me if side else me
        own = docs_all[pl.ds(lax.shift_right_logical(block, 1), 1), :]
        own = jnp.where(lax.rem(block, 2) == 1, own[:, rows:], own[:, :rows])
        own_col = jnp.transpose(jnp.broadcast_to(own, (rows, rows)))[:, :1]
        picks = [slice(c * chunk + part * own_rows, c * chunk + (part + 1) * own_rows) for c in range(2)]
        own_col = jnp.concatenate([own_col[pick] for pick in picks], axis=0)
        over = is_end & (docs_all[...] < own[:, :1])
        start = jnp.sum(over.astype(F32)).astype(jnp.int32)
        first_tile = lax.shift_right_logical(start, 1)
        last_tile = lax.shift_right_logical(block, 1) + 1
        q_place = block * rows + q_local
        heads = [list(range(kv * group, (kv + 1) * group)) for kv in range(kv_heads)]
        qs = [
            jnp.concatenate(
                [
                    q_ref[side * rows + pick.start : side * rows + pick.stop, h * HEAD_DIM : (h + 1) * HEAD_DIM]
                    for h in heads[kv]
                    for pick in picks
                ],
                axis=0,
            )
            for kv in range(kv_heads)
        ]
        top[...] = jnp.full(top.shape, NEG_BIG, F32)
        acc[...] = jnp.zeros(acc.shape, F32)

        def score_step(tile, carry, qs=qs, q_place=q_place, own_col=own_col):
            at = pl.multiple_of(tile * tile_rows, tile_rows)
            docs = docs_all[pl.ds(tile, 1), :]
            allowed = (k_place + at <= q_place) & (docs == own_col)
            for kv in range(kv_heads):
                keys = kvs[pl.ds(at, tile_rows), kv * HEAD_DIM : (kv + 1) * HEAD_DIM]
                found = lax.dot_general(
                    qs[kv], keys, (((1,), (1,)), ((), ())), preferred_element_type=F32
                )
                found = jnp.where(
                    allowed[None], found.reshape(group, chunk, tile_rows), NEG_BIG
                ).reshape(group * chunk, tile_rows)
                scores[tile, kv] = found
                top[kv] = jnp.maximum(
                    top[kv], jnp.maximum(found[:, :HEAD_DIM], found[:, HEAD_DIM:])
                )
            return carry

        lax.fori_loop(first_tile, last_tile, score_step, 0)
        row_tops = [jnp.max(top[kv], axis=1, keepdims=True) for kv in range(kv_heads)]

        def mix_step(tile, carry, row_tops=row_tops):
            at = pl.multiple_of(tile * tile_rows, tile_rows)
            for kv in range(kv_heads):
                first = (kv_heads + kv) * HEAD_DIM
                values = kvs[pl.ds(at, tile_rows), first : first + HEAD_DIM]
                values = jnp.concatenate([values, jnp.ones_like(values)], axis=1)
                weights = jnp.exp2((scores[tile, kv] - row_tops[kv]) * scale).astype(BF)
                acc[kv] += jnp.dot(weights, values, preferred_element_type=F32)
            return carry

        lax.fori_loop(first_tile, last_tile, mix_step, 0)
        for kv in range(kv_heads):
            mixed = (acc[kv, :, :HEAD_DIM] / acc[kv, :, HEAD_DIM:]).astype(BF)
            for e, h in enumerate(heads[kv]):
                ctx[side * chunk : (side + 1) * chunk, h * HEAD_DIM : (h + 1) * HEAD_DIM] = mixed[
                    e * chunk : (e + 1) * chunk
                ]
    mixed = ctx[...]
    columns = w_ref.shape[1]
    made = [
        jnp.dot(mixed, w_ref[:, at : at + 256], preferred_element_type=F32).astype(BF)
        for at in range(0, columns, 256)
    ]

    def put(low_ref, high_ref):
        for at, got in enumerate(made):
            lanes = slice(at * 256, (at + 1) * 256)
            for side in range(2):
                first = 2 * side * own_rows
                low_ref[side * own_rows : (side + 1) * own_rows, lanes] = got[first : first + own_rows]
                high_ref[side * own_rows : (side + 1) * own_rows, lanes] = got[
                    first + own_rows : first + 2 * own_rows
                ]

    @pl.when(odd == 0)
    def _():
        put(keep_ref, send_ref)

    @pl.when(odd == 1)
    def _():
        put(send_ref, keep_ref)


def attend(queries, out_weight, part, places, operands):
    count = lax.axis_size("seq")
    rows = queries.shape[0] // 2
    chunk = rows // 2
    kv_width = operands[0].shape[1]
    kv_heads = kv_width // (2 * HEAD_DIM)
    group = queries.shape[1] // (kv_heads * HEAD_DIM)
    columns = out_weight.shape[1]
    outs = [jax.ShapeDtypeStruct((chunk, columns), BF)] * 2
    if part == 0:
        specs = [vmem()] * len(operands)
        outs = outs + [
            pltpu.VMEM((2 * count * rows, kv_width), BF),
            pltpu.VMEM((count, 2 * rows), F32),
            pltpu.VMEM((2, EDGE, kv_width), BF),
        ]
    else:
        specs = [vmem(), vmem(), anywhere()]
    return pl.pallas_call(
        functools.partial(attend_kernel, places, count, part),
        in_specs=[vmem()] * 2 + specs,
        out_specs=[vmem()] * len(outs),
        out_shape=outs,
        scratch_shapes=[
            pltpu.VMEM((count, kv_heads, group * chunk, 2 * rows), F32),
            pltpu.VMEM((kv_heads, group * chunk, HEAD_DIM), F32),
            pltpu.VMEM((kv_heads, group * chunk, 2 * HEAD_DIM), F32),
            pltpu.VMEM((rows, queries.shape[1]), BF),
        ],
        compiler_params=params(8 + count * 7 // 8),
        cost_estimate=takes(8),
        name="attend_late" if part else "attend_early",
    )(queries, out_weight, *operands)


def pair_kernel(got_ref, keep_ref, after_ref, send_out, keep_out, *through):
    for ref in through:
        ref[...] = after_ref[...]
    own_rows = send_out.shape[0]
    low = lax.axis_index("head") < 2

    def add(first):
        rows = slice(first, first + own_rows)
        return (got_ref[rows].astype(F32) + keep_ref[rows].astype(F32)).astype(BF)

    @pl.when(low)
    def _():
        keep_out[...] = add(0)
        send_out[...] = add(own_rows)

    @pl.when(jnp.logical_not(low))
    def _():
        keep_out[...] = add(own_rows)
        send_out[...] = add(0)


def pair_sum(got, keep, after, through):
    rows, columns = keep.shape
    outs = [jax.ShapeDtypeStruct((rows // 2, columns), BF)] * 2
    if through:
        outs = outs + [jax.ShapeDtypeStruct(after.shape, after.dtype)]
    return pl.pallas_call(
        pair_kernel,
        in_specs=[vmem(), vmem(), vmem() if through else anywhere()],
        out_specs=[vmem()] * len(outs),
        out_shape=outs,
        compiler_params=params(8),
        cost_estimate=takes(0),
        name="pair_sum",
    )(got, keep, after)


def last_kernel(early_got, early_keep, late_got, late_keep, after_ref, out_ref):
    rows = early_got.shape[0]
    out_ref[:rows] = (early_got[...].astype(F32) + early_keep[...].astype(F32)).astype(BF)
    out_ref[rows:] = (late_got[...].astype(F32) + late_keep[...].astype(F32)).astype(BF)


def prepare_kernel(k_ref, v_ref, docs_ref, xf_ref, xb_ref, bc_ref, kv_ref, flat_ref):
    rows = k_ref.shape[0] // 2
    width = k_ref.shape[1]
    part = bc_ref.shape[2]
    for at in range(2):
        flat_ref[:, at * part : (at + 1) * part] = bc_ref[:, at, :]
    docs = jnp.broadcast_to(docs_ref[...], (LEAD, 2 * rows)).astype(F32)[:1]
    docs = jnp.concatenate([docs, jnp.zeros((1, 2 * width - 2 * rows), F32)], axis=1)
    for half, x_ref in ((0, xf_ref), (1, xb_ref)):
        first = half * (rows + EDGE)
        kv_ref[first : first + rows, :width] = k_ref[half * rows : (half + 1) * rows]
        kv_ref[first : first + rows, width:] = v_ref[half * rows : (half + 1) * rows]
        x_edge = x_ref[...].astype(F32)
        bc_edge = flat_ref[(half + 1) * rows - LEAD : (half + 1) * rows].astype(F32)
        lines = []
        for t in range(LEAD - 3, LEAD):
            for edge in (x_edge, bc_edge):
                lines += [edge[t : t + 1, c : c + CHUNK] for c in range(0, edge.shape[1], CHUNK)]
        kv_ref[first + rows : first + rows + EDGE] = jnp.concatenate(lines + [docs], axis=0).astype(BF)


def load_kernel(w_ref, q_ref, x_ref, kv_ref, w_out, q_out, x_out, kv_out, sems):
    copies = [
        pltpu.make_async_copy(q_ref, q_out, sems.at[0]),
        pltpu.make_async_copy(x_ref, x_out, sems.at[5]),
    ]
    parts = 4
    size = w_ref.shape[0] // parts
    for at in range(parts):
        piece = pl.ds(at * size, size)
        copies.append(pltpu.make_async_copy(w_ref.at[piece], w_out.at[piece], sems.at[at + 1]))
    for copy in copies:
        copy.start()
    kv_out[...] = kv_ref[...]
    for copy in copies:
        copy.wait()


def spread(values, expand):
    high = values.astype(BF)
    low = (values - high.astype(F32)).astype(BF)
    return jnp.dot(jnp.concatenate([high, low], axis=1), expand, preferred_element_type=F32)


def local_kernel(
    count, docs_ref, lead_ref, x_ref, bc_ref, tx_ref, tbc_ref, step_ref, rate_ref, expand_ref, after_ref,
    xc_ref, xt_ref, mix_ref, reach_ref, keep_ref, send_ref, ext,
):
    half = pl.program_id(0)
    me = lax.axis_index("seq")
    core = lax.rem(me, 2)
    rows = xc_ref.shape[0]
    x_width = x_ref.shape[1]
    mine = pl.ds(pl.multiple_of(half * rows, rows), rows)
    bc_width = bc_ref.shape[1]
    groups = bc_width // (2 * STATE)
    x_group = x_width // groups
    block = jnp.where(half == 0, me, 2 * count - 1 - me)

    def doc_row(where):
        got = docs_ref[pl.ds(lax.shift_right_logical(where, 1), 1), :]
        return jnp.where(lax.rem(where, 2) == 1, got[:, rows:], got[:, :rows])

    own = doc_row(block)
    before = jnp.where(block > 0, doc_row(jnp.maximum(block - 1, 0)), -1.0)
    lead = lead_ref[half].astype(F32)
    chunks = (x_width + bc_width) // CHUNK
    lane = lax.broadcasted_iota(jnp.int32, (1, rows), 1)
    own_b = jnp.broadcast_to(own, (8, rows))
    before_b = jnp.broadcast_to(before, (8, rows))
    lane_b = jnp.broadcast_to(lane, (8, rows))
    lines = []
    for k in range(1, 4):
        moved = jnp.where(lane_b < k, pltpu.roll(before_b, k, 1), pltpu.roll(own_b, k, 1))
        lines.append((moved == own_b)[:1].astype(F32))
    last_doc = before[:, rows - 1 :]
    end_doc = own[:, rows - 1 :]
    lines.append((own == end_doc).astype(F32))
    lines.append((own == last_doc).astype(F32))
    lines.append(own)
    lines.append(jnp.zeros((2, rows), F32))
    table = jnp.transpose(jnp.concatenate(lines, axis=0))
    same = [table[:, k : k + 1] for k in range(3)]
    ending, alive, own_col = table[:, 3:4], table[:, 4:5], table[:, 5:6]

    def conv(source, taps, chunk, width):
        for t in range(3):
            for c in range(width // CHUNK):
                line = t * chunks + chunk + c
                ext[LEAD - 3 + t : LEAD - 2 + t, c * CHUNK : (c + 1) * CHUNK] = lead[line : line + 1]
        ext[LEAD:, :width] = source.astype(F32)
        total = ext[LEAD:, :width] * taps[0:1]
        for k in range(1, 4):
            total += same[k - 1] * (ext[LEAD - k : LEAD - k + rows, :width] * taps[k : k + 1])
        return (total * (0.5 * jnp.tanh(0.5 * total) + 0.5)).astype(BF)

    tbc = jnp.concatenate([tbc_ref[:, 0, :], tbc_ref[:, 1, :]], axis=1)
    bc = conv(bc_ref[mine, :], tbc, x_width // CHUNK, bc_width)
    row_id = lax.broadcasted_iota(jnp.int32, (rows, rows), 0)
    col_id = lax.broadcasted_iota(jnp.int32, (rows, rows), 1)
    lower = row_id >= col_id
    steps = jnp.transpose(step_ref[...])
    logs = jnp.dot(
        lower.astype(F32), -rate_ref[...] * steps, preferred_element_type=F32, precision=HI
    )
    grow = jnp.exp(-logs) * steps
    reach = jnp.exp(logs)
    reach_ref[...] = reach
    expand = expand_ref[...]
    fade_end = spread(reach[rows - 8 :], expand)[7:8]
    carries = jnp.max(jnp.where(end_doc == last_doc, 1.0, 0.0))
    fade = fade_end * carries
    fade_high = fade.astype(BF)
    fade_low = (fade - fade_high.astype(F32)).astype(BF)
    allowed = lower & (own_col == own)
    for g in range(groups):
        lanes = slice(g * x_group, (g + 1) * x_group)
        xc = conv(x_ref[mine, lanes], tx_ref[:, lanes], g * x_group // CHUNK, x_group)
        xc_ref[:, lanes] = xc
        xt = (xc.astype(F32) * spread(grow, expand[:, lanes])).astype(BF)
        xt_ref[:, lanes] = xt
        b = bc[:, g * STATE : (g + 1) * STATE]
        c = bc[:, (groups + g) * STATE : (groups + g + 1) * STATE]
        cb = lax.dot_general(c, b, (((1,), (1,)), ((), ())), preferred_element_type=F32)
        mix_ref[:, g * 2 * rows : g * 2 * rows + rows] = jnp.where(allowed, cb, 0.0).astype(BF)
        mix_ref[:, g * 2 * rows + rows : (g + 1) * 2 * rows] = (c.astype(F32) * alive).astype(BF)
        b_t = jnp.transpose(b.astype(F32) * ending).astype(BF)
        state = jnp.dot(b_t, xt, preferred_element_type=F32) * fade_end[:, lanes]
        packed = jnp.concatenate(
            [
                state.astype(BF),
                jnp.broadcast_to(fade_high[:, lanes], (8, x_group)),
                jnp.broadcast_to(fade_low[:, lanes], (8, x_group)),
            ],
            axis=0,
        )

        @pl.when(core == g)
        def _(packed=packed):
            keep_ref[0] = packed

        @pl.when(core != g)
        def _(packed=packed):
            send_ref[0] = packed


def unpack(packed):
    state = packed[:STATE].astype(F32)
    fade = packed[STATE : STATE + 1].astype(F32) + packed[STATE + 8 : STATE + 9].astype(F32)
    return fade, state


def pack(fade, state):
    high = fade.astype(BF)
    low = (fade - high.astype(F32)).astype(BF)
    shape = (8, state.shape[1])
    return jnp.concatenate(
        [state.astype(BF), jnp.broadcast_to(high, shape), jnp.broadcast_to(low, shape)], axis=0
    )


def join_kernel(mine_ref, other_ref, after_ref, out_ref):
    core = lax.rem(lax.axis_index("seq"), 2)
    for half in range(2):
        first_is_mine = core == half

        def joined(first, second):
            fade_a, state_a = unpack(first)
            fade_b, state_b = unpack(second)
            return pack(fade_a * fade_b, fade_b * state_a + state_b)

        @pl.when(first_is_mine)
        def _(half=half):
            out_ref[half] = joined(mine_ref[half], other_ref[half])

        @pl.when(jnp.logical_not(first_is_mine))
        def _(half=half):
            out_ref[half] = joined(other_ref[half], mine_ref[half])


def enter_kernel(places, count, mine_ref, other_ref, after_ref, *rest):
    total = len(places)
    pieces = rest[:total]
    keep_ref, send_ref, fronts, backs, sems, run = rest[total:]
    me = lax.axis_index("seq")
    core = lax.rem(me, 2)
    chip = lax.shift_right_logical(me, 1)
    chips = count // 2
    copies = []
    for at, pattern in enumerate(places):
        slot = lax.bitwise_xor(chip, pattern // 2)
        for half, target in enumerate((fronts, backs)):
            copy = pltpu.make_async_copy(pieces[at].at[half], target.at[slot], sems.at[len(copies)])
            copy.start()
            copies.append(copy)
    for copy in copies:
        copy.wait()
    run[...] = jnp.zeros(run.shape, F32)

    def put(half):
        entering = run[...]
        mine_first = core == half

        def after(packed):
            fade, state = unpack(packed)
            return (fade * entering + state).astype(BF)

        @pl.when(mine_first)
        def _():
            keep_ref[half] = entering.astype(BF)
            send_ref[half] = after(mine_ref[half])

        @pl.when(jnp.logical_not(mine_first))
        def _():
            send_ref[half] = entering.astype(BF)
            keep_ref[half] = after(other_ref[half])

    def front_step(at, carry):
        @pl.when(at == chip)
        def _():
            put(0)

        fade, state = unpack(fronts[at])
        run[...] = fade * run[...] + state
        return carry

    lax.fori_loop(0, chips, front_step, 0)

    def back_step(k, carry):
        at = chips - 1 - k

        @pl.when(at == chip)
        def _():
            put(1)

        fade, state = unpack(backs[at])
        run[...] = fade * run[...] + state
        return carry

    lax.fori_loop(0, chips - chip, back_step, 0)


def finish_kernel(
    xc_ref, xt_ref, mix_ref, reach_ref, skip_ref, expand_ref, mine_ref, other_ref, out_ref, done_ref, both
):
    done_ref[...] = jnp.zeros(done_ref.shape, F32)
    core = lax.rem(lax.axis_index("seq"), 2)
    half = pl.program_id(0)
    rows, x_width = out_ref.shape
    groups = mix_ref.shape[1] // (2 * rows)
    x_group = x_width // groups
    for g in range(groups):
        lanes = slice(g * x_group, (g + 1) * x_group)
        expand = expand_ref[:, lanes]
        both[:rows] = xt_ref[:, lanes]

        @pl.when(core == g)
        def _():
            both[rows:] = mine_ref[half]

        @pl.when(core != g)
        def _():
            both[rows:] = other_ref[half]

        mix = mix_ref[:, g * 2 * rows : (g + 1) * 2 * rows]
        made = jnp.dot(mix, both[...], preferred_element_type=F32)
        made = made * spread(reach_ref[...], expand)
        skip = spread(jnp.broadcast_to(skip_ref[...], (8, skip_ref.shape[1])), expand)[:1]
        out_ref[:, lanes] = (made + skip * xc_ref[:, lanes].astype(F32)).astype(BF)


def shards(
    queries, key_rows, value_rows, out_weight, ssm_input, bc_input, conv_input, conv_bc, step_size,
    decay_rate, skip_gain, doc_ids,
):
    count = lax.axis_size("seq")
    rows_dev = queries.shape[0]
    rows = rows_dev // 2
    x_width = ssm_input.shape[1]
    bc_width = bc_input.shape[1] * bc_input.shape[2]
    taps = conv_input.shape[0]
    groups = bc_width // (2 * STATE)
    heads = decay_rate.shape[0]
    x_group = x_width // groups

    docs = doc_ids.reshape(1, rows_dev)
    row_block = rows // LEAD
    kv, bc = pl.pallas_call(
        prepare_kernel,
        grid=(1,),
        in_specs=[
            vmem(),
            vmem(),
            vmem(),
            pl.BlockSpec((LEAD, x_width), lambda t: (row_block - 1, 0)),
            pl.BlockSpec((LEAD, x_width), lambda t: (2 * row_block - 1, 0)),
            vmem(),
        ],
        out_specs=[vmem()] * 2,
        out_shape=[
            jax.ShapeDtypeStruct((rows_dev + 2 * EDGE, 2 * key_rows.shape[1]), BF),
            pltpu.VMEM((rows_dev, bc_width), BF),
        ],
        compiler_params=params(12),
        name="prepare",
    )(in_hbm(key_rows), in_hbm(value_rows), docs, in_hbm(ssm_input), in_hbm(ssm_input), in_hbm(bc_input))

    weight, query_rows, x_rows, kv_again = pl.pallas_call(
        load_kernel,
        in_specs=[anywhere()] * 3 + [vmem()],
        out_specs=[vmem()] * 4,
        out_shape=[
            pltpu.VMEM(out_weight.shape, BF),
            pltpu.VMEM(queries.shape, BF),
            pltpu.VMEM(ssm_input.shape, BF),
            jax.ShapeDtypeStruct(kv.shape, BF),
        ],
        scratch_shapes=[pltpu.SemaphoreType.DMA((6,))],
        compiler_params=params(10),
        cost_estimate=takes(5),
        name="load",
    )(in_hbm(out_weight), in_hbm(queries), in_hbm(ssm_input), kv)

    pieces = chip_gather(kv)
    pieces = pieces + [(1, swap(kv_again, 1))] + [(pattern ^ 1, swap(array, 1)) for pattern, array in pieces[1:]]

    expand = np.repeat(np.eye(heads, dtype=np.float32), x_width // heads, axis=1)
    expand = jnp.asarray(np.concatenate([expand, expand], axis=0), BF)
    pack_rows = STATE + 16
    full = lambda shape: pl.BlockSpec(shape, lambda h: (0,) * len(shape))
    half = lambda width: pl.BlockSpec((rows, width), lambda h: (h, 0))
    packed_spec = pl.BlockSpec((1, pack_rows, x_group), lambda h: (h, 0, 0))
    pair = [(i, i ^ 1) for i in range(4)]
    cross = [(i, i ^ 2) for i in range(4)]
    early_send, early_keep, kvs, docs_all, lead = attend(
        query_rows, weight, 0, [pattern for pattern, _ in pieces], [array for _, array in pieces]
    )
    early_pair = lax.ppermute(early_send, "head", pair)
    late_send, late_keep = attend(query_rows, weight, 1, None, [kvs, docs_all, early_keep])
    late_pair = lax.ppermute(late_send, "head", pair)
    xc, xt, mix, reach, keep, send = pl.pallas_call(
        functools.partial(local_kernel, count),
        grid=(2,),
        in_specs=[
            vmem(),
            vmem(),
            vmem(),
            vmem(),
            full((taps, x_width)),
            full(conv_bc.shape),
            pl.BlockSpec((heads, rows), lambda h: (0, h)),
            full((1, heads)),
            full((2 * heads, x_width)),
            anywhere(),
        ],
        out_specs=[half(x_width), half(x_width), half(groups * 2 * rows), half(heads), packed_spec, packed_spec],
        out_shape=[
            pltpu.HBM((rows_dev, x_width), BF),
            pltpu.HBM((rows_dev, x_width), BF),
            pltpu.HBM((rows_dev, groups * 2 * rows), BF),
            pltpu.HBM((rows_dev, heads), F32),
            jax.ShapeDtypeStruct((2, pack_rows, x_group), BF),
            jax.ShapeDtypeStruct((2, pack_rows, x_group), BF),
        ],
        scratch_shapes=[pltpu.VMEM((rows + LEAD, x_group), F32)],
        cost_estimate=takes(5.5),
        compiler_params=params(16 + count // 4),
        name="local_states",
    )(
        docs_all, lead, x_rows, bc, in_hbm(conv_input), in_hbm(conv_bc), in_hbm(step_size.T),
        decay_rate.reshape(1, heads), expand, late_keep,
    )

    early_cross, early_mine, send = pair_sum(early_pair, early_keep, send, True)
    other = swap(send, 1)
    early_got = lax.ppermute(early_cross, "head", cross)
    chip = pl.pallas_call(
        join_kernel,
        in_specs=[vmem(), vmem(), anywhere()],
        out_specs=vmem(),
        out_shape=jax.ShapeDtypeStruct(keep.shape, BF),
        compiler_params=params(12),
        cost_estimate=takes(0),
        name="join_states",
    )(keep, other, late_keep)
    late_cross, late_mine = pair_sum(late_pair, late_keep, early_got, False)
    late_got = lax.ppermute(late_cross, "head", cross)
    chip_pieces = chip_gather(chip)
    chips = count // 2
    state_shape = jax.ShapeDtypeStruct((2, STATE, x_group), BF)
    enter_mine, enter_other = pl.pallas_call(
        functools.partial(enter_kernel, [pattern for pattern, _ in chip_pieces], count),
        in_specs=[vmem(), vmem()] + [anywhere()] * (1 + len(chip_pieces)),
        out_specs=[vmem(), vmem()],
        out_shape=[state_shape, state_shape],
        scratch_shapes=[
            pltpu.VMEM((chips, pack_rows, x_group), BF),
            pltpu.VMEM((chips, pack_rows, x_group), BF),
            pltpu.SemaphoreType.DMA((2 * chips,)),
            pltpu.VMEM((STATE, x_group), F32),
        ],
        compiler_params=params(14 + chips),
        cost_estimate=takes(0),
        name="enter_states",
    )(keep, other, late_got, *[array for _, array in chip_pieces])
    enter_got = swap(enter_other, 1)

    ssm_out, finished = pl.pallas_call(
        finish_kernel,
        grid=(2,),
        in_specs=[
            half(x_width),
            half(x_width),
            half(groups * 2 * rows),
            half(heads),
            full((1, heads)),
            full((2 * heads, x_width)),
            vmem(),
            vmem(),
        ],
        out_specs=[half(x_width), full((8, 128))],
        out_shape=[pltpu.HBM((rows_dev, x_width), BF), jax.ShapeDtypeStruct((8, 128), F32)],
        scratch_shapes=[pltpu.VMEM((2 * rows, x_group), BF)],
        cost_estimate=takes(0),
        compiler_params=params(20),
        name="finish",
    )(xc, xt, mix, reach, skip_gain.reshape(1, heads), expand, enter_mine, enter_got)
    attn_out = pl.pallas_call(
        last_kernel,
        in_specs=[vmem()] * 4 + [anywhere()],
        out_specs=vmem(),
        out_shape=jax.ShapeDtypeStruct((rows // 2, out_weight.shape[1]), BF),
        compiler_params=params(6),
        cost_estimate=takes(0),
        name="last_sum",
    )(early_got, early_mine, late_got, late_mine, finished)
    return (attn_out, ssm_out)


def solution(mesh):
    in_specs = (
        P("seq", "head"),
        P("seq", "head"),
        P("seq", "head"),
        P("head", None),
        P("seq", "head"),
        P("seq", None, "head"),
        P(None, "head"),
        P(None, None, "head"),
        P("seq", "head"),
        P("head"),
        P("head"),
        P("seq"),
    )
    out_specs = (P(("seq", "head"), None), P("seq", "head"))
    return jax.shard_map(shards, mesh=mesh, in_specs=in_specs, out_specs=out_specs, check_vma=False)
```

time: 113 us -> 82.1 us (0.73)
  the two profiles are of different devices: /device:TPU:26 before, /device:TPU:0 now
where the time goes in v2:
time: 82.1 us; the launch traced here: 82 us
  waiting for transfers between devices  37.3 us (45%)
  Pallas kernels  25 us (30%)
  starting transfers between devices  18.3 us (22%)
    ppermute x12, waiting for transfers between devices, swap(): return lax.ppermute(x, 'seq', [(i, i ^ bit) for i in range(count)])  12.5 us
    ppermute x1, waiting for transfers between devices, shards(): late_got = lax.ppermute(late_cross, 'head', cross)  11.6 us
    ppermute x1, waiting for transfers between devices, shards(): late_pair = lax.ppermute(late_send, 'head', pair)  11 us
    ppermute x12, starting transfers between devices, swap(): return lax.ppermute(x, 'seq', [(i, i ^ bit) for i in range(count)])  9.27 us
    pallas_call x2, Pallas kernels, attend(): pl.pallas_call(functools.partial(attend_kernel, places, count, part), in_...  7.35 us
    pallas_call x1, Pallas kernels, shards(): pl.pallas_call(functools.partial(local_kernel, count), grid=(2,), in_spec...  6.38 us
    pallas_call x1, Pallas kernels, shards(): pl.pallas_call(load_kernel, in_specs=[anywhere()] * 3 + [vmem()], out_spe...  3.99 us
    ppermute x1, starting transfers between devices, shards(): late_got = lax.ppermute(late_cross, 'head', cross)  2.8 us
  transfers between devices with their start and end apart: 16, of which 10 were waited for; matrix products, arithmetic and copies ran while one was open for 0% of the time, Pallas kernels for 17%

profile of v2, /device:TPU:0, one launch (start us, length us, event | category | flops | bytes accessed | tf_op | source)
XLA Modules:
  0.0 82.0 jit_solution(9882063618260576325)
XLA Ops:
  0.6 0.7 copy-done.5
  1.3 1.9 %prepare.1 = (bf16[288,512]{1,0:T(8,128)(2,1)S(1)}, bf16[256,512]{1,0:T(8,128)(2,1)S(1)}) custom-call(bf16[256,256]{1,0:T(8,128)(2,1)} %k_ref.1, bf16[256,256]{1,0:T(8,128)(2,1)} %v_ref.1, s32[1,256]{1,0:T(1,128)S(1)} %bitcast.4, bf16[256,2048]{1,0:T(8,128)(2,1)} %x_ref.1, bf16[256,2048]{1,0:T(8,128)(2,1)} %x_ref.1, bf16[256,2,256]{2,1,0:T(2,128)(2,1)} %bc_ref.1), custom_call_target="tpu_custom_call" | custom-call | tf_op jit(solution)/shard_map/prepare/pallas_call | solution.py:564
  3.2 4.0 %collective-permute-start.2 = (bf16[288,512]{1,0:T(8,128)(2,1)S(1)}, bf16[288,512]{1,0:T(8,128)(2,1)S(1)}, u32[]{:S(2)}, u32[]{:S(2)}) collective-permute-start(bf16[288,512]{1,0:T(8,128)(2,1)S(1)} %get-tuple-element.30.kv_ref.rest_0_), channel_id=1, source_target_pairs={{0,24},{4,28},{8,16},{12,20},{16,8},{20,12},{24,0},{28,4},{1,25},{... | collective-permute-start | bytes 884744 | tf_op jit(solution)/shard_map/ppermute | solution.py:49
  7.2 0.5 collective-permute-start.1
  7.7 0.1 collective-permute-start
  7.9 4.0 %load.1 = (bf16[1024,4096]{1,0:T(8,128)(2,1)S(1)}, bf16[256,1024]{1,0:T(8,128)(2,1)S(1)}, bf16[256,2048]{1,0:T(8,128)(2,1)S(1)}, bf16[288,512]{1,0:T(8,128)(2,1)S(1)}) custom-call(bf16[1024,4096]{1,0:T(8,128)(2,1)} %w_ref.1, bf16[256,1024]{1,0:T(8,128)(2,1)} %q_ref.1, bf16[256,2048]{1,0:T(8,128)(2,1)} %x_ref.1, ...), custom_call_target="tpu_custom_call" | custom-call | flops 49999998976 | bytes 18500000 | tf_op jit(solution)/shard_map/load/pallas_call | solution.py:584
  11.9 3.2 %collective-permute-done.2.rest_3_ = bf16[288,512]{1,0:T(8,128)(2,1)S(1)} collective-permute-done((bf16[288,512]{1,0:T(8,128)(2,1)S(1)}, bf16[288,512]{1,0:T(8,128)(2,1)S(1)}, u32[]{:S(2)}, u32[]{:S(2)}) %collective-permute-start.2) | collective-permute-done | bytes 294944 | tf_op jit(solution)/shard_map/ppermute | solution.py:49
  15.1 5.4 %collective-permute-done.1.rest_2_ = bf16[288,512]{1,0:T(8,128)(2,1)S(1)} collective-permute-done((bf16[288,512]{1,0:T(8,128)(2,1)S(1)}, bf16[288,512]{1,0:T(8,128)(2,1)S(1)}, u32[]{:S(2)}, u32[]{:S(2)}) %collective-permute-start.1) | collective-permute-done | bytes 294944 | tf_op jit(solution)/shard_map/ppermute | solution.py:49
  20.6 0.3 collective-permute-done.rest_1_
  20.8 0.2 collective-permute-start.4
  21.1 1.1 %collective-permute-done.5.rest_6_ = bf16[288,512]{1,0:T(8,128)(2,1)S(1)} collective-permute-done((bf16[288,512]{1,0:T(8,128)(2,1)S(1)}, bf16[288,512]{1,0:T(8,128)(2,1)S(1)}, u32[]{:S(2)}, u32[]{:S(2)}) %collective-permute-start.5) | collective-permute-done | bytes 294944 | tf_op jit(solution)/shard_map/ppermute | solution.py:49
  22.1 0.4 collective-permute-done.4.rest_5_
  22.6 3.8 %attend_early.1 = (bf16[64,4096]{1,0:T(8,128)(2,1)S(1)}, bf16[64,4096]{1,0:T(8,128)(2,1)S(1)}, bf16[2048,512]{1,0:T(8,128)(2,1)S(1)}, f32[8,256]{1,0:T(8,128)S(1)}, bf16[2,16,512]{2,1,0:T(8,128)(2,1)S(1)}) custom-call(bf16[256,1024]{1,0:T(8,128)(2,1)S(1)} %get-tuple-element.31.q_ref, bf16[1024,4096]{1,0:T(8,128)(2,1)S(1)} %get-tuple-element.32.w_ref, ...), custom_call_target="tpu_custom_call" | custom-call | flops 80000000000 | bytes 29600000 | tf_op jit(solution)/shard_map/attend_early/pallas_call | solution.py:217
  26.4 1.8 %collective-permute-start.7 = (bf16[64,4096]{1,0:T(8,128)(2,1)S(1)}, bf16[64,4096]{1,0:T(8,128)(2,1)S(1)}, u32[]{:S(2)}, u32[]{:S(2)}) collective-permute-start(bf16[64,4096]{1,0:T(8,128)(2,1)S(1)} %get-tuple-element.34), channel_id=1, source_target_pairs={{0,1},{1,0},{2,3},{3,2},{4,5},{5,4},{6,7},{7,6},{8,9},{9,8},{10,11... | collective-permute-start | bytes 1572872 | tf_op jit(solution)/shard_map/ppermute | solution.py:614
  28.2 3.6 %attend_late.1 = (bf16[64,4096]{1,0:T(8,128)(2,1)S(1)}, bf16[64,4096]{1,0:T(8,128)(2,1)S(1)}) custom-call(bf16[256,1024]{1,0:T(8,128)(2,1)S(1)} %get-tuple-element.31.q_ref, bf16[1024,4096]{1,0:T(8,128)(2,1)S(1)} %get-tuple-element.32.w_ref, bf16[2048,512]{1,0:T(8,128)(2,1)S(1)} %get-tuple-element.40.rest_0_, ...), custom_call_target="tpu_custom_call" | custom-call | flops 80000000000 | bytes 29600000 | tf_op jit(solution)/shard_map/attend_late/pallas_call | solution.py:217
  31.8 6.4 %local_states.1 = (bf16[256,2048]{1,0:T(8,128)(2,1)}, bf16[256,2048]{1,0:T(8,128)(2,1)}, bf16[256,512]{1,0:T(8,128)(2,1)}, f32[256,32]{1,0:T(8,128)}, bf16[2,144...) custom-call(f32[8,256]{1,0:T(8,128)S(1)} %get-tuple-element.36.rest_1_.docs_ref, ...), custom_call_target="tpu_custom_call" | custom-call | flops 54999998464 | bytes 20350000 | tf_op jit(solution)/shard_map/local_states/pallas_call | solution.py:617
  38.2 2.2 %collective-permute-done.7.got_ref = bf16[64,4096]{1,0:T(8,128)(2,1)S(1)} collective-permute-done((bf16[64,4096]{1,0:T(8,128)(2,1)S(1)}, bf16[64,4096]{1,0:T(8,128)(2,1)S(1)}, u32[]{:S(2)}, u32[]{:S(2)}) %collective-permute-start.7) | collective-permute-done | bytes 524320 | tf_op jit(solution)/shard_map/ppermute | solution.py:614
  40.4 0.2 pair_sum.2
  40.6 1.8 %collective-permute-start.9 = (bf16[64,4096]{1,0:T(8,128)(2,1)S(1)}, bf16[64,4096]{1,0:T(8,128)(2,1)S(1)}, u32[]{:S(2)}, u32[]{:S(2)}) collective-permute-start(bf16[64,4096]{1,0:T(8,128)(2,1)S(1)} %get-tuple-element.45), channel_id=1, source_target_pairs={{0,1},{1,0},{2,3},{3,2},{4,5},{5,4},{6,7},{7,6},{8,9},{9,8},{10,11... | collective-permute-start | bytes 1572872 | tf_op jit(solution)/shard_map/ppermute | solution.py:616
  42.4 0.2 collective-permute-done.11.other_ref
  42.6 0.2 join_states.1.rest_0_
  42.8 2.8 %collective-permute-start.14 = (bf16[2,144,1024]{2,1,0:T(8,128)(2,1)S(1)}, bf16[2,144,1024]{2,1,0:T(8,128)(2,1)S(1)}, u32[]{:S(2)}, u32[]{:S(2)}) collective-permute-start(bf16[2,144,1024]{2,1,0:T(8,128)(2,1)S(1)} %join_states.1.rest_0_), channel_id=1, source_target_pairs={{0,24},{4,28},{8,16},{12,20},{16,8},{20,12},{24,0},{28,4},{1,25},{... | collective-permute-start | bytes 1769480 | tf_op jit(solution)/shard_map/ppermute | solution.py:49
  45.7 0.9 %collective-permute-start.13 = (bf16[2,144,1024]{2,1,0:T(8,128)(2,1)S(1)}, bf16[2,144,1024]{2,1,0:T(8,128)(2,1)S(1)}, u32[]{:S(2)}, u32[]{:S(2)}) collective-permute-start(bf16[2,144,1024]{2,1,0:T(8,128)(2,1)S(1)} %join_states.1.rest_0_), channel_id=1, source_target_pairs={{0,16},{4,20},{8,24},{12,28},{16,0},{20,4},{24,8},{28,12},{1,17},{... | collective-permute-start | bytes 1769480 | tf_op jit(solution)/shard_map/ppermute | solution.py:49
  46.5 0.5 collective-permute-start.12
  47.0 2.6 %collective-permute-start.8 = (bf16[32,4096]{1,0:T(8,128)(2,1)S(1)}, bf16[32,4096]{1,0:T(8,128)(2,1)S(1)}, u32[]{:S(2)}, u32[]{:S(2)}) collective-permute-start(bf16[32,4096]{1,0:T(8,128)(2,1)S(1)} %get-tuple-element.43), channel_id=1, source_target_pairs={{0,2},{1,3},{2,0},{3,1},{4,6},{5,7},{6,4},{7,5},{8,10},{9,11},{10,... | collective-permute-start | bytes 786440 | tf_op jit(solution)/shard_map/ppermute | solution.py:652
  49.6 11.0 %collective-permute-done.9.got_ref = bf16[64,4096]{1,0:T(8,128)(2,1)S(1)} collective-permute-done((bf16[64,4096]{1,0:T(8,128)(2,1)S(1)}, bf16[64,4096]{1,0:T(8,128)(2,1)S(1)}, u32[]{:S(2)}, u32[]{:S(2)}) %collective-permute-start.9) | collective-permute-done | bytes 524320 | tf_op jit(solution)/shard_map/ppermute | solution.py:616
  60.7 2.8 %collective-permute-start.10 = (bf16[32,4096]{1,0:T(8,128)(2,1)S(1)}, bf16[32,4096]{1,0:T(8,128)(2,1)S(1)}, u32[]{:S(2)}, u32[]{:S(2)}) collective-permute-start(bf16[32,4096]{1,0:T(8,128)(2,1)S(1)} %get-tuple-element.46), channel_id=1, source_target_pairs={{0,2},{1,3},{2,0},{3,1},{4,6},{5,7},{6,4},{7,5},{8,10},{9,11},{10,... | collective-permute-start | bytes 786440 | tf_op jit(solution)/shard_map/ppermute | solution.py:663
  63.5 11.6 %collective-permute-done.10.after_ref.late_got = bf16[32,4096]{1,0:T(8,128)(2,1)S(1)} collective-permute-done((bf16[32,4096]{1,0:T(8,128)(2,1)S(1)}, bf16[32,4096]{1,0:T(8,128)(2,1)S(1)}, u32[]{:S(2)}, u32[]{:S(2)}) %collective-permute-start.10) | collective-permute-done | bytes 262176 | tf_op jit(solution)/shard_map/ppermute | solution.py:663
  75.1 1.4 %enter_states.1 = (bf16[2,128,1024]{2,1,0:T(8,128)(2,1)S(1)}, bf16[2,128,1024]{2,1,0:T(8,128)(2,1)S(1)}) custom-call(bf16[2,144,1024]{2,1,0:T(8,128)(2,1)S(1)} %get-tuple-element.52.mine_ref, bf16[2,144,1024]{2,1,0:T(8,128)(2,1)S(1)} %collective-permute-done.11.other_ref, bf16[32,4096]{1,0:T(8,128)(2,1)S(1)} %collective-permute-done.10.after_ref.late_got, ...), custom_call_target="tpu_custom_call" | custom-call | tf_op jit(solution)/shard_map/enter_states/pallas_call | solution.py:667
  76.6 1.9 %collective-permute-done.15.other_ref = bf16[2,128,1024]{2,1,0:T(8,128)(2,1)S(1)} collective-permute-done((bf16[2,128,1024]{2,1,0:T(8,128)(2,1)S(1)}, bf16[2,128,1024]{2,1,0:T(8,128)(2,1)S(1)}, u32[]{:S(2)}, u32[]{:S(2)}) %collective-permute-start.15) | collective-permute-done | bytes 524320 | tf_op jit(solution)/shard_map/ppermute | solution.py:49
  78.5 2.5 %finish.1 = (bf16[256,2048]{1,0:T(8,128)(2,1)}, f32[8,128]{1,0:T(8,128)S(1)}) custom-call(bf16[256,2048]{1,0:T(8,128)(2,1)S(1)} %copy-done, bf16[256,2048]{1,0:T(8,128)(2,1)S(1)} %copy-done.1, bf16[256,512]{1,0:T(8,128)(2,1)S(1)} %copy-done.3, f32[256,32]{1,0:T(8,128)S(1)} %copy-done.4, f32[1,32]{1,0:T(1,128)S(1)} %bitcast.5, ...), custom_call_target="tpu_custom_call" | custom-call | tf_op jit(solution)/shard_map/finish/pallas_call | solution.py:684
  81.1 0.9 %last_sum.1 = bf16[64,4096]{1,0:T(8,128)(2,1)} custom-call(bf16[32,4096]{1,0:T(8,128)(2,1)S(1)} %collective-permute-done.8.after_ref.early_got, bf16[32,4096]{1,0:T(8,128)(2,1)S(1)} %get-tuple-element.44.early_keep, bf16[32,4096]{1,0:T(8,128)(2,1)S(1)} %collective-permute-done.10.after_ref.late_got, bf16[32,4096]{1,0:T(8,128)(2,1)S(1)} %get-tuple-element.47.late_keep, ...), custom_call_target="tpu_custom_call" | custom-call | tf_op jit(solution)/shard_map/last_sum/pallas_call | solution.py:704
  (27 shorter events, 0.4 us)
Async XLA Ops:
  0.6 0.7 copy-start.5
  3.2 11.9 %collective-permute-start.2 = (bf16[288,512]{1,0:T(8,128)(2,1)S(1)}, bf16[288,512]{1,0:T(8,128)(2,1)S(1)}, u32[]{:S(2)}, u32[]{:S(2)}) collective-permute-start(bf16[288,512]{1,0:T(8,128)(2,1)S(1)} %get-tuple-element.30.kv_ref.rest_0_), channel_id=1, source_target_pairs={{0,24},{4,28},{8,16},{12,20},{16,8},{20,12},{24,0},{28,4},{1,25},{... | collective-permute-start | bytes 884744 | tf_op jit(solution)/shard_map/ppermute | solution.py:49
  7.2 13.3 %collective-permute-start.1 = (bf16[288,512]{1,0:T(8,128)(2,1)S(1)}, bf16[288,512]{1,0:T(8,128)(2,1)S(1)}, u32[]{:S(2)}, u32[]{:S(2)}) collective-permute-start(bf16[288,512]{1,0:T(8,128)(2,1)S(1)} %get-tuple-element.30.kv_ref.rest_0_), channel_id=1, source_target_pairs={{0,16},{4,20},{8,24},{12,28},{16,0},{20,4},{24,8},{28,12},{1,17},{... | collective-permute-start | bytes 884744 | tf_op jit(solution)/shard_map/ppermute | solution.py:49
  7.7 13.1 %collective-permute-start = (bf16[288,512]{1,0:T(8,128)(2,1)S(1)}, bf16[288,512]{1,0:T(8,128)(2,1)S(1)}, u32[]{:S(2)}, u32[]{:S(2)}) collective-permute-start(bf16[288,512]{1,0:T(8,128)(2,1)S(1)} %get-tuple-element.30.kv_ref.rest_0_), channel_id=1, source_target_pairs={{0,8},{4,12},{8,0},{12,4},{16,24},{20,28},{24,16},{28,20},{1,9},{5... | collective-permute-start | bytes 884744 | tf_op jit(solution)/shard_map/ppermute | solution.py:49
  11.9 9.2 %collective-permute-start.3 = (bf16[288,512]{1,0:T(8,128)(2,1)S(1)}, bf16[288,512]{1,0:T(8,128)(2,1)S(1)}, u32[]{:S(2)}, u32[]{:S(2)}) collective-permute-start(bf16[288,512]{1,0:T(8,128)(2,1)S(1)} %get-tuple-element.33), channel_id=1, source_target_pairs={{0,4},{4,0},{8,12},{12,8},{16,20},{20,16},{24,28},{28,24},{1,5},{5... | collective-permute-start | bytes 884744 | tf_op jit(solution)/shard_map/ppermute | solution.py:49
  15.1 5.9 %collective-permute-start.6 = (bf16[288,512]{1,0:T(8,128)(2,1)S(1)}, bf16[288,512]{1,0:T(8,128)(2,1)S(1)}, u32[]{:S(2)}, u32[]{:S(2)}) collective-permute-start(bf16[288,512]{1,0:T(8,128)(2,1)S(1)} %collective-permute-done.2.rest_3_), channel_id=1, source_target_pairs={{0,4},{4,0},{8,12},{12,8},{16,20},{20,16},{24,28},{28,24},{1,5},{5... | collective-permute-start | bytes 884744 | tf_op jit(solution)/shard_map/ppermute | solution.py:49
  20.5 1.6 %collective-permute-start.5 = (bf16[288,512]{1,0:T(8,128)(2,1)S(1)}, bf16[288,512]{1,0:T(8,128)(2,1)S(1)}, u32[]{:S(2)}, u32[]{:S(2)}) collective-permute-start(bf16[288,512]{1,0:T(8,128)(2,1)S(1)} %collective-permute-done.1.rest_2_), channel_id=1, source_target_pairs={{0,4},{4,0},{8,12},{12,8},{16,20},{20,16},{24,28},{28,24},{1,5},{5... | collective-permute-start | bytes 884744 | tf_op jit(solution)/shard_map/ppermute | solution.py:49
  20.8 1.7 %collective-permute-start.4 = (bf16[288,512]{1,0:T(8,128)(2,1)S(1)}, bf16[288,512]{1,0:T(8,128)(2,1)S(1)}, u32[]{:S(2)}, u32[]{:S(2)}) collective-permute-start(bf16[288,512]{1,0:T(8,128)(2,1)S(1)} %collective-permute-done.rest_1_), channel_id=1, source_target_pairs={{0,4},{4,0},{8,12},{12,8},{16,20},{20,16},{24,28},{28,24},{1,5},{5... | collective-permute-start | bytes 884744 | tf_op jit(solution)/shard_map/ppermute | solution.py:49
  26.4 14.0 %collective-permute-start.7 = (bf16[64,4096]{1,0:T(8,128)(2,1)S(1)}, bf16[64,4096]{1,0:T(8,128)(2,1)S(1)}, u32[]{:S(2)}, u32[]{:S(2)}) collective-permute-start(bf16[64,4096]{1,0:T(8,128)(2,1)S(1)} %get-tuple-element.34), channel_id=1, source_target_pairs={{0,1},{1,0},{2,3},{3,2},{4,5},{5,4},{6,7},{7,6},{8,9},{9,8},{10,11... | collective-permute-start | bytes 1572872 | tf_op jit(solution)/shard_map/ppermute | solution.py:614
  28.2 3.6 %copy-start.2 = (bf16[64,2048]{1,0:T(8,128)(2,1)S(1)}, bf16[64,2048]{1,0:T(8,128)(2,1)}, u32[]{:S(2)}) copy-start(bf16[64,2048]{1,0:T(8,128)(2,1)} %constant.2.clone.expand_ref) | copy-start | bytes 786436
  28.2 3.6 %copy-start.7 = (f32[32]{0:T(128)S(1)}, f32[32]{0:T(128)}, u32[]{:S(2)}) copy-start(f32[32]{0:T(128)} %param.22) | copy-start | bytes 388
  38.1 40.3 %copy-start = (bf16[256,2048]{1,0:T(8,128)(2,1)S(1)}, bf16[256,2048]{1,0:T(8,128)(2,1)}, u32[]{:S(2)}) copy-start(bf16[256,2048]{1,0:T(8,128)(2,1)} %get-tuple-element.48.xc_ref) | copy-start | bytes 3145732
  38.1 40.3 %copy-start.1 = (bf16[256,2048]{1,0:T(8,128)(2,1)S(1)}, bf16[256,2048]{1,0:T(8,128)(2,1)}, u32[]{:S(2)}) copy-start(bf16[256,2048]{1,0:T(8,128)(2,1)} %get-tuple-element.49.xt_ref) | copy-start | bytes 3145732
  38.1 40.3 %copy-start.3 = (bf16[256,512]{1,0:T(8,128)(2,1)S(1)}, bf16[256,512]{1,0:T(8,128)(2,1)}, u32[]{:S(2)}) copy-start(bf16[256,512]{1,0:T(8,128)(2,1)} %get-tuple-element.50.mix_ref) | copy-start | bytes 786436
  38.2 40.3 %copy-start.4 = (f32[256,32]{1,0:T(8,128)S(1)}, f32[256,32]{1,0:T(8,128)}, u32[]{:S(2)}) copy-start(f32[256,32]{1,0:T(8,128)} %get-tuple-element.51.reach_ref) | copy-start | bytes 98308
  38.2 40.3 %copy-start.6 = (f32[32]{0:T(128)S(1)}, f32[32]{0:T(128)}, u32[]{:S(2)}) copy-start(f32[32]{0:T(128)} %param.23) | copy-start | bytes 388
  40.6 2.1 %collective-permute-start.11 = (bf16[2,144,1024]{2,1,0:T(8,128)(2,1)S(1)}, bf16[2,144,1024]{2,1,0:T(8,128)(2,1)S(1)}, u32[]{:S(2)}, u32[]{:S(2)}) collective-permute-start(bf16[2,144,1024]{2,1,0:T(8,128)(2,1)S(1)} %get-tuple-element.53), channel_id=1, source_target_pairs={{0,4},{4,0},{8,12},{12,8},{16,20},{20,16},{24,28},{28,24},{1,5},{5... | collective-permute-start | bytes 1769480 | tf_op jit(solution)/shard_map/ppermute | solution.py:49
  40.6 19.9 %collective-permute-start.9 = (bf16[64,4096]{1,0:T(8,128)(2,1)S(1)}, bf16[64,4096]{1,0:T(8,128)(2,1)S(1)}, u32[]{:S(2)}, u32[]{:S(2)}) collective-permute-start(bf16[64,4096]{1,0:T(8,128)(2,1)S(1)} %get-tuple-element.45), channel_id=1, source_target_pairs={{0,1},{1,0},{2,3},{3,2},{4,5},{5,4},{6,7},{7,6},{8,9},{9,8},{10,11... | collective-permute-start | bytes 1572872 | tf_op jit(solution)/shard_map/ppermute | solution.py:616
  42.8 32.3 %collective-permute-start.14 = (bf16[2,144,1024]{2,1,0:T(8,128)(2,1)S(1)}, bf16[2,144,1024]{2,1,0:T(8,128)(2,1)S(1)}, u32[]{:S(2)}, u32[]{:S(2)}) collective-permute-start(bf16[2,144,1024]{2,1,0:T(8,128)(2,1)S(1)} %join_states.1.rest_0_), channel_id=1, source_target_pairs={{0,24},{4,28},{8,16},{12,20},{16,8},{20,12},{24,0},{28,4},{1,25},{... | collective-permute-start | bytes 1769480 | tf_op jit(solution)/shard_map/ppermute | solution.py:49
  45.7 29.5 %collective-permute-start.13 = (bf16[2,144,1024]{2,1,0:T(8,128)(2,1)S(1)}, bf16[2,144,1024]{2,1,0:T(8,128)(2,1)S(1)}, u32[]{:S(2)}, u32[]{:S(2)}) collective-permute-start(bf16[2,144,1024]{2,1,0:T(8,128)(2,1)S(1)} %join_states.1.rest_0_), channel_id=1, source_target_pairs={{0,16},{4,20},{8,24},{12,28},{16,0},{20,4},{24,8},{28,12},{1,17},{... | collective-permute-start | bytes 1769480 | tf_op jit(solution)/shard_map/ppermute | solution.py:49
  46.5 28.6 %collective-permute-start.12 = (bf16[2,144,1024]{2,1,0:T(8,128)(2,1)S(1)}, bf16[2,144,1024]{2,1,0:T(8,128)(2,1)S(1)}, u32[]{:S(2)}, u32[]{:S(2)}) collective-permute-start(bf16[2,144,1024]{2,1,0:T(8,128)(2,1)S(1)} %join_states.1.rest_0_), channel_id=1, source_target_pairs={{0,8},{4,12},{8,0},{12,4},{16,24},{20,28},{24,16},{28,20},{1,9},{5... | collective-permute-start | bytes 1769480 | tf_op jit(solution)/shard_map/ppermute | solution.py:49
  47.0 13.6 %collective-permute-start.8 = (bf16[32,4096]{1,0:T(8,128)(2,1)S(1)}, bf16[32,4096]{1,0:T(8,128)(2,1)S(1)}, u32[]{:S(2)}, u32[]{:S(2)}) collective-permute-start(bf16[32,4096]{1,0:T(8,128)(2,1)S(1)} %get-tuple-element.43), channel_id=1, source_target_pairs={{0,2},{1,3},{2,0},{3,1},{4,6},{5,7},{6,4},{7,5},{8,10},{9,11},{10,... | collective-permute-start | bytes 786440 | tf_op jit(solution)/shard_map/ppermute | solution.py:652
  60.7 14.4 %collective-permute-start.10 = (bf16[32,4096]{1,0:T(8,128)(2,1)S(1)}, bf16[32,4096]{1,0:T(8,128)(2,1)S(1)}, u32[]{:S(2)}, u32[]{:S(2)}) collective-permute-start(bf16[32,4096]{1,0:T(8,128)(2,1)S(1)} %get-tuple-element.46), channel_id=1, source_target_pairs={{0,2},{1,3},{2,0},{3,1},{4,6},{5,7},{6,4},{7,5},{8,10},{9,11},{10,... | collective-permute-start | bytes 786440 | tf_op jit(solution)/shard_map/ppermute | solution.py:663
  76.5 2.0 %collective-permute-start.15 = (bf16[2,128,1024]{2,1,0:T(8,128)(2,1)S(1)}, bf16[2,128,1024]{2,1,0:T(8,128)(2,1)S(1)}, u32[]{:S(2)}, u32[]{:S(2)}) collective-permute-start(bf16[2,128,1024]{2,1,0:T(8,128)(2,1)S(1)} %get-tuple-element.55), channel_id=1, source_target_pairs={{0,4},{4,0},{8,12},{12,8},{16,20},{20,16},{24,28},{28,24},{1,5},{5... | collective-permute-start | bytes 1572872 | tf_op jit(solution)/shard_map/ppermute | solution.py:49

commit v3 on v2

--- a/solution.py
+++ b/solution.py
@@ -268,26 +268,24 @@
     )(got, keep, after)
 
 
-def last_kernel(early_got, early_keep, late_got, late_keep, after_ref, out_ref):
+def last_kernel(early_got, early_keep, late_got, late_keep, after_ref, out_ref, done_ref):
+    done_ref[...] = jnp.zeros(done_ref.shape, F32)
     rows = early_got.shape[0]
     out_ref[:rows] = (early_got[...].astype(F32) + early_keep[...].astype(F32)).astype(BF)
     out_ref[rows:] = (late_got[...].astype(F32) + late_keep[...].astype(F32)).astype(BF)
 
 
-def prepare_kernel(k_ref, v_ref, docs_ref, xf_ref, xb_ref, bc_ref, kv_ref, flat_ref):
+def prepare_kernel(k_ref, v_ref, docs_ref, xf_ref, xb_ref, bf_ref, bb_ref, kv_ref):
     rows = k_ref.shape[0] // 2
     width = k_ref.shape[1]
-    part = bc_ref.shape[2]
-    for at in range(2):
-        flat_ref[:, at * part : (at + 1) * part] = bc_ref[:, at, :]
     docs = jnp.broadcast_to(docs_ref[...], (LEAD, 2 * rows)).astype(F32)[:1]
     docs = jnp.concatenate([docs, jnp.zeros((1, 2 * width - 2 * rows), F32)], axis=1)
-    for half, x_ref in ((0, xf_ref), (1, xb_ref)):
+    for half, x_ref, bc_ref in ((0, xf_ref, bf_ref), (1, xb_ref, bb_ref)):
         first = half * (rows + EDGE)
         kv_ref[first : first + rows, :width] = k_ref[half * rows : (half + 1) * rows]
         kv_ref[first : first + rows, width:] = v_ref[half * rows : (half + 1) * rows]
         x_edge = x_ref[...].astype(F32)
-        bc_edge = flat_ref[(half + 1) * rows - LEAD : (half + 1) * rows].astype(F32)
+        bc_edge = jnp.concatenate([bc_ref[:, 0, :], bc_ref[:, 1, :]], axis=1).astype(F32)
         lines = []
         for t in range(LEAD - 3, LEAD):
             for edge in (x_edge, bc_edge):
@@ -295,7 +293,9 @@
         kv_ref[first + rows : first + rows + EDGE] = jnp.concatenate(lines + [docs], axis=0).astype(BF)
 
 
-def load_kernel(w_ref, q_ref, x_ref, kv_ref, w_out, q_out, x_out, kv_out, sems):
+def load_kernel(w_ref, q_ref, x_ref, bc_ref, kv_ref, w_out, q_out, x_out, bc_out, kv_out, bc_in, sems):
+    bc_copy = pltpu.make_async_copy(bc_ref, bc_in, sems.at[6])
+    bc_copy.start()
     copies = [
         pltpu.make_async_copy(q_ref, q_out, sems.at[0]),
         pltpu.make_async_copy(x_ref, x_out, sems.at[5]),
@@ -308,6 +308,10 @@
     for copy in copies:
         copy.start()
     kv_out[...] = kv_ref[...]
+    bc_copy.wait()
+    part = bc_in.shape[2]
+    for at in range(2):
+        bc_out[:, at * part : (at + 1) * part] = bc_in[:, at, :]
     for copy in copies:
         copy.wait()
 
@@ -386,8 +390,6 @@
     fade_end = spread(reach[rows - 8 :], expand)[7:8]
     carries = jnp.max(jnp.where(end_doc == last_doc, 1.0, 0.0))
     fade = fade_end * carries
-    fade_high = fade.astype(BF)
-    fade_low = (fade - fade_high.astype(F32)).astype(BF)
     allowed = lower & (own_col == own)
     for g in range(groups):
         lanes = slice(g * x_group, (g + 1) * x_group)
@@ -402,37 +404,31 @@
         mix_ref[:, g * 2 * rows + rows : (g + 1) * 2 * rows] = (c.astype(F32) * alive).astype(BF)
         b_t = jnp.transpose(b.astype(F32) * ending).astype(BF)
         state = jnp.dot(b_t, xt, preferred_element_type=F32) * fade_end[:, lanes]
-        packed = jnp.concatenate(
-            [
-                state.astype(BF),
-                jnp.broadcast_to(fade_high[:, lanes], (8, x_group)),
-                jnp.broadcast_to(fade_low[:, lanes], (8, x_group)),
-            ],
-            axis=0,
-        )
+        state = state.astype(BF)
+        tail = fade_rows(fade[:, lanes])
 
         @pl.when(core == g)
-        def _(packed=packed):
-            keep_ref[0] = packed
+        def _(state=state, tail=tail):
+            keep_ref[0, :STATE] = state
+            keep_ref[0, STATE:] = tail
 
         @pl.when(core != g)
-        def _(packed=packed):
-            send_ref[0] = packed
+        def _(state=state, tail=tail):
+            send_ref[0, :STATE] = state
+            send_ref[0, STATE:] = tail
 
 
 def unpack(packed):
     state = packed[:STATE].astype(F32)
-    fade = packed[STATE : STATE + 1].astype(F32) + packed[STATE + 8 : STATE + 9].astype(F32)
-    return fade, state
-
-
-def pack(fade, state):
-    high = fade.astype(BF)
-    low = (fade - high.astype(F32)).astype(BF)
-    shape = (8, state.shape[1])
-    return jnp.concatenate(
-        [state.astype(BF), jnp.broadcast_to(high, shape), jnp.broadcast_to(low, shape)], axis=0
-    )
+    tail = packed[STATE : STATE + LEAD].astype(F32)
+    return tail[:1] + tail[LEAD - 1 :], state
+
+
+def fade_rows(fade):
+    high = fade.astype(BF).astype(F32)
+    shape = (LEAD // 2, fade.shape[1])
+    parts = [jnp.broadcast_to(high, shape), jnp.broadcast_to(fade - high, shape)]
+    return jnp.concatenate(parts, axis=0).astype(BF)
 
 
 def join_kernel(mine_ref, other_ref, after_ref, out_ref):
@@ -440,18 +436,19 @@
     for half in range(2):
         first_is_mine = core == half
 
-        def joined(first, second):
+        def joined(first, second, half=half):
             fade_a, state_a = unpack(first)
             fade_b, state_b = unpack(second)
-            return pack(fade_a * fade_b, fade_b * state_a + state_b)
+            out_ref[half, :STATE] = (fade_b * state_a + state_b).astype(BF)
+            out_ref[half, STATE:] = fade_rows(fade_a * fade_b)
 
         @pl.when(first_is_mine)
         def _(half=half):
-            out_ref[half] = joined(mine_ref[half], other_ref[half])
+            joined(mine_ref[half], other_ref[half])
 
         @pl.when(jnp.logical_not(first_is_mine))
         def _(half=half):
-            out_ref[half] = joined(other_ref[half], mine_ref[half])
+            joined(other_ref[half], mine_ref[half])
 
 
 def enter_kernel(places, count, mine_ref, other_ref, after_ref, *rest):
@@ -517,9 +514,8 @@
 
 
 def finish_kernel(
-    xc_ref, xt_ref, mix_ref, reach_ref, skip_ref, expand_ref, mine_ref, other_ref, out_ref, done_ref, both
+    xc_ref, xt_ref, mix_ref, reach_ref, skip_ref, expand_ref, mine_ref, other_ref, after_ref, out_ref, both
 ):
-    done_ref[...] = jnp.zeros(done_ref.shape, F32)
     core = lax.rem(lax.axis_index("seq"), 2)
     half = pl.program_id(0)
     rows, x_width = out_ref.shape
@@ -561,7 +557,7 @@
 
     docs = doc_ids.reshape(1, rows_dev)
     row_block = rows // LEAD
-    kv, bc = pl.pallas_call(
+    kv = pl.pallas_call(
         prepare_kernel,
         grid=(1,),
         in_specs=[
@@ -570,39 +566,41 @@
             vmem(),
             pl.BlockSpec((LEAD, x_width), lambda t: (row_block - 1, 0)),
             pl.BlockSpec((LEAD, x_width), lambda t: (2 * row_block - 1, 0)),
-            vmem(),
+            pl.BlockSpec((LEAD,) + bc_input.shape[1:], lambda t: (row_block - 1, 0, 0)),
+            pl.BlockSpec((LEAD,) + bc_input.shape[1:], lambda t: (2 * row_block - 1, 0, 0)),
         ],
-        out_specs=[vmem()] * 2,
-        out_shape=[
-            jax.ShapeDtypeStruct((rows_dev + 2 * EDGE, 2 * key_rows.shape[1]), BF),
-            pltpu.VMEM((rows_dev, bc_width), BF),
-        ],
+        out_specs=vmem(),
+        out_shape=jax.ShapeDtypeStruct((rows_dev + 2 * EDGE, 2 * key_rows.shape[1]), BF),
         compiler_params=params(12),
         name="prepare",
-    )(in_hbm(key_rows), in_hbm(value_rows), docs, in_hbm(ssm_input), in_hbm(ssm_input), in_hbm(bc_input))
-
-    weight, query_rows, x_rows, kv_again = pl.pallas_call(
+    )(
+        in_hbm(key_rows), in_hbm(value_rows), in_hbm(docs), in_hbm(ssm_input), in_hbm(ssm_input),
+        in_hbm(bc_input), in_hbm(bc_input),
+    )
+
+    weight, query_rows, x_rows, bc, kv_again = pl.pallas_call(
         load_kernel,
-        in_specs=[anywhere()] * 3 + [vmem()],
-        out_specs=[vmem()] * 4,
+        in_specs=[anywhere()] * 4 + [vmem()],
+        out_specs=[vmem()] * 5,
         out_shape=[
             pltpu.VMEM(out_weight.shape, BF),
             pltpu.VMEM(queries.shape, BF),
             pltpu.VMEM(ssm_input.shape, BF),
+            pltpu.VMEM((rows_dev, bc_width), BF),
             jax.ShapeDtypeStruct(kv.shape, BF),
         ],
-        scratch_shapes=[pltpu.SemaphoreType.DMA((6,))],
+        scratch_shapes=[pltpu.VMEM(bc_input.shape, BF), pltpu.SemaphoreType.DMA((7,))],
         compiler_params=params(10),
         cost_estimate=takes(5),
         name="load",
-    )(in_hbm(out_weight), in_hbm(queries), in_hbm(ssm_input), kv)
+    )(in_hbm(out_weight), in_hbm(queries), in_hbm(ssm_input), in_hbm(bc_input), kv)
 
     pieces = chip_gather(kv)
     pieces = pieces + [(1, swap(kv_again, 1))] + [(pattern ^ 1, swap(array, 1)) for pattern, array in pieces[1:]]
 
     expand = np.repeat(np.eye(heads, dtype=np.float32), x_width // heads, axis=1)
     expand = jnp.asarray(np.concatenate([expand, expand], axis=0), BF)
-    pack_rows = STATE + 16
+    pack_rows = STATE + LEAD
     full = lambda shape: pl.BlockSpec(shape, lambda h: (0,) * len(shape))
     half = lambda width: pl.BlockSpec((rows, width), lambda h: (h, 0))
     packed_spec = pl.BlockSpec((1, pack_rows, x_group), lambda h: (h, 0, 0))
@@ -681,7 +679,19 @@
     )(keep, other, late_got, *[array for _, array in chip_pieces])
     enter_got = swap(enter_other, 1)
 
-    ssm_out, finished = pl.pallas_call(
+    attn_out, summed = pl.pallas_call(
+        last_kernel,
+        in_specs=[vmem()] * 4 + [anywhere()],
+        out_specs=[vmem()] * 2,
+        out_shape=[
+            jax.ShapeDtypeStruct((rows // 2, out_weight.shape[1]), BF),
+            jax.ShapeDtypeStruct((8, 128), F32),
+        ],
+        compiler_params=params(6),
+        cost_estimate=takes(0),
+        name="last_sum",
+    )(early_got, early_mine, late_got, late_mine, enter_other)
+    ssm_out = pl.pallas_call(
         finish_kernel,
         grid=(2,),
         in_specs=[
@@ -693,23 +703,15 @@
             full((2 * heads, x_width)),
             vmem(),
             vmem(),
+            anywhere(),
         ],
-        out_specs=[half(x_width), full((8, 128))],
-        out_shape=[pltpu.HBM((rows_dev, x_width), BF), jax.ShapeDtypeStruct((8, 128), F32)],
+        out_specs=half(x_width),
+        out_shape=pltpu.HBM((rows_dev, x_width), BF),
         scratch_shapes=[pltpu.VMEM((2 * rows, x_group), BF)],
         cost_estimate=takes(0),
         compiler_params=params(20),
         name="finish",
-    )(xc, xt, mix, reach, skip_gain.reshape(1, heads), expand, enter_mine, enter_got)
-    attn_out = pl.pallas_call(
-        last_kernel,
-        in_specs=[vmem()] * 4 + [anywhere()],
-        out_specs=vmem(),
-        out_shape=jax.ShapeDtypeStruct((rows // 2, out_weight.shape[1]), BF),
-        compiler_params=params(6),
-        cost_estimate=takes(0),
-        name="last_sum",
-    )(early_got, early_mine, late_got, late_mine, finished)
+    )(xc, xt, mix, reach, skip_gain.reshape(1, heads), expand, enter_mine, enter_got, summed)
     return (attn_out, ssm_out)
 
 

time: 82.1 us -> 79.9 us (0.973)
  waiting for transfers between devices: 37.3 us -> 35.9 us
  Pallas kernels: 25 us -> 24 us
    ppermute x12, waiting for transfers between devices: 12.5 us -> 11.4 us  [swap(): return lax.ppermute(x, 'seq', [(i, i ^ bit) for i in range(count)])]
    pallas_call x1, Pallas kernels: 1.92 us -> 1.09 us  [shards(): pl.pallas_call(prepare_kernel, grid=(1,), in_specs=[vmem(), vmem(), vmem(...]
  transfers between devices with their start and end apart: 16 -> 16, of which waited for: 10 -> 10; matrix products, arithmetic and copies ran while one was open for 0% -> 0% of each run, Pallas kernels for 17% -> 19%
where the time goes in v3:
time: 79.9 us; the launch traced here: 79.4 us
  waiting for transfers between devices  35.9 us (45%)
  Pallas kernels  24 us (30%)
  starting transfers between devices  18.6 us (23%)
  between operations  0.8 us (1%)
    ppermute x1, waiting for transfers between devices, shards(): late_got = lax.ppermute(late_cross, 'head', cross)  11.6 us
    ppermute x12, waiting for transfers between devices, swap(): return lax.ppermute(x, 'seq', [(i, i ^ bit) for i in range(count)])  11.4 us
    ppermute x1, waiting for transfers between devices, shards(): late_pair = lax.ppermute(late_send, 'head', pair)  10.7 us
    ppermute x12, starting transfers between devices, swap(): return lax.ppermute(x, 'seq', [(i, i ^ bit) for i in range(count)])  9.52 us
    pallas_call x2, Pallas kernels, attend(): pl.pallas_call(functools.partial(attend_kernel, places, count, part), in_...  7.34 us
    pallas_call x1, Pallas kernels, shards(): pl.pallas_call(functools.partial(local_kernel, count), grid=(2,), in_spec...  6.35 us
    pallas_call x1, Pallas kernels, shards(): pl.pallas_call(load_kernel, in_specs=[anywhere()] * 4 + [vmem()], out_spe...  4.07 us
    ppermute x1, starting transfers between devices, shards(): late_got = lax.ppermute(late_cross, 'head', cross)  2.79 us
  transfers between devices with their start and end apart: 16, of which 10 were waited for; matrix products, arithmetic and copies ran while one was open for 0% of the time, Pallas kernels for 19%

profile of v3, /device:TPU:0, one launch (start us, length us, event | category | flops | bytes accessed | tf_op | source)
XLA Modules:
  0.0 79.4 jit_solution(3740075483927037814)
XLA Ops:
  0.6 1.1 %prepare.1.kv_ref.rest_0_ = bf16[288,512]{1,0:T(8,128)(2,1)S(1)} custom-call(bf16[256,256]{1,0:T(8,128)(2,1)} %k_ref.1, bf16[256,256]{1,0:T(8,128)(2,1)} %v_ref.1, s32[1,256]{1,0:T(1,128)} %bitcast.6, bf16[256,2048]{1,0:T(8,128)(2,1)} %x_ref.1, bf16[256,2048]{1,0:T(8,128)(2,1)} %x_ref.1, bf16[256,2,256]{2,1,0:T(2,128)(2,1)} %bc_ref.1, ...), custom_call_target="tpu_custom_call" | custom-call | tf_op jit(solution)/shard_map/prepare/pallas_call | solution.py:560
  1.7 4.0 %collective-permute-start.2 = (bf16[288,512]{1,0:T(8,128)(2,1)S(1)}, bf16[288,512]{1,0:T(8,128)(2,1)S(1)}, u32[]{:S(2)}, u32[]{:S(2)}) collective-permute-start(bf16[288,512]{1,0:T(8,128)(2,1)S(1)} %prepare.1.kv_ref.rest_0_), channel_id=1, source_target_pairs={{0,24},{4,28},{8,16},{12,20},{16,8},{20,12},{24,0},{28,4},{1,25},{... | collective-permute-start | bytes 884744 | tf_op jit(solution)/shard_map/ppermute | solution.py:49
  5.7 0.5 collective-permute-start.1
  6.2 0.1 collective-permute-start
  6.4 4.1 %load.1 = (bf16[1024,4096]{1,0:T(8,128)(2,1)S(1)}, bf16[256,1024]{1,0:T(8,128)(2,1)S(1)}, bf16[256,2048]{1,0:T(8,128)(2,1)S(1)}, bf16[256,512]{1,0:T(8,128)(2,1)S(1)}, bf16[288,512]{1,0:T(8,128)(2,1)S(1)}) custom-call(bf16[1024,4096]{1,0:T(8,128)(2,1)} %w_ref.1, bf16[256,1024]{1,0:T(8,128)(2,1)} %q_ref.1, bf16[256,2048]{1,0:T(8,128)(2,1)} %x_ref.1, ...), custom_call_target="tpu_custom_call" | custom-call | flops 49999998976 | bytes 18500000 | tf_op jit(solution)/shard_map/load/pallas_call | solution.py:581
  10.5 3.1 %collective-permute-done.2.rest_3_ = bf16[288,512]{1,0:T(8,128)(2,1)S(1)} collective-permute-done((bf16[288,512]{1,0:T(8,128)(2,1)S(1)}, bf16[288,512]{1,0:T(8,128)(2,1)S(1)}, u32[]{:S(2)}, u32[]{:S(2)}) %collective-permute-start.2) | collective-permute-done | bytes 294944 | tf_op jit(solution)/shard_map/ppermute | solution.py:49
  13.6 5.4 %collective-permute-done.1.rest_2_ = bf16[288,512]{1,0:T(8,128)(2,1)S(1)} collective-permute-done((bf16[288,512]{1,0:T(8,128)(2,1)S(1)}, bf16[288,512]{1,0:T(8,128)(2,1)S(1)}, u32[]{:S(2)}, u32[]{:S(2)}) %collective-permute-start.1) | collective-permute-done | bytes 294944 | tf_op jit(solution)/shard_map/ppermute | solution.py:49
  19.1 0.3 collective-permute-done.rest_1_
  19.3 0.2 collective-permute-start.4
  19.6 1.1 %collective-permute-done.5.rest_6_ = bf16[288,512]{1,0:T(8,128)(2,1)S(1)} collective-permute-done((bf16[288,512]{1,0:T(8,128)(2,1)S(1)}, bf16[288,512]{1,0:T(8,128)(2,1)S(1)}, u32[]{:S(2)}, u32[]{:S(2)}) %collective-permute-start.5) | collective-permute-done | bytes 294944 | tf_op jit(solution)/shard_map/ppermute | solution.py:49
  20.6 0.4 collective-permute-done.4.rest_5_
  21.0 3.8 %attend_early.1 = (bf16[64,4096]{1,0:T(8,128)(2,1)S(1)}, bf16[64,4096]{1,0:T(8,128)(2,1)S(1)}, bf16[2048,512]{1,0:T(8,128)(2,1)S(1)}, f32[8,256]{1,0:T(8,128)S(1)}, bf16[2,16,512]{2,1,0:T(8,128)(2,1)S(1)}) custom-call(bf16[256,1024]{1,0:T(8,128)(2,1)S(1)} %get-tuple-element.29.q_ref, bf16[1024,4096]{1,0:T(8,128)(2,1)S(1)} %get-tuple-element.30.w_ref, ...), custom_call_target="tpu_custom_call" | custom-call | flops 80000000000 | bytes 29600000 | tf_op jit(solution)/shard_map/attend_early/pallas_call | solution.py:217
  24.8 1.8 %collective-permute-start.7 = (bf16[64,4096]{1,0:T(8,128)(2,1)S(1)}, bf16[64,4096]{1,0:T(8,128)(2,1)S(1)}, u32[]{:S(2)}, u32[]{:S(2)}) collective-permute-start(bf16[64,4096]{1,0:T(8,128)(2,1)S(1)} %get-tuple-element.32), channel_id=1, source_target_pairs={{0,1},{1,0},{2,3},{3,2},{4,5},{5,4},{6,7},{7,6},{8,9},{9,8},{10,11... | collective-permute-start | bytes 1572872 | tf_op jit(solution)/shard_map/ppermute | solution.py:612
  26.7 3.5 %attend_late.1 = (bf16[64,4096]{1,0:T(8,128)(2,1)S(1)}, bf16[64,4096]{1,0:T(8,128)(2,1)S(1)}) custom-call(bf16[256,1024]{1,0:T(8,128)(2,1)S(1)} %get-tuple-element.29.q_ref, bf16[1024,4096]{1,0:T(8,128)(2,1)S(1)} %get-tuple-element.30.w_ref, bf16[2048,512]{1,0:T(8,128)(2,1)S(1)} %get-tuple-element.38.rest_0_, ...), custom_call_target="tpu_custom_call" | custom-call | flops 80000000000 | bytes 29600000 | tf_op jit(solution)/shard_map/attend_late/pallas_call | solution.py:217
  30.2 6.3 %local_states.1 = (bf16[256,2048]{1,0:T(8,128)(2,1)}, bf16[256,2048]{1,0:T(8,128)(2,1)}, bf16[256,512]{1,0:T(8,128)(2,1)}, f32[256,32]{1,0:T(8,128)}, bf16[2,136...) custom-call(f32[8,256]{1,0:T(8,128)S(1)} %get-tuple-element.34.rest_1_.docs_ref, ...), custom_call_target="tpu_custom_call" | custom-call | flops 54999998464 | bytes 20350000 | tf_op jit(solution)/shard_map/local_states/pallas_call | solution.py:615
  36.6 2.3 %collective-permute-done.7.got_ref = bf16[64,4096]{1,0:T(8,128)(2,1)S(1)} collective-permute-done((bf16[64,4096]{1,0:T(8,128)(2,1)S(1)}, bf16[64,4096]{1,0:T(8,128)(2,1)S(1)}, u32[]{:S(2)}, u32[]{:S(2)}) %collective-permute-start.7) | collective-permute-done | bytes 524320 | tf_op jit(solution)/shard_map/ppermute | solution.py:612
  38.9 0.2 pair_sum.2
  39.0 0.1 collective-permute-start.11
  39.1 1.8 %collective-permute-start.9 = (bf16[64,4096]{1,0:T(8,128)(2,1)S(1)}, bf16[64,4096]{1,0:T(8,128)(2,1)S(1)}, u32[]{:S(2)}, u32[]{:S(2)}) collective-permute-start(bf16[64,4096]{1,0:T(8,128)(2,1)S(1)} %get-tuple-element.43), channel_id=1, source_target_pairs={{0,1},{1,0},{2,3},{3,2},{4,5},{5,4},{6,7},{7,6},{8,9},{9,8},{10,11... | collective-permute-start | bytes 1572872 | tf_op jit(solution)/shard_map/ppermute | solution.py:614
  40.9 0.1 collective-permute-done.11.other_ref
  41.1 0.2 join_states.1.rest_0_
  41.3 3.8 %collective-permute-start.14 = (bf16[2,136,1024]{2,1,0:T(8,128)(2,1)S(1)}, bf16[2,136,1024]{2,1,0:T(8,128)(2,1)S(1)}, u32[]{:S(2)}, u32[]{:S(2)}) collective-permute-start(bf16[2,136,1024]{2,1,0:T(8,128)(2,1)S(1)} %join_states.1.rest_0_), channel_id=1, source_target_pairs={{0,24},{4,28},{8,16},{12,20},{16,8},{20,12},{24,0},{28,4},{1,25},{... | collective-permute-start | bytes 1671176 | tf_op jit(solution)/shard_map/ppermute | solution.py:49
  45.1 0.6 collective-permute-start.12
  45.7 2.7 %collective-permute-start.8 = (bf16[32,4096]{1,0:T(8,128)(2,1)S(1)}, bf16[32,4096]{1,0:T(8,128)(2,1)S(1)}, u32[]{:S(2)}, u32[]{:S(2)}) collective-permute-start(bf16[32,4096]{1,0:T(8,128)(2,1)S(1)} %get-tuple-element.41), channel_id=1, source_target_pairs={{0,2},{1,3},{2,0},{3,1},{4,6},{5,7},{6,4},{7,5},{8,10},{9,11},{10,... | collective-permute-start | bytes 786440 | tf_op jit(solution)/shard_map/ppermute | solution.py:650
  48.4 10.7 %collective-permute-done.9.got_ref = bf16[64,4096]{1,0:T(8,128)(2,1)S(1)} collective-permute-done((bf16[64,4096]{1,0:T(8,128)(2,1)S(1)}, bf16[64,4096]{1,0:T(8,128)(2,1)S(1)}, u32[]{:S(2)}, u32[]{:S(2)}) %collective-permute-start.9) | collective-permute-done | bytes 524320 | tf_op jit(solution)/shard_map/ppermute | solution.py:614
  59.1 0.1 pair_sum.3
  59.2 2.8 %collective-permute-start.10 = (bf16[32,4096]{1,0:T(8,128)(2,1)S(1)}, bf16[32,4096]{1,0:T(8,128)(2,1)S(1)}, u32[]{:S(2)}, u32[]{:S(2)}) collective-permute-start(bf16[32,4096]{1,0:T(8,128)(2,1)S(1)} %get-tuple-element.44), channel_id=1, source_target_pairs={{0,2},{1,3},{2,0},{3,1},{4,6},{5,7},{6,4},{7,5},{8,10},{9,11},{10,... | collective-permute-start | bytes 786440 | tf_op jit(solution)/shard_map/ppermute | solution.py:661
  62.0 11.6 %collective-permute-done.10.after_ref.late_got = bf16[32,4096]{1,0:T(8,128)(2,1)S(1)} collective-permute-done((bf16[32,4096]{1,0:T(8,128)(2,1)S(1)}, bf16[32,4096]{1,0:T(8,128)(2,1)S(1)}, u32[]{:S(2)}, u32[]{:S(2)}) %collective-permute-start.10) | collective-permute-done | bytes 262176 | tf_op jit(solution)/shard_map/ppermute | solution.py:661
  73.6 1.2 %enter_states.1 = (bf16[2,128,1024]{2,1,0:T(8,128)(2,1)S(1)}, bf16[2,128,1024]{2,1,0:T(8,128)(2,1)S(1)}) custom-call(bf16[2,136,1024]{2,1,0:T(8,128)(2,1)S(1)} %get-tuple-element.46.mine_ref, bf16[2,136,1024]{2,1,0:T(8,128)(2,1)S(1)} %collective-permute-done.11.other_ref, bf16[32,4096]{1,0:T(8,128)(2,1)S(1)} %collective-permute-done.10.after_ref.late_got, ...), custom_call_target="tpu_custom_call" | custom-call | tf_op jit(solution)/shard_map/enter_states/pallas_call | solution.py:665
  74.9 0.9 %last_sum.1 = (bf16[64,4096]{1,0:T(8,128)(2,1)}, f32[8,128]{1,0:T(8,128)S(1)}) custom-call(bf16[32,4096]{1,0:T(8,128)(2,1)S(1)} %collective-permute-done.8.after_ref.early_got, bf16[32,4096]{1,0:T(8,128)(2,1)S(1)} %get-tuple-element.42.early_keep, bf16[32,4096]{1,0:T(8,128)(2,1)S(1)} %collective-permute-done.10.after_ref.late_got, ...), custom_call_target="tpu_custom_call" | custom-call | tf_op jit(solution)/shard_map/last_sum/pallas_call | solution.py:682
  75.8 1.0 %collective-permute-done.15.other_ref = bf16[2,128,1024]{2,1,0:T(8,128)(2,1)S(1)} collective-permute-done((bf16[2,128,1024]{2,1,0:T(8,128)(2,1)S(1)}, bf16[2,128,1024]{2,1,0:T(8,128)(2,1)S(1)}, u32[]{:S(2)}, u32[]{:S(2)}) %collective-permute-start.15) | collective-permute-done | bytes 524320 | tf_op jit(solution)/shard_map/ppermute | solution.py:49
  76.8 2.5 %finish.1 = bf16[256,2048]{1,0:T(8,128)(2,1)} custom-call(bf16[256,2048]{1,0:T(8,128)(2,1)S(1)} %copy-done, bf16[256,2048]{1,0:T(8,128)(2,1)S(1)} %copy-done.1, bf16[256,512]{1,0:T(8,128)(2,1)S(1)} %copy-done.3, f32[256,32]{1,0:T(8,128)S(1)} %copy-done.4, f32[1,32]{1,0:T(1,128)S(1)} %bitcast.4, bf16[64,2048]{1,0:T(8,128)(2,1)S(1)} %copy-done.2, ...), custom_call_target="tpu_custom_call" | custom-call | tf_op jit(solution)/shard_map/finish/pallas_call | solution.py:694
  (25 shorter events, 0.2 us)
Async XLA Ops:
  1.7 11.9 %collective-permute-start.2 = (bf16[288,512]{1,0:T(8,128)(2,1)S(1)}, bf16[288,512]{1,0:T(8,128)(2,1)S(1)}, u32[]{:S(2)}, u32[]{:S(2)}) collective-permute-start(bf16[288,512]{1,0:T(8,128)(2,1)S(1)} %prepare.1.kv_ref.rest_0_), channel_id=1, source_target_pairs={{0,24},{4,28},{8,16},{12,20},{16,8},{20,12},{24,0},{28,4},{1,25},{... | collective-permute-start | bytes 884744 | tf_op jit(solution)/shard_map/ppermute | solution.py:49
  5.7 13.3 %collective-permute-start.1 = (bf16[288,512]{1,0:T(8,128)(2,1)S(1)}, bf16[288,512]{1,0:T(8,128)(2,1)S(1)}, u32[]{:S(2)}, u32[]{:S(2)}) collective-permute-start(bf16[288,512]{1,0:T(8,128)(2,1)S(1)} %prepare.1.kv_ref.rest_0_), channel_id=1, source_target_pairs={{0,16},{4,20},{8,24},{12,28},{16,0},{20,4},{24,8},{28,12},{1,17},{... | collective-permute-start | bytes 884744 | tf_op jit(solution)/shard_map/ppermute | solution.py:49
  6.2 13.1 %collective-permute-start = (bf16[288,512]{1,0:T(8,128)(2,1)S(1)}, bf16[288,512]{1,0:T(8,128)(2,1)S(1)}, u32[]{:S(2)}, u32[]{:S(2)}) collective-permute-start(bf16[288,512]{1,0:T(8,128)(2,1)S(1)} %prepare.1.kv_ref.rest_0_), channel_id=1, source_target_pairs={{0,8},{4,12},{8,0},{12,4},{16,24},{20,28},{24,16},{28,20},{1,9},{5... | collective-permute-start | bytes 884744 | tf_op jit(solution)/shard_map/ppermute | solution.py:49
  10.4 9.1 %collective-permute-start.3 = (bf16[288,512]{1,0:T(8,128)(2,1)S(1)}, bf16[288,512]{1,0:T(8,128)(2,1)S(1)}, u32[]{:S(2)}, u32[]{:S(2)}) collective-permute-start(bf16[288,512]{1,0:T(8,128)(2,1)S(1)} %get-tuple-element.31), channel_id=1, source_target_pairs={{0,4},{4,0},{8,12},{12,8},{16,20},{20,16},{24,28},{28,24},{1,5},{5... | collective-permute-start | bytes 884744 | tf_op jit(solution)/shard_map/ppermute | solution.py:49
  13.6 5.9 %collective-permute-start.6 = (bf16[288,512]{1,0:T(8,128)(2,1)S(1)}, bf16[288,512]{1,0:T(8,128)(2,1)S(1)}, u32[]{:S(2)}, u32[]{:S(2)}) collective-permute-start(bf16[288,512]{1,0:T(8,128)(2,1)S(1)} %collective-permute-done.2.rest_3_), channel_id=1, source_target_pairs={{0,4},{4,0},{8,12},{12,8},{16,20},{20,16},{24,28},{28,24},{1,5},{5... | collective-permute-start | bytes 884744 | tf_op jit(solution)/shard_map/ppermute | solution.py:49
  19.0 1.6 %collective-permute-start.5 = (bf16[288,512]{1,0:T(8,128)(2,1)S(1)}, bf16[288,512]{1,0:T(8,128)(2,1)S(1)}, u32[]{:S(2)}, u32[]{:S(2)}) collective-permute-start(bf16[288,512]{1,0:T(8,128)(2,1)S(1)} %collective-permute-done.1.rest_2_), channel_id=1, source_target_pairs={{0,4},{4,0},{8,12},{12,8},{16,20},{20,16},{24,28},{28,24},{1,5},{5... | collective-permute-start | bytes 884744 | tf_op jit(solution)/shard_map/ppermute | solution.py:49
  19.3 1.7 %collective-permute-start.4 = (bf16[288,512]{1,0:T(8,128)(2,1)S(1)}, bf16[288,512]{1,0:T(8,128)(2,1)S(1)}, u32[]{:S(2)}, u32[]{:S(2)}) collective-permute-start(bf16[288,512]{1,0:T(8,128)(2,1)S(1)} %collective-permute-done.rest_1_), channel_id=1, source_target_pairs={{0,4},{4,0},{8,12},{12,8},{16,20},{20,16},{24,28},{28,24},{1,5},{5... | collective-permute-start | bytes 884744 | tf_op jit(solution)/shard_map/ppermute | solution.py:49
  24.8 14.0 %collective-permute-start.7 = (bf16[64,4096]{1,0:T(8,128)(2,1)S(1)}, bf16[64,4096]{1,0:T(8,128)(2,1)S(1)}, u32[]{:S(2)}, u32[]{:S(2)}) collective-permute-start(bf16[64,4096]{1,0:T(8,128)(2,1)S(1)} %get-tuple-element.32), channel_id=1, source_target_pairs={{0,1},{1,0},{2,3},{3,2},{4,5},{5,4},{6,7},{7,6},{8,9},{9,8},{10,11... | collective-permute-start | bytes 1572872 | tf_op jit(solution)/shard_map/ppermute | solution.py:612
  26.7 3.6 %copy-start.2 = (bf16[64,2048]{1,0:T(8,128)(2,1)S(1)}, bf16[64,2048]{1,0:T(8,128)(2,1)}, u32[]{:S(2)}) copy-start(bf16[64,2048]{1,0:T(8,128)(2,1)} %constant.2.clone.expand_ref) | copy-start | bytes 786436
  26.7 3.6 %copy-start.6 = (f32[32]{0:T(128)S(1)}, f32[32]{0:T(128)}, u32[]{:S(2)}) copy-start(f32[32]{0:T(128)} %param.22) | copy-start | bytes 388
  36.6 40.2 %copy-start = (bf16[256,2048]{1,0:T(8,128)(2,1)S(1)}, bf16[256,2048]{1,0:T(8,128)(2,1)}, u32[]{:S(2)}) copy-start(bf16[256,2048]{1,0:T(8,128)(2,1)} %get-tuple-element.50.xc_ref) | copy-start | bytes 3145732
  36.6 40.2 %copy-start.1 = (bf16[256,2048]{1,0:T(8,128)(2,1)S(1)}, bf16[256,2048]{1,0:T(8,128)(2,1)}, u32[]{:S(2)}) copy-start(bf16[256,2048]{1,0:T(8,128)(2,1)} %get-tuple-element.51.xt_ref) | copy-start | bytes 3145732
  36.6 40.2 %copy-start.3 = (bf16[256,512]{1,0:T(8,128)(2,1)S(1)}, bf16[256,512]{1,0:T(8,128)(2,1)}, u32[]{:S(2)}) copy-start(bf16[256,512]{1,0:T(8,128)(2,1)} %get-tuple-element.52.mix_ref) | copy-start | bytes 786436
  36.6 40.2 %copy-start.4 = (f32[256,32]{1,0:T(8,128)S(1)}, f32[256,32]{1,0:T(8,128)}, u32[]{:S(2)}) copy-start(f32[256,32]{1,0:T(8,128)} %get-tuple-element.53.reach_ref) | copy-start | bytes 98308
  36.6 40.2 %copy-start.5 = (f32[32]{0:T(128)S(1)}, f32[32]{0:T(128)}, u32[]{:S(2)}) copy-start(f32[32]{0:T(128)} %param.23) | copy-start | bytes 388
  39.0 2.0 %collective-permute-start.11 = (bf16[2,136,1024]{2,1,0:T(8,128)(2,1)S(1)}, bf16[2,136,1024]{2,1,0:T(8,128)(2,1)S(1)}, u32[]{:S(2)}, u32[]{:S(2)}) collective-permute-start(bf16[2,136,1024]{2,1,0:T(8,128)(2,1)S(1)} %get-tuple-element.47), channel_id=1, source_target_pairs={{0,4},{4,0},{8,12},{12,8},{16,20},{20,16},{24,28},{28,24},{1,5},{5... | collective-permute-start | bytes 1671176 | tf_op jit(solution)/shard_map/ppermute | solution.py:49
  39.1 19.9 %collective-permute-start.9 = (bf16[64,4096]{1,0:T(8,128)(2,1)S(1)}, bf16[64,4096]{1,0:T(8,128)(2,1)S(1)}, u32[]{:S(2)}, u32[]{:S(2)}) collective-permute-start(bf16[64,4096]{1,0:T(8,128)(2,1)S(1)} %get-tuple-element.43), channel_id=1, source_target_pairs={{0,1},{1,0},{2,3},{3,2},{4,5},{5,4},{6,7},{7,6},{8,9},{9,8},{10,11... | collective-permute-start | bytes 1572872 | tf_op jit(solution)/shard_map/ppermute | solution.py:614
  41.3 32.3 %collective-permute-start.14 = (bf16[2,136,1024]{2,1,0:T(8,128)(2,1)S(1)}, bf16[2,136,1024]{2,1,0:T(8,128)(2,1)S(1)}, u32[]{:S(2)}, u32[]{:S(2)}) collective-permute-start(bf16[2,136,1024]{2,1,0:T(8,128)(2,1)S(1)} %join_states.1.rest_0_), channel_id=1, source_target_pairs={{0,24},{4,28},{8,16},{12,20},{16,8},{20,12},{24,0},{28,4},{1,25},{... | collective-permute-start | bytes 1671176 | tf_op jit(solution)/shard_map/ppermute | solution.py:49
  45.1 28.5 %collective-permute-start.13 = (bf16[2,136,1024]{2,1,0:T(8,128)(2,1)S(1)}, bf16[2,136,1024]{2,1,0:T(8,128)(2,1)S(1)}, u32[]{:S(2)}, u32[]{:S(2)}) collective-permute-start(bf16[2,136,1024]{2,1,0:T(8,128)(2,1)S(1)} %join_states.1.rest_0_), channel_id=1, source_target_pairs={{0,16},{4,20},{8,24},{12,28},{16,0},{20,4},{24,8},{28,12},{1,17},{... | collective-permute-start | bytes 1671176 | tf_op jit(solution)/shard_map/ppermute | solution.py:49
  45.1 28.5 %collective-permute-start.12 = (bf16[2,136,1024]{2,1,0:T(8,128)(2,1)S(1)}, bf16[2,136,1024]{2,1,0:T(8,128)(2,1)S(1)}, u32[]{:S(2)}, u32[]{:S(2)}) collective-permute-start(bf16[2,136,1024]{2,1,0:T(8,128)(2,1)S(1)} %join_states.1.rest_0_), channel_id=1, source_target_pairs={{0,8},{4,12},{8,0},{12,4},{16,24},{20,28},{24,16},{28,20},{1,9},{5... | collective-permute-start | bytes 1671176 | tf_op jit(solution)/shard_map/ppermute | solution.py:49
  45.7 13.4 %collective-permute-start.8 = (bf16[32,4096]{1,0:T(8,128)(2,1)S(1)}, bf16[32,4096]{1,0:T(8,128)(2,1)S(1)}, u32[]{:S(2)}, u32[]{:S(2)}) collective-permute-start(bf16[32,4096]{1,0:T(8,128)(2,1)S(1)} %get-tuple-element.41), channel_id=1, source_target_pairs={{0,2},{1,3},{2,0},{3,1},{4,6},{5,7},{6,4},{7,5},{8,10},{9,11},{10,... | collective-permute-start | bytes 786440 | tf_op jit(solution)/shard_map/ppermute | solution.py:650
  59.2 14.4 %collective-permute-start.10 = (bf16[32,4096]{1,0:T(8,128)(2,1)S(1)}, bf16[32,4096]{1,0:T(8,128)(2,1)S(1)}, u32[]{:S(2)}, u32[]{:S(2)}) collective-permute-start(bf16[32,4096]{1,0:T(8,128)(2,1)S(1)} %get-tuple-element.44), channel_id=1, source_target_pairs={{0,2},{1,3},{2,0},{3,1},{4,6},{5,7},{6,4},{7,5},{8,10},{9,11},{10,... | collective-permute-start | bytes 786440 | tf_op jit(solution)/shard_map/ppermute | solution.py:661
  74.8 2.0 %collective-permute-start.15 = (bf16[2,128,1024]{2,1,0:T(8,128)(2,1)S(1)}, bf16[2,128,1024]{2,1,0:T(8,128)(2,1)S(1)}, u32[]{:S(2)}, u32[]{:S(2)}) collective-permute-start(bf16[2,128,1024]{2,1,0:T(8,128)(2,1)S(1)} %get-tuple-element.48.after_ref), channel_id=1, source_target_pairs={{0,4},{4,0},{8,12},{12,8},{16,20},{20,16},{24,28},{28,24},{1,5},{5... | collective-permute-start | bytes 1572872 | tf_op jit(solution)/shard_map/ppermute | solution.py:49

commit v4 on v3

--- a/solution.py
+++ b/solution.py
@@ -231,7 +231,8 @@
     )(queries, out_weight, *operands)
 
 
-def pair_kernel(got_ref, keep_ref, after_ref, send_out, keep_out, *through):
+def pair_kernel(skipped, got_ref, keep_ref, after_ref, *rest):
+    send_out, keep_out, *through = rest[skipped:]
     for ref in through:
         ref[...] = after_ref[...]
     own_rows = send_out.shape[0]
@@ -252,20 +253,20 @@
         send_out[...] = add(0)
 
 
-def pair_sum(got, keep, after, through):
+def pair_sum(got, keep, after, through, *also):
     rows, columns = keep.shape
     outs = [jax.ShapeDtypeStruct((rows // 2, columns), BF)] * 2
     if through:
         outs = outs + [jax.ShapeDtypeStruct(after.shape, after.dtype)]
     return pl.pallas_call(
-        pair_kernel,
-        in_specs=[vmem(), vmem(), vmem() if through else anywhere()],
+        functools.partial(pair_kernel, len(also)),
+        in_specs=[vmem(), vmem(), vmem() if through else anywhere()] + [anywhere()] * len(also),
         out_specs=[vmem()] * len(outs),
         out_shape=outs,
         compiler_params=params(8),
         cost_estimate=takes(0),
         name="pair_sum",
-    )(got, keep, after)
+    )(got, keep, after, *also)
 
 
 def last_kernel(early_got, early_keep, late_got, late_keep, after_ref, out_ref, done_ref):
@@ -513,32 +514,45 @@
     lax.fori_loop(0, chips - chip, back_step, 0)
 
 
-def finish_kernel(
-    xc_ref, xt_ref, mix_ref, reach_ref, skip_ref, expand_ref, mine_ref, other_ref, after_ref, out_ref, both
-):
+def ready_kernel(xc_ref, xt_ref, mix_ref, reach_ref, skip_ref, expand_ref, base_ref, wide_ref):
+    rows = mix_ref.shape[0] // 2
+    x_width = xc_ref.shape[1]
+    groups = mix_ref.shape[1] // (2 * rows)
+    x_group = x_width // groups
+    skip = spread(jnp.broadcast_to(skip_ref[...], (8, skip_ref.shape[1])), expand_ref[...])[:1]
+    for half in range(2):
+        mine = slice(half * rows, (half + 1) * rows)
+        for g in range(groups):
+            lanes = slice(g * x_group, (g + 1) * x_group)
+            mix = mix_ref[mine, g * 2 * rows : g * 2 * rows + rows]
+            made = jnp.dot(mix, xt_ref[mine, lanes], preferred_element_type=F32)
+            wide = spread(reach_ref[mine, :], expand_ref[:, lanes])
+            wide_ref[mine, lanes] = wide
+            base_ref[mine, lanes] = made * wide + skip[:, lanes] * xc_ref[mine, lanes].astype(F32)
+
+
+def finish_kernel(mix_ref, base_ref, wide_ref, mine_ref, other_ref, after_ref, out_ref):
     core = lax.rem(lax.axis_index("seq"), 2)
     half = pl.program_id(0)
     rows, x_width = out_ref.shape
+    mine = pl.ds(pl.multiple_of(half * rows, rows), rows)
     groups = mix_ref.shape[1] // (2 * rows)
     x_group = x_width // groups
     for g in range(groups):
         lanes = slice(g * x_group, (g + 1) * x_group)
-        expand = expand_ref[:, lanes]
-        both[:rows] = xt_ref[:, lanes]
+        reads = mix_ref[mine, g * 2 * rows + rows : (g + 1) * 2 * rows]
+
+        def put(state, reads=reads, lanes=lanes):
+            made = jnp.dot(reads, state, preferred_element_type=F32)
+            out_ref[:, lanes] = (base_ref[mine, lanes] + wide_ref[mine, lanes] * made).astype(BF)
 
         @pl.when(core == g)
-        def _():
-            both[rows:] = mine_ref[half]
+        def _(put=put):
+            put(mine_ref[half])
 
         @pl.when(core != g)
-        def _():
-            both[rows:] = other_ref[half]
-
-        mix = mix_ref[:, g * 2 * rows : (g + 1) * 2 * rows]
-        made = jnp.dot(mix, both[...], preferred_element_type=F32)
-        made = made * spread(reach_ref[...], expand)
-        skip = spread(jnp.broadcast_to(skip_ref[...], (8, skip_ref.shape[1])), expand)[:1]
-        out_ref[:, lanes] = (made + skip * xc_ref[:, lanes].astype(F32)).astype(BF)
+        def _(put=put):
+            put(other_ref[half])
 
 
 def shards(
@@ -657,7 +671,16 @@
         cost_estimate=takes(0),
         name="join_states",
     )(keep, other, late_keep)
-    late_cross, late_mine = pair_sum(late_pair, late_keep, early_got, False)
+    base, wide = pl.pallas_call(
+        ready_kernel,
+        in_specs=[vmem()] * 6,
+        out_specs=[vmem()] * 2,
+        out_shape=[pltpu.VMEM((rows_dev, x_width), F32)] * 2,
+        cost_estimate=takes(4),
+        compiler_params=params(12),
+        name="ready",
+    )(xc, xt, mix, reach, skip_gain.reshape(1, heads), expand)
+    late_cross, late_mine = pair_sum(late_pair, late_keep, early_got, False, base)
     late_got = lax.ppermute(late_cross, "head", cross)
     chip_pieces = chip_gather(chip)
     chips = count // 2
@@ -694,24 +717,13 @@
     ssm_out = pl.pallas_call(
         finish_kernel,
         grid=(2,),
-        in_specs=[
-            half(x_width),
-            half(x_width),
-            half(groups * 2 * rows),
-            half(heads),
-            full((1, heads)),
-            full((2 * heads, x_width)),
-            vmem(),
-            vmem(),
-            anywhere(),
-        ],
+        in_specs=[vmem()] * 5 + [anywhere()],
         out_specs=half(x_width),
         out_shape=pltpu.HBM((rows_dev, x_width), BF),
-        scratch_shapes=[pltpu.VMEM((2 * rows, x_group), BF)],
         cost_estimate=takes(0),
-        compiler_params=params(20),
+        compiler_params=params(12),
         name="finish",
-    )(xc, xt, mix, reach, skip_gain.reshape(1, heads), expand, enter_mine, enter_got, summed)
+    )(mix, base, wide, enter_mine, enter_got, summed)
     return (attn_out, ssm_out)
 
 

time: 79.9 us -> 79.5 us (level)
  Pallas kernels: 24 us -> 23 us
    ppermute x1, waiting for transfers between devices: 2.26 us -> 3.4 us  [shards(): early_pair = lax.ppermute(early_send, 'head', pair)]
    pallas_call x2, Pallas kernels: 7.34 us -> 6.36 us  [attend(): pl.pallas_call(functools.partial(attend_kernel, places, count, part), in_...]
    ppermute x1, waiting for transfers between devices: 10.7 us -> 9.71 us  [shards(): late_pair = lax.ppermute(late_send, 'head', pair)]
    pallas_call x3 -> x4, Pallas kernels: 2.82 us -> 2.86 us  [the longest x1 1.72 us: shards(): pl.pallas_call(finish_kernel, grid=(2,), in_specs=[vmem()] * 5 + [anywher...]
  transfers between devices with their start and end apart: 16 -> 16, of which waited for: 10 -> 9; matrix products, arithmetic and copies ran while one was open for 0% -> 0% of each run, Pallas kernels for 19% -> 20%
where the time goes in v4:
time: 79.5 us; the launch traced here: 78.7 us
  waiting for transfers between devices  36.1 us (45%)
  Pallas kernels  23 us (29%)
  starting transfers between devices  18.8 us (24%)
    ppermute x1, waiting for transfers between devices, shards(): late_got = lax.ppermute(late_cross, 'head', cross)  11.7 us
    ppermute x12, waiting for transfers between devices, swap(): return lax.ppermute(x, 'seq', [(i, i ^ bit) for i in range(count)])  11.3 us
    ppermute x12, starting transfers between devices, swap(): return lax.ppermute(x, 'seq', [(i, i ^ bit) for i in range(count)])  9.91 us
    ppermute x1, waiting for transfers between devices, shards(): late_pair = lax.ppermute(late_send, 'head', pair)  9.71 us
    pallas_call x2, Pallas kernels, attend(): pl.pallas_call(functools.partial(attend_kernel, places, count, part), in_...  6.36 us
    pallas_call x1, Pallas kernels, shards(): pl.pallas_call(functools.partial(local_kernel, count), grid=(2,), in_spec...  6.34 us
    pallas_call x1, Pallas kernels, shards(): pl.pallas_call(load_kernel, in_specs=[anywhere()] * 4 + [vmem()], out_spe...  4.07 us
    ppermute x1, waiting for transfers between devices, shards(): early_pair = lax.ppermute(early_send, 'head', pair)  3.4 us
  transfers between devices with their start and end apart: 16, of which 9 were waited for; matrix products, arithmetic and copies ran while one was open for 0% of the time, Pallas kernels for 20%

profile of v4, /device:TPU:0, one launch (start us, length us, event | category | flops | bytes accessed | tf_op | source)
XLA Modules:
  0.0 78.7 jit_solution(14983803695016073468)
XLA Ops:
  0.6 1.1 %prepare.1.kv_ref.rest_0_ = bf16[288,512]{1,0:T(8,128)(2,1)S(1)} custom-call(bf16[256,256]{1,0:T(8,128)(2,1)} %k_ref.1, bf16[256,256]{1,0:T(8,128)(2,1)} %v_ref.1, s32[1,256]{1,0:T(1,128)} %bitcast.6, bf16[256,2048]{1,0:T(8,128)(2,1)} %x_ref.1, bf16[256,2048]{1,0:T(8,128)(2,1)} %x_ref.1, bf16[256,2,256]{2,1,0:T(2,128)(2,1)} %bc_ref.1, ...), custom_call_target="tpu_custom_call" | custom-call | tf_op jit(solution)/shard_map/prepare/pallas_call | solution.py:574
  1.7 4.0 %collective-permute-start.2 = (bf16[288,512]{1,0:T(8,128)(2,1)S(1)}, bf16[288,512]{1,0:T(8,128)(2,1)S(1)}, u32[]{:S(2)}, u32[]{:S(2)}) collective-permute-start(bf16[288,512]{1,0:T(8,128)(2,1)S(1)} %prepare.1.kv_ref.rest_0_), channel_id=1, source_target_pairs={{0,24},{4,28},{8,16},{12,20},{16,8},{20,12},{24,0},{28,4},{1,25},{... | collective-permute-start | bytes 884744 | tf_op jit(solution)/shard_map/ppermute | solution.py:49
  5.7 0.5 collective-permute-start.1
  6.2 0.1 collective-permute-start
  6.4 4.1 %load.1 = (bf16[1024,4096]{1,0:T(8,128)(2,1)S(1)}, bf16[256,1024]{1,0:T(8,128)(2,1)S(1)}, bf16[256,2048]{1,0:T(8,128)(2,1)S(1)}, bf16[256,512]{1,0:T(8,128)(2,1)S(1)}, bf16[288,512]{1,0:T(8,128)(2,1)S(1)}) custom-call(bf16[1024,4096]{1,0:T(8,128)(2,1)} %w_ref.1, bf16[256,1024]{1,0:T(8,128)(2,1)} %q_ref.1, bf16[256,2048]{1,0:T(8,128)(2,1)} %x_ref.1, ...), custom_call_target="tpu_custom_call" | custom-call | flops 49999998976 | bytes 18500000 | tf_op jit(solution)/shard_map/load/pallas_call | solution.py:595
  10.5 3.1 %collective-permute-done.2.rest_3_ = bf16[288,512]{1,0:T(8,128)(2,1)S(1)} collective-permute-done((bf16[288,512]{1,0:T(8,128)(2,1)S(1)}, bf16[288,512]{1,0:T(8,128)(2,1)S(1)}, u32[]{:S(2)}, u32[]{:S(2)}) %collective-permute-start.2) | collective-permute-done | bytes 294944 | tf_op jit(solution)/shard_map/ppermute | solution.py:49
  13.6 5.4 %collective-permute-done.1.rest_2_ = bf16[288,512]{1,0:T(8,128)(2,1)S(1)} collective-permute-done((bf16[288,512]{1,0:T(8,128)(2,1)S(1)}, bf16[288,512]{1,0:T(8,128)(2,1)S(1)}, u32[]{:S(2)}, u32[]{:S(2)}) %collective-permute-start.1) | collective-permute-done | bytes 294944 | tf_op jit(solution)/shard_map/ppermute | solution.py:49
  19.1 0.3 collective-permute-done.rest_1_
  19.3 0.2 collective-permute-start.4
  19.6 1.1 %collective-permute-done.5.rest_6_ = bf16[288,512]{1,0:T(8,128)(2,1)S(1)} collective-permute-done((bf16[288,512]{1,0:T(8,128)(2,1)S(1)}, bf16[288,512]{1,0:T(8,128)(2,1)S(1)}, u32[]{:S(2)}, u32[]{:S(2)}) %collective-permute-start.5) | collective-permute-done | bytes 294944 | tf_op jit(solution)/shard_map/ppermute | solution.py:49
  20.6 0.4 collective-permute-done.4.rest_5_
  21.0 3.3 %attend_early.1 = (bf16[64,4096]{1,0:T(8,128)(2,1)S(1)}, bf16[64,4096]{1,0:T(8,128)(2,1)S(1)}, bf16[2048,512]{1,0:T(8,128)(2,1)S(1)}, f32[8,256]{1,0:T(8,128)S(1)}, bf16[2,16,512]{2,1,0:T(8,128)(2,1)S(1)}) custom-call(bf16[256,1024]{1,0:T(8,128)(2,1)S(1)} %get-tuple-element.31.q_ref, bf16[1024,4096]{1,0:T(8,128)(2,1)S(1)} %get-tuple-element.32.w_ref, ...), custom_call_target="tpu_custom_call" | custom-call | flops 80000000000 | bytes 29600000 | tf_op jit(solution)/shard_map/attend_early/pallas_call | solution.py:217
  24.4 1.8 %collective-permute-start.7 = (bf16[64,4096]{1,0:T(8,128)(2,1)S(1)}, bf16[64,4096]{1,0:T(8,128)(2,1)S(1)}, u32[]{:S(2)}, u32[]{:S(2)}) collective-permute-start(bf16[64,4096]{1,0:T(8,128)(2,1)S(1)} %get-tuple-element.34), channel_id=1, source_target_pairs={{0,1},{1,0},{2,3},{3,2},{4,5},{5,4},{6,7},{7,6},{8,9},{9,8},{10,11... | collective-permute-start | bytes 1572872 | tf_op jit(solution)/shard_map/ppermute | solution.py:626
  26.2 3.1 %attend_late.1 = (bf16[64,4096]{1,0:T(8,128)(2,1)S(1)}, bf16[64,4096]{1,0:T(8,128)(2,1)S(1)}) custom-call(bf16[256,1024]{1,0:T(8,128)(2,1)S(1)} %get-tuple-element.31.q_ref, bf16[1024,4096]{1,0:T(8,128)(2,1)S(1)} %get-tuple-element.32.w_ref, bf16[2048,512]{1,0:T(8,128)(2,1)S(1)} %get-tuple-element.40.rest_0_, ...), custom_call_target="tpu_custom_call" | custom-call | flops 80000000000 | bytes 29600000 | tf_op jit(solution)/shard_map/attend_late/pallas_call | solution.py:217
  29.3 6.3 %local_states.1 = (bf16[256,2048]{1,0:T(8,128)(2,1)}, bf16[256,2048]{1,0:T(8,128)(2,1)}, bf16[256,512]{1,0:T(8,128)(2,1)}, f32[256,32]{1,0:T(8,128)}, bf16[2,136...) custom-call(f32[8,256]{1,0:T(8,128)S(1)} %get-tuple-element.36.rest_1_.docs_ref, ...), custom_call_target="tpu_custom_call" | custom-call | flops 54999998464 | bytes 20350000 | tf_op jit(solution)/shard_map/local_states/pallas_call | solution.py:629
  35.7 3.4 %collective-permute-done.7.got_ref = bf16[64,4096]{1,0:T(8,128)(2,1)S(1)} collective-permute-done((bf16[64,4096]{1,0:T(8,128)(2,1)S(1)}, bf16[64,4096]{1,0:T(8,128)(2,1)S(1)}, u32[]{:S(2)}, u32[]{:S(2)}) %collective-permute-start.7) | collective-permute-done | bytes 524320 | tf_op jit(solution)/shard_map/ppermute | solution.py:626
  39.1 0.2 pair_sum.2
  39.2 0.2 collective-permute-start.11
  39.4 1.8 %collective-permute-start.9 = (bf16[64,4096]{1,0:T(8,128)(2,1)S(1)}, bf16[64,4096]{1,0:T(8,128)(2,1)S(1)}, u32[]{:S(2)}, u32[]{:S(2)}) collective-permute-start(bf16[64,4096]{1,0:T(8,128)(2,1)S(1)} %get-tuple-element.45), channel_id=1, source_target_pairs={{0,1},{1,0},{2,3},{3,2},{4,5},{5,4},{6,7},{7,6},{8,9},{9,8},{10,11... | collective-permute-start | bytes 1572872 | tf_op jit(solution)/shard_map/ppermute | solution.py:628
  41.2 2.6 %collective-permute-start.8 = (bf16[32,4096]{1,0:T(8,128)(2,1)S(1)}, bf16[32,4096]{1,0:T(8,128)(2,1)S(1)}, u32[]{:S(2)}, u32[]{:S(2)}) collective-permute-start(bf16[32,4096]{1,0:T(8,128)(2,1)S(1)} %get-tuple-element.43), channel_id=1, source_target_pairs={{0,2},{1,3},{2,0},{3,1},{4,6},{5,7},{6,4},{7,5},{8,10},{9,11},{10,... | collective-permute-start | bytes 786440 | tf_op jit(solution)/shard_map/ppermute | solution.py:664
  43.8 0.2 join_states.1.rest_0_
  44.0 3.5 %collective-permute-start.14 = (bf16[2,136,1024]{2,1,0:T(8,128)(2,1)S(1)}, bf16[2,136,1024]{2,1,0:T(8,128)(2,1)S(1)}, u32[]{:S(2)}, u32[]{:S(2)}) collective-permute-start(bf16[2,136,1024]{2,1,0:T(8,128)(2,1)S(1)} %join_states.1.rest_0_), channel_id=1, source_target_pairs={{0,24},{4,28},{8,16},{12,20},{16,8},{20,12},{24,0},{28,4},{1,25},{... | collective-permute-start | bytes 1671176 | tf_op jit(solution)/shard_map/ppermute | solution.py:49
  47.5 1.2 %collective-permute-start.12 = (bf16[2,136,1024]{2,1,0:T(8,128)(2,1)S(1)}, bf16[2,136,1024]{2,1,0:T(8,128)(2,1)S(1)}, u32[]{:S(2)}, u32[]{:S(2)}) collective-permute-start(bf16[2,136,1024]{2,1,0:T(8,128)(2,1)S(1)} %join_states.1.rest_0_), channel_id=1, source_target_pairs={{0,8},{4,12},{8,0},{12,4},{16,24},{20,28},{24,16},{28,20},{1,9},{5... | collective-permute-start | bytes 1671176 | tf_op jit(solution)/shard_map/ppermute | solution.py:49
  48.7 0.9 %ready.1 = (f32[256,2048]{1,0:T(8,128)S(1)}, f32[256,2048]{1,0:T(8,128)S(1)}) custom-call(bf16[256,2048]{1,0:T(8,128)(2,1)S(1)} %copy-done.4, bf16[256,2048]{1,0:T(8,128)(2,1)S(1)} %copy-done.5, bf16[256,512]{1,0:T(8,128)(2,1)S(1)} %copy-done, f32[256,32]{1,0:T(8,128)S(1)} %copy-done.6, f32[1,32]{1,0:T(1,128)S(1)} %bitcast.5, bf16[64,2048]{1,0:T(8,128)(2,1)S(1)} %copy-done.3), custom_call_target="tpu_custom_call" | custom-call | flops 40000000000 | bytes 14800000 | tf_op jit(solution)/shard_map/ready/pallas_call | solution.py:674
  49.6 9.7 %collective-permute-done.9.got_ref = bf16[64,4096]{1,0:T(8,128)(2,1)S(1)} collective-permute-done((bf16[64,4096]{1,0:T(8,128)(2,1)S(1)}, bf16[64,4096]{1,0:T(8,128)(2,1)S(1)}, u32[]{:S(2)}, u32[]{:S(2)}) %collective-permute-start.9) | collective-permute-done | bytes 524320 | tf_op jit(solution)/shard_map/ppermute | solution.py:628
  59.3 0.1 pair_sum.3
  59.4 2.7 %collective-permute-start.10 = (bf16[32,4096]{1,0:T(8,128)(2,1)S(1)}, bf16[32,4096]{1,0:T(8,128)(2,1)S(1)}, u32[]{:S(2)}, u32[]{:S(2)}) collective-permute-start(bf16[32,4096]{1,0:T(8,128)(2,1)S(1)} %get-tuple-element.51), channel_id=1, source_target_pairs={{0,2},{1,3},{2,0},{3,1},{4,6},{5,7},{6,4},{7,5},{8,10},{9,11},{10,... | collective-permute-start | bytes 786440 | tf_op jit(solution)/shard_map/ppermute | solution.py:684
  62.1 11.7 %collective-permute-done.10.after_ref.late_got = bf16[32,4096]{1,0:T(8,128)(2,1)S(1)} collective-permute-done((bf16[32,4096]{1,0:T(8,128)(2,1)S(1)}, bf16[32,4096]{1,0:T(8,128)(2,1)S(1)}, u32[]{:S(2)}, u32[]{:S(2)}) %collective-permute-start.10) | collective-permute-done | bytes 262176 | tf_op jit(solution)/shard_map/ppermute | solution.py:684
  73.8 1.2 %enter_states.1 = (bf16[2,128,1024]{2,1,0:T(8,128)(2,1)S(1)}, bf16[2,128,1024]{2,1,0:T(8,128)(2,1)S(1)}) custom-call(bf16[2,136,1024]{2,1,0:T(8,128)(2,1)S(1)} %get-tuple-element.53.mine_ref, bf16[2,136,1024]{2,1,0:T(8,128)(2,1)S(1)} %collective-permute-done.11.other_ref, bf16[32,4096]{1,0:T(8,128)(2,1)S(1)} %collective-permute-done.10.after_ref.late_got, ...), custom_call_target="tpu_custom_call" | custom-call | tf_op jit(solution)/shard_map/enter_states/pallas_call | solution.py:688
  75.1 0.9 %last_sum.1 = (bf16[64,4096]{1,0:T(8,128)(2,1)}, f32[8,128]{1,0:T(8,128)S(1)}) custom-call(bf16[32,4096]{1,0:T(8,128)(2,1)S(1)} %collective-permute-done.8.after_ref.early_got, bf16[32,4096]{1,0:T(8,128)(2,1)S(1)} %get-tuple-element.44.early_keep, bf16[32,4096]{1,0:T(8,128)(2,1)S(1)} %collective-permute-done.10.after_ref.late_got, ...), custom_call_target="tpu_custom_call" | custom-call | tf_op jit(solution)/shard_map/last_sum/pallas_call | solution.py:705
  76.0 1.0 %collective-permute-done.15.other_ref = bf16[2,128,1024]{2,1,0:T(8,128)(2,1)S(1)} collective-permute-done((bf16[2,128,1024]{2,1,0:T(8,128)(2,1)S(1)}, bf16[2,128,1024]{2,1,0:T(8,128)(2,1)S(1)}, u32[]{:S(2)}, u32[]{:S(2)}) %collective-permute-start.15) | collective-permute-done | bytes 524320 | tf_op jit(solution)/shard_map/ppermute | solution.py:49
  77.0 1.7 %finish.1 = bf16[256,2048]{1,0:T(8,128)(2,1)} custom-call(bf16[256,512]{1,0:T(8,128)(2,1)S(1)} %copy-done, f32[256,2048]{1,0:T(8,128)S(1)} %get-tuple-element.50.rest_0_.base_ref, f32[256,2048]{1,0:T(8,128)S(1)} %get-tuple-element.57.wide_ref, bf16[2,128,1024]{2,1,0:T(8,128)(2,1)S(1)} %get-tuple-element.58.mine_ref, ...), custom_call_target="tpu_custom_call" | custom-call | tf_op jit(solution)/shard_map/finish/pallas_call | solution.py:717
  (26 shorter events, 0.2 us)
Async XLA Ops:
  1.7 11.9 %collective-permute-start.2 = (bf16[288,512]{1,0:T(8,128)(2,1)S(1)}, bf16[288,512]{1,0:T(8,128)(2,1)S(1)}, u32[]{:S(2)}, u32[]{:S(2)}) collective-permute-start(bf16[288,512]{1,0:T(8,128)(2,1)S(1)} %prepare.1.kv_ref.rest_0_), channel_id=1, source_target_pairs={{0,24},{4,28},{8,16},{12,20},{16,8},{20,12},{24,0},{28,4},{1,25},{... | collective-permute-start | bytes 884744 | tf_op jit(solution)/shard_map/ppermute | solution.py:49
  5.7 13.3 %collective-permute-start.1 = (bf16[288,512]{1,0:T(8,128)(2,1)S(1)}, bf16[288,512]{1,0:T(8,128)(2,1)S(1)}, u32[]{:S(2)}, u32[]{:S(2)}) collective-permute-start(bf16[288,512]{1,0:T(8,128)(2,1)S(1)} %prepare.1.kv_ref.rest_0_), channel_id=1, source_target_pairs={{0,16},{4,20},{8,24},{12,28},{16,0},{20,4},{24,8},{28,12},{1,17},{... | collective-permute-start | bytes 884744 | tf_op jit(solution)/shard_map/ppermute | solution.py:49
  6.2 13.1 %collective-permute-start = (bf16[288,512]{1,0:T(8,128)(2,1)S(1)}, bf16[288,512]{1,0:T(8,128)(2,1)S(1)}, u32[]{:S(2)}, u32[]{:S(2)}) collective-permute-start(bf16[288,512]{1,0:T(8,128)(2,1)S(1)} %prepare.1.kv_ref.rest_0_), channel_id=1, source_target_pairs={{0,8},{4,12},{8,0},{12,4},{16,24},{20,28},{24,16},{28,20},{1,9},{5... | collective-permute-start | bytes 884744 | tf_op jit(solution)/shard_map/ppermute | solution.py:49
  10.4 9.1 %collective-permute-start.3 = (bf16[288,512]{1,0:T(8,128)(2,1)S(1)}, bf16[288,512]{1,0:T(8,128)(2,1)S(1)}, u32[]{:S(2)}, u32[]{:S(2)}) collective-permute-start(bf16[288,512]{1,0:T(8,128)(2,1)S(1)} %get-tuple-element.33), channel_id=1, source_target_pairs={{0,4},{4,0},{8,12},{12,8},{16,20},{20,16},{24,28},{28,24},{1,5},{5... | collective-permute-start | bytes 884744 | tf_op jit(solution)/shard_map/ppermute | solution.py:49
  13.6 5.9 %collective-permute-start.6 = (bf16[288,512]{1,0:T(8,128)(2,1)S(1)}, bf16[288,512]{1,0:T(8,128)(2,1)S(1)}, u32[]{:S(2)}, u32[]{:S(2)}) collective-permute-start(bf16[288,512]{1,0:T(8,128)(2,1)S(1)} %collective-permute-done.2.rest_3_), channel_id=1, source_target_pairs={{0,4},{4,0},{8,12},{12,8},{16,20},{20,16},{24,28},{28,24},{1,5},{5... | collective-permute-start | bytes 884744 | tf_op jit(solution)/shard_map/ppermute | solution.py:49
  19.0 1.6 %collective-permute-start.5 = (bf16[288,512]{1,0:T(8,128)(2,1)S(1)}, bf16[288,512]{1,0:T(8,128)(2,1)S(1)}, u32[]{:S(2)}, u32[]{:S(2)}) collective-permute-start(bf16[288,512]{1,0:T(8,128)(2,1)S(1)} %collective-permute-done.1.rest_2_), channel_id=1, source_target_pairs={{0,4},{4,0},{8,12},{12,8},{16,20},{20,16},{24,28},{28,24},{1,5},{5... | collective-permute-start | bytes 884744 | tf_op jit(solution)/shard_map/ppermute | solution.py:49
  19.3 1.7 %collective-permute-start.4 = (bf16[288,512]{1,0:T(8,128)(2,1)S(1)}, bf16[288,512]{1,0:T(8,128)(2,1)S(1)}, u32[]{:S(2)}, u32[]{:S(2)}) collective-permute-start(bf16[288,512]{1,0:T(8,128)(2,1)S(1)} %collective-permute-done.rest_1_), channel_id=1, source_target_pairs={{0,4},{4,0},{8,12},{12,8},{16,20},{20,16},{24,28},{28,24},{1,5},{5... | collective-permute-start | bytes 884744 | tf_op jit(solution)/shard_map/ppermute | solution.py:49
  24.4 14.7 %collective-permute-start.7 = (bf16[64,4096]{1,0:T(8,128)(2,1)S(1)}, bf16[64,4096]{1,0:T(8,128)(2,1)S(1)}, u32[]{:S(2)}, u32[]{:S(2)}) collective-permute-start(bf16[64,4096]{1,0:T(8,128)(2,1)S(1)} %get-tuple-element.34), channel_id=1, source_target_pairs={{0,1},{1,0},{2,3},{3,2},{4,5},{5,4},{6,7},{7,6},{8,9},{9,8},{10,11... | collective-permute-start | bytes 1572872 | tf_op jit(solution)/shard_map/ppermute | solution.py:626
  26.2 3.1 %copy-start.1 = (f32[32]{0:T(128)S(1)}, f32[32]{0:T(128)}, u32[]{:S(2)}) copy-start(f32[32]{0:T(128)} %param.22) | copy-start | bytes 388
  26.2 3.1 %copy-start.3 = (bf16[64,2048]{1,0:T(8,128)(2,1)S(1)}, bf16[64,2048]{1,0:T(8,128)(2,1)}, u32[]{:S(2)}) copy-start(bf16[64,2048]{1,0:T(8,128)(2,1)} %constant.2.clone.expand_ref) | copy-start | bytes 786436
  35.6 13.1 %copy-start = (bf16[256,512]{1,0:T(8,128)(2,1)S(1)}, bf16[256,512]{1,0:T(8,128)(2,1)}, u32[]{:S(2)}) copy-start(bf16[256,512]{1,0:T(8,128)(2,1)} %get-tuple-element.48.mix_ref) | copy-start | bytes 786436
  35.6 13.1 %copy-start.2 = (f32[32]{0:T(128)S(1)}, f32[32]{0:T(128)}, u32[]{:S(2)}) copy-start(f32[32]{0:T(128)} %param.23) | copy-start | bytes 388
  35.6 13.1 %copy-start.4 = (bf16[256,2048]{1,0:T(8,128)(2,1)S(1)}, bf16[256,2048]{1,0:T(8,128)(2,1)}, u32[]{:S(2)}) copy-start(bf16[256,2048]{1,0:T(8,128)(2,1)} %get-tuple-element.46.xc_ref) | copy-start | bytes 3145732
  35.6 13.1 %copy-start.5 = (bf16[256,2048]{1,0:T(8,128)(2,1)S(1)}, bf16[256,2048]{1,0:T(8,128)(2,1)}, u32[]{:S(2)}) copy-start(bf16[256,2048]{1,0:T(8,128)(2,1)} %get-tuple-element.47.xt_ref) | copy-start | bytes 3145732
  35.6 13.1 %copy-start.6 = (f32[256,32]{1,0:T(8,128)S(1)}, f32[256,32]{1,0:T(8,128)}, u32[]{:S(2)}) copy-start(f32[256,32]{1,0:T(8,128)} %get-tuple-element.49.reach_ref) | copy-start | bytes 98308
  39.2 4.5 %collective-permute-start.11 = (bf16[2,136,1024]{2,1,0:T(8,128)(2,1)S(1)}, bf16[2,136,1024]{2,1,0:T(8,128)(2,1)S(1)}, u32[]{:S(2)}, u32[]{:S(2)}) collective-permute-start(bf16[2,136,1024]{2,1,0:T(8,128)(2,1)S(1)} %get-tuple-element.54), channel_id=1, source_target_pairs={{0,4},{4,0},{8,12},{12,8},{16,20},{20,16},{24,28},{28,24},{1,5},{5... | collective-permute-start | bytes 1671176 | tf_op jit(solution)/shard_map/ppermute | solution.py:49
  39.4 19.9 %collective-permute-start.9 = (bf16[64,4096]{1,0:T(8,128)(2,1)S(1)}, bf16[64,4096]{1,0:T(8,128)(2,1)S(1)}, u32[]{:S(2)}, u32[]{:S(2)}) collective-permute-start(bf16[64,4096]{1,0:T(8,128)(2,1)S(1)} %get-tuple-element.45), channel_id=1, source_target_pairs={{0,1},{1,0},{2,3},{3,2},{4,5},{5,4},{6,7},{7,6},{8,9},{9,8},{10,11... | collective-permute-start | bytes 1572872 | tf_op jit(solution)/shard_map/ppermute | solution.py:628
  41.2 18.1 %collective-permute-start.8 = (bf16[32,4096]{1,0:T(8,128)(2,1)S(1)}, bf16[32,4096]{1,0:T(8,128)(2,1)S(1)}, u32[]{:S(2)}, u32[]{:S(2)}) collective-permute-start(bf16[32,4096]{1,0:T(8,128)(2,1)S(1)} %get-tuple-element.43), channel_id=1, source_target_pairs={{0,2},{1,3},{2,0},{3,1},{4,6},{5,7},{6,4},{7,5},{8,10},{9,11},{10,... | collective-permute-start | bytes 786440 | tf_op jit(solution)/shard_map/ppermute | solution.py:664
  44.0 29.8 %collective-permute-start.14 = (bf16[2,136,1024]{2,1,0:T(8,128)(2,1)S(1)}, bf16[2,136,1024]{2,1,0:T(8,128)(2,1)S(1)}, u32[]{:S(2)}, u32[]{:S(2)}) collective-permute-start(bf16[2,136,1024]{2,1,0:T(8,128)(2,1)S(1)} %join_states.1.rest_0_), channel_id=1, source_target_pairs={{0,24},{4,28},{8,16},{12,20},{16,8},{20,12},{24,0},{28,4},{1,25},{... | collective-permute-start | bytes 1671176 | tf_op jit(solution)/shard_map/ppermute | solution.py:49
  47.5 26.4 %collective-permute-start.13 = (bf16[2,136,1024]{2,1,0:T(8,128)(2,1)S(1)}, bf16[2,136,1024]{2,1,0:T(8,128)(2,1)S(1)}, u32[]{:S(2)}, u32[]{:S(2)}) collective-permute-start(bf16[2,136,1024]{2,1,0:T(8,128)(2,1)S(1)} %join_states.1.rest_0_), channel_id=1, source_target_pairs={{0,16},{4,20},{8,24},{12,28},{16,0},{20,4},{24,8},{28,12},{1,17},{... | collective-permute-start | bytes 1671176 | tf_op jit(solution)/shard_map/ppermute | solution.py:49
  47.5 26.4 %collective-permute-start.12 = (bf16[2,136,1024]{2,1,0:T(8,128)(2,1)S(1)}, bf16[2,136,1024]{2,1,0:T(8,128)(2,1)S(1)}, u32[]{:S(2)}, u32[]{:S(2)}) collective-permute-start(bf16[2,136,1024]{2,1,0:T(8,128)(2,1)S(1)} %join_states.1.rest_0_), channel_id=1, source_target_pairs={{0,8},{4,12},{8,0},{12,4},{16,24},{20,28},{24,16},{28,20},{1,9},{5... | collective-permute-start | bytes 1671176 | tf_op jit(solution)/shard_map/ppermute | solution.py:49
  59.4 14.4 %collective-permute-start.10 = (bf16[32,4096]{1,0:T(8,128)(2,1)S(1)}, bf16[32,4096]{1,0:T(8,128)(2,1)S(1)}, u32[]{:S(2)}, u32[]{:S(2)}) collective-permute-start(bf16[32,4096]{1,0:T(8,128)(2,1)S(1)} %get-tuple-element.51), channel_id=1, source_target_pairs={{0,2},{1,3},{2,0},{3,1},{4,6},{5,7},{6,4},{7,5},{8,10},{9,11},{10,... | collective-permute-start | bytes 786440 | tf_op jit(solution)/shard_map/ppermute | solution.py:684
  75.0 2.0 %collective-permute-start.15 = (bf16[2,128,1024]{2,1,0:T(8,128)(2,1)S(1)}, bf16[2,128,1024]{2,1,0:T(8,128)(2,1)S(1)}, u32[]{:S(2)}, u32[]{:S(2)}) collective-permute-start(bf16[2,128,1024]{2,1,0:T(8,128)(2,1)S(1)} %get-tuple-element.55.after_ref), channel_id=1, source_target_pairs={{0,4},{4,0},{8,12},{12,8},{16,20},{20,16},{24,28},{28,24},{1,5},{5... | collective-permute-start | bytes 1572872 | tf_op jit(solution)/shard_map/ppermute | solution.py:49

commit v5 on v4

--- a/solution.py
+++ b/solution.py
@@ -88,9 +88,12 @@
     if part == 0:
         total = len(places)
         send_ref, keep_ref, kvs, docs_all, lead_ref, scores, top, acc, ctx = rest[total:]
+        send_refs, keep_refs = [send_ref], [keep_ref]
         assemble(places, count, rest[:total], kvs, docs_all, lead_ref)
     else:
-        kvs, docs_all, _, send_ref, keep_ref, scores, top, acc, ctx = rest
+        kvs, docs_all = rest[:2]
+        send_refs, keep_refs = rest[3:5], rest[5:7]
+        scores, top, acc, ctx = rest[7:]
     me = lax.axis_index("seq")
     odd = lax.rem(lax.axis_index("head"), 2)
     rows = q_ref.shape[0] // 2
@@ -177,9 +180,11 @@
         for at in range(0, columns, 256)
     ]
 
-    def put(low_ref, high_ref):
+    def put(low_refs, high_refs):
+        wide = low_refs[0].shape[1] // 256
         for at, got in enumerate(made):
-            lanes = slice(at * 256, (at + 1) * 256)
+            low_ref, high_ref = low_refs[at // wide], high_refs[at // wide]
+            lanes = slice(at % wide * 256, (at % wide + 1) * 256)
             for side in range(2):
                 first = 2 * side * own_rows
                 low_ref[side * own_rows : (side + 1) * own_rows, lanes] = got[first : first + own_rows]
@@ -189,11 +194,11 @@
 
     @pl.when(odd == 0)
     def _():
-        put(keep_ref, send_ref)
+        put(keep_refs, send_refs)
 
     @pl.when(odd == 1)
     def _():
-        put(send_ref, keep_ref)
+        put(send_refs, keep_refs)
 
 
 def attend(queries, out_weight, part, places, operands):
@@ -214,6 +219,7 @@
         ]
     else:
         specs = [vmem(), vmem(), anywhere()]
+        outs = [jax.ShapeDtypeStruct((chunk, columns // 2), BF)] * 4
     return pl.pallas_call(
         functools.partial(attend_kernel, places, count, part),
         in_specs=[vmem()] * 2 + specs,
@@ -269,11 +275,13 @@
     )(got, keep, after, *also)
 
 
-def last_kernel(early_got, early_keep, late_got, late_keep, after_ref, out_ref, done_ref):
+def last_kernel(early_got, early_keep, got_a, keep_a, got_b, keep_b, after_ref, out_ref, done_ref):
     done_ref[...] = jnp.zeros(done_ref.shape, F32)
-    rows = early_got.shape[0]
+    rows, columns = early_got.shape
     out_ref[:rows] = (early_got[...].astype(F32) + early_keep[...].astype(F32)).astype(BF)
-    out_ref[rows:] = (late_got[...].astype(F32) + late_keep[...].astype(F32)).astype(BF)
+    for at, (got, keep) in enumerate(((got_a, keep_a), (got_b, keep_b))):
+        lanes = slice(at * columns // 2, (at + 1) * columns // 2)
+        out_ref[rows:, lanes] = (got[...].astype(F32) + keep[...].astype(F32)).astype(BF)
 
 
 def prepare_kernel(k_ref, v_ref, docs_ref, xf_ref, xb_ref, bf_ref, bb_ref, kv_ref):
@@ -452,7 +460,7 @@
             joined(other_ref[half], mine_ref[half])
 
 
-def enter_kernel(places, count, mine_ref, other_ref, after_ref, *rest):
+def enter_kernel(places, count, mine_ref, other_ref, after_ref, also_ref, *rest):
     total = len(places)
     pieces = rest[:total]
     keep_ref, send_ref, fronts, backs, sems, run = rest[total:]
@@ -624,8 +632,9 @@
         query_rows, weight, 0, [pattern for pattern, _ in pieces], [array for _, array in pieces]
     )
     early_pair = lax.ppermute(early_send, "head", pair)
-    late_send, late_keep = attend(query_rows, weight, 1, None, [kvs, docs_all, early_keep])
-    late_pair = lax.ppermute(late_send, "head", pair)
+    late = attend(query_rows, weight, 1, None, [kvs, docs_all, early_keep])
+    late_keep = late[2]
+    late_pairs = [lax.ppermute(send, "head", pair) for send in late[:2]]
     xc, xt, mix, reach, keep, send = pl.pallas_call(
         functools.partial(local_kernel, count),
         grid=(2,),
@@ -680,14 +689,18 @@
         compiler_params=params(12),
         name="ready",
     )(xc, xt, mix, reach, skip_gain.reshape(1, heads), expand)
-    late_cross, late_mine = pair_sum(late_pair, late_keep, early_got, False, base)
-    late_got = lax.ppermute(late_cross, "head", cross)
+    late_cross, late_mine = pair_sum(late_pairs[0], late[2], late[2], False, base)
+    late_got = [lax.ppermute(late_cross, "head", cross)]
+    late_mine = [late_mine]
+    late_cross, mine = pair_sum(late_pairs[1], late[3], early_got, False)
+    late_got.append(lax.ppermute(late_cross, "head", cross))
+    late_mine.append(mine)
     chip_pieces = chip_gather(chip)
     chips = count // 2
     state_shape = jax.ShapeDtypeStruct((2, STATE, x_group), BF)
     enter_mine, enter_other = pl.pallas_call(
         functools.partial(enter_kernel, [pattern for pattern, _ in chip_pieces], count),
-        in_specs=[vmem(), vmem()] + [anywhere()] * (1 + len(chip_pieces)),
+        in_specs=[vmem(), vmem()] + [anywhere()] * (2 + len(chip_pieces)),
         out_specs=[vmem(), vmem()],
         out_shape=[state_shape, state_shape],
         scratch_shapes=[
@@ -699,12 +712,12 @@
         compiler_params=params(14 + chips),
         cost_estimate=takes(0),
         name="enter_states",
-    )(keep, other, late_got, *[array for _, array in chip_pieces])
+    )(keep, other, *late_got, *[array for _, array in chip_pieces])
     enter_got = swap(enter_other, 1)
 
     attn_out, summed = pl.pallas_call(
         last_kernel,
-        in_specs=[vmem()] * 4 + [anywhere()],
+        in_specs=[vmem()] * 6 + [anywhere()],
         out_specs=[vmem()] * 2,
         out_shape=[
             jax.ShapeDtypeStruct((rows // 2, out_weight.shape[1]), BF),
@@ -713,7 +726,7 @@
         compiler_params=params(6),
         cost_estimate=takes(0),
         name="last_sum",
-    )(early_got, early_mine, late_got, late_mine, enter_other)
+    )(early_got, early_mine, late_got[0], late_mine[0], late_got[1], late_mine[1], enter_other)
     ssm_out = pl.pallas_call(
         finish_kernel,
         grid=(2,),

time: 79.5 us -> 79.2 us (level); the launches traced: 78.7 us -> 79.3 us
  Pallas kernels: 23 us -> 26 us
  waiting for transfers between devices: 36.1 us -> 33.1 us
    pallas_call x2, Pallas kernels: 6.36 us -> 9.25 us  [attend(): pl.pallas_call(functools.partial(attend_kernel, places, count, part), in_...]
    ppermute x1, waiting for transfers between devices: 3.4 us -> 1.3 us  [shards(): early_pair = lax.ppermute(early_send, 'head', pair)]
    ppermute x2 -> x4, waiting for transfers between devices: 21.4 us -> 20.5 us  [the longest x1 9.63 us: shards(): late_got = [lax.ppermute(late_cross, 'head', cross)]]
    ppermute x2 -> x4, starting transfers between devices: 4.49 us -> 5.08 us  [the longest x2 2.09 us: shards(): late_pairs = [lax.ppermute(send, 'head', pair) for send in late[:2]]]
  transfers between devices with their start and end apart: 16 -> 18, of which waited for: 9 -> 11; matrix products, arithmetic and copies ran while one was open for 0% -> 0% of each run, Pallas kernels for 20% -> 21%
where the time goes in v5:
time: 79.2 us; the launch traced here: 79.3 us
  waiting for transfers between devices  33.1 us (42%)
  Pallas kernels  26 us (33%)
  starting transfers between devices  19.4 us (24%)
  between operations  0.81 us (1%)
    ppermute x12, waiting for transfers between devices, swap(): return lax.ppermute(x, 'seq', [(i, i ^ bit) for i in range(count)])  11.3 us
    ppermute x12, starting transfers between devices, swap(): return lax.ppermute(x, 'seq', [(i, i ^ bit) for i in range(count)])  9.77 us
    ppermute x1, waiting for transfers between devices, shards(): late_got = [lax.ppermute(late_cross, 'head', cross)]  9.63 us
    pallas_call x2, Pallas kernels, attend(): pl.pallas_call(functools.partial(attend_kernel, places, count, part), in_...  9.25 us
    ppermute x2, waiting for transfers between devices, shards(): late_pairs = [lax.ppermute(send, 'head', pair) for send in late[:2]]  9.23 us
    pallas_call x1, Pallas kernels, shards(): pl.pallas_call(functools.partial(local_kernel, count), grid=(2,), in_spec...  6.35 us
    pallas_call x1, Pallas kernels, shards(): pl.pallas_call(load_kernel, in_specs=[anywhere()] * 4 + [vmem()], out_spe...  4.07 us
    ppermute x1, starting transfers between devices, shards(): early_got = lax.ppermute(early_cross, 'head', cross)  2.74 us
  transfers between devices with their start and end apart: 18, of which 11 were waited for; matrix products, arithmetic and copies ran while one was open for 0% of the time, Pallas kernels for 21%

profile of v5, /device:TPU:0, one launch (start us, length us, event | category | flops | bytes accessed | tf_op | source)
XLA Modules:
  0.0 79.3 jit_solution(948193609960363767)
XLA Ops:
  0.6 1.1 %prepare.1.kv_ref.rest_0_ = bf16[288,512]{1,0:T(8,128)(2,1)S(1)} custom-call(bf16[256,256]{1,0:T(8,128)(2,1)} %k_ref.1, bf16[256,256]{1,0:T(8,128)(2,1)} %v_ref.1, s32[1,256]{1,0:T(1,128)} %bitcast.6, bf16[256,2048]{1,0:T(8,128)(2,1)} %x_ref.1, bf16[256,2048]{1,0:T(8,128)(2,1)} %x_ref.1, bf16[256,2,256]{2,1,0:T(2,128)(2,1)} %bc_ref.1, ...), custom_call_target="tpu_custom_call" | custom-call | tf_op jit(solution)/shard_map/prepare/pallas_call | solution.py:582
  1.7 4.0 %collective-permute-start.2 = (bf16[288,512]{1,0:T(8,128)(2,1)S(1)}, bf16[288,512]{1,0:T(8,128)(2,1)S(1)}, u32[]{:S(2)}, u32[]{:S(2)}) collective-permute-start(bf16[288,512]{1,0:T(8,128)(2,1)S(1)} %prepare.1.kv_ref.rest_0_), channel_id=1, source_target_pairs={{0,24},{4,28},{8,16},{12,20},{16,8},{20,12},{24,0},{28,4},{1,25},{... | collective-permute-start | bytes 884744 | tf_op jit(solution)/shard_map/ppermute | solution.py:49
  5.7 0.5 collective-permute-start.1
  6.4 4.1 %load.1 = (bf16[1024,4096]{1,0:T(8,128)(2,1)S(1)}, bf16[256,1024]{1,0:T(8,128)(2,1)S(1)}, bf16[256,2048]{1,0:T(8,128)(2,1)S(1)}, bf16[256,512]{1,0:T(8,128)(2,1)S(1)}, bf16[288,512]{1,0:T(8,128)(2,1)S(1)}) custom-call(bf16[1024,4096]{1,0:T(8,128)(2,1)} %w_ref.1, bf16[256,1024]{1,0:T(8,128)(2,1)} %q_ref.1, bf16[256,2048]{1,0:T(8,128)(2,1)} %x_ref.1, ...), custom_call_target="tpu_custom_call" | custom-call | flops 49999998976 | bytes 18500000 | tf_op jit(solution)/shard_map/load/pallas_call | solution.py:603
  10.5 3.1 %collective-permute-done.2.rest_3_ = bf16[288,512]{1,0:T(8,128)(2,1)S(1)} collective-permute-done((bf16[288,512]{1,0:T(8,128)(2,1)S(1)}, bf16[288,512]{1,0:T(8,128)(2,1)S(1)}, u32[]{:S(2)}, u32[]{:S(2)}) %collective-permute-start.2) | collective-permute-done | bytes 294944 | tf_op jit(solution)/shard_map/ppermute | solution.py:49
  13.6 5.4 %collective-permute-done.1.rest_2_ = bf16[288,512]{1,0:T(8,128)(2,1)S(1)} collective-permute-done((bf16[288,512]{1,0:T(8,128)(2,1)S(1)}, bf16[288,512]{1,0:T(8,128)(2,1)S(1)}, u32[]{:S(2)}, u32[]{:S(2)}) %collective-permute-start.1) | collective-permute-done | bytes 294944 | tf_op jit(solution)/shard_map/ppermute | solution.py:49
  19.1 0.3 collective-permute-done.rest_1_
  19.3 0.2 collective-permute-start.4
  19.6 1.1 %collective-permute-done.5.rest_6_ = bf16[288,512]{1,0:T(8,128)(2,1)S(1)} collective-permute-done((bf16[288,512]{1,0:T(8,128)(2,1)S(1)}, bf16[288,512]{1,0:T(8,128)(2,1)S(1)}, u32[]{:S(2)}, u32[]{:S(2)}) %collective-permute-start.5) | collective-permute-done | bytes 294944 | tf_op jit(solution)/shard_map/ppermute | solution.py:49
  20.6 0.4 collective-permute-done.4.rest_5_
  21.0 4.7 %attend_early.1 = (bf16[64,4096]{1,0:T(8,128)(2,1)S(1)}, bf16[64,4096]{1,0:T(8,128)(2,1)S(1)}, bf16[2048,512]{1,0:T(8,128)(2,1)S(1)}, f32[8,256]{1,0:T(8,128)S(1)}, bf16[2,16,512]{2,1,0:T(8,128)(2,1)S(1)}) custom-call(bf16[256,1024]{1,0:T(8,128)(2,1)S(1)} %get-tuple-element.35.q_ref, bf16[1024,4096]{1,0:T(8,128)(2,1)S(1)} %get-tuple-element.36.w_ref, ...), custom_call_target="tpu_custom_call" | custom-call | flops 80000000000 | bytes 29600000 | tf_op jit(solution)/shard_map/attend_early/pallas_call | solution.py:223
  25.8 1.8 %collective-permute-start.7 = (bf16[64,4096]{1,0:T(8,128)(2,1)S(1)}, bf16[64,4096]{1,0:T(8,128)(2,1)S(1)}, u32[]{:S(2)}, u32[]{:S(2)}) collective-permute-start(bf16[64,4096]{1,0:T(8,128)(2,1)S(1)} %get-tuple-element.38), channel_id=1, source_target_pairs={{0,1},{1,0},{2,3},{3,2},{4,5},{5,4},{6,7},{7,6},{8,9},{9,8},{10,11... | collective-permute-start | bytes 1572872 | tf_op jit(solution)/shard_map/ppermute | solution.py:634
  27.6 4.5 %attend_late.1 = (bf16[64,2048]{1,0:T(8,128)(2,1)S(1)}, bf16[64,2048]{1,0:T(8,128)(2,1)S(1)}, bf16[64,2048]{1,0:T(8,128)(2,1)S(1)}, bf16[64,2048]{1,0:T(8,128)(2,1)S(1)}) custom-call(bf16[256,1024]{1,0:T(8,128)(2,1)S(1)} %get-tuple-element.35.q_ref, bf16[1024,4096]{1,0:T(8,128)(2,1)S(1)} %get-tuple-element.36.w_ref, ...), custom_call_target="tpu_custom_call" | custom-call | flops 80000000000 | bytes 29600000 | tf_op jit(solution)/shard_map/attend_late/pallas_call | solution.py:223
  32.2 6.3 %local_states.1 = (bf16[256,2048]{1,0:T(8,128)(2,1)}, bf16[256,2048]{1,0:T(8,128)(2,1)}, bf16[256,512]{1,0:T(8,128)(2,1)}, f32[256,32]{1,0:T(8,128)}, bf16[2,136...) custom-call(f32[8,256]{1,0:T(8,128)S(1)} %get-tuple-element.40.rest_1_.docs_ref, ...), custom_call_target="tpu_custom_call" | custom-call | flops 54999998464 | bytes 20350000 | tf_op jit(solution)/shard_map/local_states/pallas_call | solution.py:638
  38.6 1.3 %collective-permute-done.7.got_ref = bf16[64,4096]{1,0:T(8,128)(2,1)S(1)} collective-permute-done((bf16[64,4096]{1,0:T(8,128)(2,1)S(1)}, bf16[64,4096]{1,0:T(8,128)(2,1)S(1)}, u32[]{:S(2)}, u32[]{:S(2)}) %collective-permute-start.7) | collective-permute-done | bytes 524320 | tf_op jit(solution)/shard_map/ppermute | solution.py:634
  40.1 1.8 %collective-permute-start.9 = (bf16[64,2048]{1,0:T(8,128)(2,1)S(1)}, bf16[64,2048]{1,0:T(8,128)(2,1)S(1)}, u32[]{:S(2)}, u32[]{:S(2)}) collective-permute-start(bf16[64,2048]{1,0:T(8,128)(2,1)S(1)} %get-tuple-element.49), channel_id=1, source_target_pairs={{0,1},{1,0},{2,3},{3,2},{4,5},{5,4},{6,7},{7,6},{8,9},{9,8},{10,11... | collective-permute-start | bytes 786440 | tf_op jit(solution)/shard_map/ppermute | solution.py:637
  41.9 0.3 collective-permute-start.11
  42.2 2.7 %collective-permute-start.8 = (bf16[32,4096]{1,0:T(8,128)(2,1)S(1)}, bf16[32,4096]{1,0:T(8,128)(2,1)S(1)}, u32[]{:S(2)}, u32[]{:S(2)}) collective-permute-start(bf16[32,4096]{1,0:T(8,128)(2,1)S(1)} %get-tuple-element.47), channel_id=1, source_target_pairs={{0,2},{1,3},{2,0},{3,1},{4,6},{5,7},{6,4},{7,5},{8,10},{9,11},{10,... | collective-permute-start | bytes 786440 | tf_op jit(solution)/shard_map/ppermute | solution.py:673
  45.1 0.8 %collective-permute-start.16 = (bf16[2,136,1024]{2,1,0:T(8,128)(2,1)S(1)}, bf16[2,136,1024]{2,1,0:T(8,128)(2,1)S(1)}, u32[]{:S(2)}, u32[]{:S(2)}) collective-permute-start(bf16[2,136,1024]{2,1,0:T(8,128)(2,1)S(1)} %join_states.1.rest_0_), channel_id=1, source_target_pairs={{0,24},{4,28},{8,16},{12,20},{16,8},{20,12},{24,0},{28,4},{1,25},{... | collective-permute-start | bytes 1671176 | tf_op jit(solution)/shard_map/ppermute | solution.py:49
  46.0 2.2 %collective-permute-start.15 = (bf16[2,136,1024]{2,1,0:T(8,128)(2,1)S(1)}, bf16[2,136,1024]{2,1,0:T(8,128)(2,1)S(1)}, u32[]{:S(2)}, u32[]{:S(2)}) collective-permute-start(bf16[2,136,1024]{2,1,0:T(8,128)(2,1)S(1)} %join_states.1.rest_0_), channel_id=1, source_target_pairs={{0,16},{4,20},{8,24},{12,28},{16,0},{20,4},{24,8},{28,12},{1,17},{... | collective-permute-start | bytes 1671176 | tf_op jit(solution)/shard_map/ppermute | solution.py:49
  48.2 6.8 %collective-permute-done.9.got_ref = bf16[64,2048]{1,0:T(8,128)(2,1)S(1)} collective-permute-done((bf16[64,2048]{1,0:T(8,128)(2,1)S(1)}, bf16[64,2048]{1,0:T(8,128)(2,1)S(1)}, u32[]{:S(2)}, u32[]{:S(2)}) %collective-permute-start.9) | collective-permute-done | bytes 262176 | tf_op jit(solution)/shard_map/ppermute | solution.py:637
  55.0 1.7 %collective-permute-start.14 = (bf16[2,136,1024]{2,1,0:T(8,128)(2,1)S(1)}, bf16[2,136,1024]{2,1,0:T(8,128)(2,1)S(1)}, u32[]{:S(2)}, u32[]{:S(2)}) collective-permute-start(bf16[2,136,1024]{2,1,0:T(8,128)(2,1)S(1)} %join_states.1.rest_0_), channel_id=1, source_target_pairs={{0,8},{4,12},{8,0},{12,4},{16,24},{20,28},{24,16},{28,20},{1,9},{5... | collective-permute-start | bytes 1671176 | tf_op jit(solution)/shard_map/ppermute | solution.py:49
  56.7 0.9 %ready.1 = (f32[256,2048]{1,0:T(8,128)S(1)}, f32[256,2048]{1,0:T(8,128)S(1)}) custom-call(bf16[256,2048]{1,0:T(8,128)(2,1)S(1)} %copy-done.4, bf16[256,2048]{1,0:T(8,128)(2,1)S(1)} %copy-done.5, bf16[256,512]{1,0:T(8,128)(2,1)S(1)} %copy-done, f32[256,32]{1,0:T(8,128)S(1)} %copy-done.6, f32[1,32]{1,0:T(1,128)S(1)} %bitcast.5, bf16[64,2048]{1,0:T(8,128)(2,1)S(1)} %copy-done.3), custom_call_target="tpu_custom_call" | custom-call | flops 40000000000 | bytes 14800000 | tf_op jit(solution)/shard_map/ready/pallas_call | solution.py:683
  57.6 2.4 %collective-permute-done.11.got_ref = bf16[64,2048]{1,0:T(8,128)(2,1)S(1)} collective-permute-done((bf16[64,2048]{1,0:T(8,128)(2,1)S(1)}, bf16[64,2048]{1,0:T(8,128)(2,1)S(1)}, u32[]{:S(2)}, u32[]{:S(2)}) %collective-permute-start.11) | collective-permute-done | bytes 262176 | tf_op jit(solution)/shard_map/ppermute | solution.py:637
  60.0 1.8 %collective-permute-start.10 = (bf16[32,2048]{1,0:T(8,128)(2,1)S(1)}, bf16[32,2048]{1,0:T(8,128)(2,1)S(1)}, u32[]{:S(2)}, u32[]{:S(2)}) collective-permute-start(bf16[32,2048]{1,0:T(8,128)(2,1)S(1)} %get-tuple-element.55), channel_id=1, source_target_pairs={{0,2},{1,3},{2,0},{3,1},{4,6},{5,7},{6,4},{7,5},{8,10},{9,11},{10,... | collective-permute-start | bytes 393224 | tf_op jit(solution)/shard_map/ppermute | solution.py:693
  61.9 1.2 %collective-permute-start.12 = (bf16[32,2048]{1,0:T(8,128)(2,1)S(1)}, bf16[32,2048]{1,0:T(8,128)(2,1)S(1)}, u32[]{:S(2)}, u32[]{:S(2)}) collective-permute-start(bf16[32,2048]{1,0:T(8,128)(2,1)S(1)} %get-tuple-element.59), channel_id=1, source_target_pairs={{0,2},{1,3},{2,0},{3,1},{4,6},{5,7},{6,4},{7,5},{8,10},{9,11},{10,... | collective-permute-start | bytes 393224 | tf_op jit(solution)/shard_map/ppermute | solution.py:696
  63.1 9.6 %collective-permute-done.10.after_ref.got_a = bf16[32,2048]{1,0:T(8,128)(2,1)S(1)} collective-permute-done((bf16[32,2048]{1,0:T(8,128)(2,1)S(1)}, bf16[32,2048]{1,0:T(8,128)(2,1)S(1)}, u32[]{:S(2)}, u32[]{:S(2)}) %collective-permute-start.10) | collective-permute-done | bytes 131104 | tf_op jit(solution)/shard_map/ppermute | solution.py:693
  72.7 1.6 %collective-permute-done.12.also_ref.got_b = bf16[32,2048]{1,0:T(8,128)(2,1)S(1)} collective-permute-done((bf16[32,2048]{1,0:T(8,128)(2,1)S(1)}, bf16[32,2048]{1,0:T(8,128)(2,1)S(1)}, u32[]{:S(2)}, u32[]{:S(2)}) %collective-permute-start.12) | collective-permute-done | bytes 131104 | tf_op jit(solution)/shard_map/ppermute | solution.py:696
  74.4 1.2 %enter_states.1 = (bf16[2,128,1024]{2,1,0:T(8,128)(2,1)S(1)}, bf16[2,128,1024]{2,1,0:T(8,128)(2,1)S(1)}) custom-call(bf16[2,136,1024]{2,1,0:T(8,128)(2,1)S(1)} %get-tuple-element.61.mine_ref, bf16[2,136,1024]{2,1,0:T(8,128)(2,1)S(1)} %collective-permute-done.13.other_ref, bf16[32,2048]{1,0:T(8,128)(2,1)S(1)} %collective-permute-done.10.after_ref.got_a, ...), custom_call_target="tpu_custom_call" | custom-call | tf_op jit(solution)/shard_map/enter_states/pallas_call | solution.py:701
  75.6 0.9 %last_sum.1 = (bf16[64,4096]{1,0:T(8,128)(2,1)}, f32[8,128]{1,0:T(8,128)S(1)}) custom-call(bf16[32,4096]{1,0:T(8,128)(2,1)S(1)} %collective-permute-done.8.after_ref.early_got, bf16[32,4096]{1,0:T(8,128)(2,1)S(1)} %get-tuple-element.48.early_keep, bf16[32,2048]{1,0:T(8,128)(2,1)S(1)} %collective-permute-done.10.after_ref.got_a, ...), custom_call_target="tpu_custom_call" | custom-call | tf_op jit(solution)/shard_map/last_sum/pallas_call | solution.py:718
  76.6 1.0 %collective-permute-done.17.other_ref = bf16[2,128,1024]{2,1,0:T(8,128)(2,1)S(1)} collective-permute-done((bf16[2,128,1024]{2,1,0:T(8,128)(2,1)S(1)}, bf16[2,128,1024]{2,1,0:T(8,128)(2,1)S(1)}, u32[]{:S(2)}, u32[]{:S(2)}) %collective-permute-start.17) | collective-permute-done | bytes 524320 | tf_op jit(solution)/shard_map/ppermute | solution.py:49
  77.5 1.7 %finish.1 = bf16[256,2048]{1,0:T(8,128)(2,1)} custom-call(bf16[256,512]{1,0:T(8,128)(2,1)S(1)} %copy-done, f32[256,2048]{1,0:T(8,128)S(1)} %get-tuple-element.54.rest_0_.base_ref, f32[256,2048]{1,0:T(8,128)S(1)} %get-tuple-element.65.wide_ref, bf16[2,128,1024]{2,1,0:T(8,128)(2,1)S(1)} %get-tuple-element.66.mine_ref, ...), custom_call_target="tpu_custom_call" | custom-call | tf_op jit(solution)/shard_map/finish/pallas_call | solution.py:730
  (31 shorter events, 0.9 us)
Async XLA Ops:
  1.7 11.9 %collective-permute-start.2 = (bf16[288,512]{1,0:T(8,128)(2,1)S(1)}, bf16[288,512]{1,0:T(8,128)(2,1)S(1)}, u32[]{:S(2)}, u32[]{:S(2)}) collective-permute-start(bf16[288,512]{1,0:T(8,128)(2,1)S(1)} %prepare.1.kv_ref.rest_0_), channel_id=1, source_target_pairs={{0,24},{4,28},{8,16},{12,20},{16,8},{20,12},{24,0},{28,4},{1,25},{... | collective-permute-start | bytes 884744 | tf_op jit(solution)/shard_map/ppermute | solution.py:49
  5.7 13.3 %collective-permute-start.1 = (bf16[288,512]{1,0:T(8,128)(2,1)S(1)}, bf16[288,512]{1,0:T(8,128)(2,1)S(1)}, u32[]{:S(2)}, u32[]{:S(2)}) collective-permute-start(bf16[288,512]{1,0:T(8,128)(2,1)S(1)} %prepare.1.kv_ref.rest_0_), channel_id=1, source_target_pairs={{0,16},{4,20},{8,24},{12,28},{16,0},{20,4},{24,8},{28,12},{1,17},{... | collective-permute-start | bytes 884744 | tf_op jit(solution)/shard_map/ppermute | solution.py:49
  6.2 13.1 %collective-permute-start = (bf16[288,512]{1,0:T(8,128)(2,1)S(1)}, bf16[288,512]{1,0:T(8,128)(2,1)S(1)}, u32[]{:S(2)}, u32[]{:S(2)}) collective-permute-start(bf16[288,512]{1,0:T(8,128)(2,1)S(1)} %prepare.1.kv_ref.rest_0_), channel_id=1, source_target_pairs={{0,8},{4,12},{8,0},{12,4},{16,24},{20,28},{24,16},{28,20},{1,9},{5... | collective-permute-start | bytes 884744 | tf_op jit(solution)/shard_map/ppermute | solution.py:49
  10.4 9.1 %collective-permute-start.3 = (bf16[288,512]{1,0:T(8,128)(2,1)S(1)}, bf16[288,512]{1,0:T(8,128)(2,1)S(1)}, u32[]{:S(2)}, u32[]{:S(2)}) collective-permute-start(bf16[288,512]{1,0:T(8,128)(2,1)S(1)} %get-tuple-element.37), channel_id=1, source_target_pairs={{0,4},{4,0},{8,12},{12,8},{16,20},{20,16},{24,28},{28,24},{1,5},{5... | collective-permute-start | bytes 884744 | tf_op jit(solution)/shard_map/ppermute | solution.py:49
  13.6 5.9 %collective-permute-start.6 = (bf16[288,512]{1,0:T(8,128)(2,1)S(1)}, bf16[288,512]{1,0:T(8,128)(2,1)S(1)}, u32[]{:S(2)}, u32[]{:S(2)}) collective-permute-start(bf16[288,512]{1,0:T(8,128)(2,1)S(1)} %collective-permute-done.2.rest_3_), channel_id=1, source_target_pairs={{0,4},{4,0},{8,12},{12,8},{16,20},{20,16},{24,28},{28,24},{1,5},{5... | collective-permute-start | bytes 884744 | tf_op jit(solution)/shard_map/ppermute | solution.py:49
  19.0 1.6 %collective-permute-start.5 = (bf16[288,512]{1,0:T(8,128)(2,1)S(1)}, bf16[288,512]{1,0:T(8,128)(2,1)S(1)}, u32[]{:S(2)}, u32[]{:S(2)}) collective-permute-start(bf16[288,512]{1,0:T(8,128)(2,1)S(1)} %collective-permute-done.1.rest_2_), channel_id=1, source_target_pairs={{0,4},{4,0},{8,12},{12,8},{16,20},{20,16},{24,28},{28,24},{1,5},{5... | collective-permute-start | bytes 884744 | tf_op jit(solution)/shard_map/ppermute | solution.py:49
  19.3 1.7 %collective-permute-start.4 = (bf16[288,512]{1,0:T(8,128)(2,1)S(1)}, bf16[288,512]{1,0:T(8,128)(2,1)S(1)}, u32[]{:S(2)}, u32[]{:S(2)}) collective-permute-start(bf16[288,512]{1,0:T(8,128)(2,1)S(1)} %collective-permute-done.rest_1_), channel_id=1, source_target_pairs={{0,4},{4,0},{8,12},{12,8},{16,20},{20,16},{24,28},{28,24},{1,5},{5... | collective-permute-start | bytes 884744 | tf_op jit(solution)/shard_map/ppermute | solution.py:49
  25.8 14.1 %collective-permute-start.7 = (bf16[64,4096]{1,0:T(8,128)(2,1)S(1)}, bf16[64,4096]{1,0:T(8,128)(2,1)S(1)}, u32[]{:S(2)}, u32[]{:S(2)}) collective-permute-start(bf16[64,4096]{1,0:T(8,128)(2,1)S(1)} %get-tuple-element.38), channel_id=1, source_target_pairs={{0,1},{1,0},{2,3},{3,2},{4,5},{5,4},{6,7},{7,6},{8,9},{9,8},{10,11... | collective-permute-start | bytes 1572872 | tf_op jit(solution)/shard_map/ppermute | solution.py:634
  27.6 4.5 %copy-start.1 = (f32[32]{0:T(128)S(1)}, f32[32]{0:T(128)}, u32[]{:S(2)}) copy-start(f32[32]{0:T(128)} %param.22) | copy-start | bytes 388
  27.6 4.5 %copy-start.3 = (bf16[64,2048]{1,0:T(8,128)(2,1)S(1)}, bf16[64,2048]{1,0:T(8,128)(2,1)}, u32[]{:S(2)}) copy-start(bf16[64,2048]{1,0:T(8,128)(2,1)} %constant.2.clone.expand_ref) | copy-start | bytes 786436
  38.5 18.1 %copy-start = (bf16[256,512]{1,0:T(8,128)(2,1)S(1)}, bf16[256,512]{1,0:T(8,128)(2,1)}, u32[]{:S(2)}) copy-start(bf16[256,512]{1,0:T(8,128)(2,1)} %get-tuple-element.52.mix_ref) | copy-start | bytes 786436
  38.5 18.1 %copy-start.2 = (f32[32]{0:T(128)S(1)}, f32[32]{0:T(128)}, u32[]{:S(2)}) copy-start(f32[32]{0:T(128)} %param.23) | copy-start | bytes 388
  38.5 18.1 %copy-start.4 = (bf16[256,2048]{1,0:T(8,128)(2,1)S(1)}, bf16[256,2048]{1,0:T(8,128)(2,1)}, u32[]{:S(2)}) copy-start(bf16[256,2048]{1,0:T(8,128)(2,1)} %get-tuple-element.50.xc_ref) | copy-start | bytes 3145732
  38.5 18.1 %copy-start.5 = (bf16[256,2048]{1,0:T(8,128)(2,1)S(1)}, bf16[256,2048]{1,0:T(8,128)(2,1)}, u32[]{:S(2)}) copy-start(bf16[256,2048]{1,0:T(8,128)(2,1)} %get-tuple-element.51.xt_ref) | copy-start | bytes 3145732
  38.5 18.1 %copy-start.6 = (f32[256,32]{1,0:T(8,128)S(1)}, f32[256,32]{1,0:T(8,128)}, u32[]{:S(2)}) copy-start(f32[256,32]{1,0:T(8,128)} %get-tuple-element.53.reach_ref) | copy-start | bytes 98308
  40.0 4.9 %collective-permute-start.13 = (bf16[2,136,1024]{2,1,0:T(8,128)(2,1)S(1)}, bf16[2,136,1024]{2,1,0:T(8,128)(2,1)S(1)}, u32[]{:S(2)}, u32[]{:S(2)}) collective-permute-start(bf16[2,136,1024]{2,1,0:T(8,128)(2,1)S(1)} %get-tuple-element.62), channel_id=1, source_target_pairs={{0,4},{4,0},{8,12},{12,8},{16,20},{20,16},{24,28},{28,24},{1,5},{5... | collective-permute-start | bytes 1671176 | tf_op jit(solution)/shard_map/ppermute | solution.py:49
  40.1 14.9 %collective-permute-start.9 = (bf16[64,2048]{1,0:T(8,128)(2,1)S(1)}, bf16[64,2048]{1,0:T(8,128)(2,1)S(1)}, u32[]{:S(2)}, u32[]{:S(2)}) collective-permute-start(bf16[64,2048]{1,0:T(8,128)(2,1)S(1)} %get-tuple-element.49), channel_id=1, source_target_pairs={{0,1},{1,0},{2,3},{3,2},{4,5},{5,4},{6,7},{7,6},{8,9},{9,8},{10,11... | collective-permute-start | bytes 786440 | tf_op jit(solution)/shard_map/ppermute | solution.py:637
  41.9 18.1 %collective-permute-start.11 = (bf16[64,2048]{1,0:T(8,128)(2,1)S(1)}, bf16[64,2048]{1,0:T(8,128)(2,1)S(1)}, u32[]{:S(2)}, u32[]{:S(2)}) collective-permute-start(bf16[64,2048]{1,0:T(8,128)(2,1)S(1)} %get-tuple-element.57), channel_id=1, source_target_pairs={{0,1},{1,0},{2,3},{3,2},{4,5},{5,4},{6,7},{7,6},{8,9},{9,8},{10,11... | collective-permute-start | bytes 786440 | tf_op jit(solution)/shard_map/ppermute | solution.py:637
  42.2 19.7 %collective-permute-start.8 = (bf16[32,4096]{1,0:T(8,128)(2,1)S(1)}, bf16[32,4096]{1,0:T(8,128)(2,1)S(1)}, u32[]{:S(2)}, u32[]{:S(2)}) collective-permute-start(bf16[32,4096]{1,0:T(8,128)(2,1)S(1)} %get-tuple-element.47), channel_id=1, source_target_pairs={{0,2},{1,3},{2,0},{3,1},{4,6},{5,7},{6,4},{7,5},{8,10},{9,11},{10,... | collective-permute-start | bytes 786440 | tf_op jit(solution)/shard_map/ppermute | solution.py:673
  45.1 29.2 %collective-permute-start.16 = (bf16[2,136,1024]{2,1,0:T(8,128)(2,1)S(1)}, bf16[2,136,1024]{2,1,0:T(8,128)(2,1)S(1)}, u32[]{:S(2)}, u32[]{:S(2)}) collective-permute-start(bf16[2,136,1024]{2,1,0:T(8,128)(2,1)S(1)} %join_states.1.rest_0_), channel_id=1, source_target_pairs={{0,24},{4,28},{8,16},{12,20},{16,8},{20,12},{24,0},{28,4},{1,25},{... | collective-permute-start | bytes 1671176 | tf_op jit(solution)/shard_map/ppermute | solution.py:49
  46.0 28.4 %collective-permute-start.15 = (bf16[2,136,1024]{2,1,0:T(8,128)(2,1)S(1)}, bf16[2,136,1024]{2,1,0:T(8,128)(2,1)S(1)}, u32[]{:S(2)}, u32[]{:S(2)}) collective-permute-start(bf16[2,136,1024]{2,1,0:T(8,128)(2,1)S(1)} %join_states.1.rest_0_), channel_id=1, source_target_pairs={{0,16},{4,20},{8,24},{12,28},{16,0},{20,4},{24,8},{28,12},{1,17},{... | collective-permute-start | bytes 1671176 | tf_op jit(solution)/shard_map/ppermute | solution.py:49
  55.0 19.4 %collective-permute-start.14 = (bf16[2,136,1024]{2,1,0:T(8,128)(2,1)S(1)}, bf16[2,136,1024]{2,1,0:T(8,128)(2,1)S(1)}, u32[]{:S(2)}, u32[]{:S(2)}) collective-permute-start(bf16[2,136,1024]{2,1,0:T(8,128)(2,1)S(1)} %join_states.1.rest_0_), channel_id=1, source_target_pairs={{0,8},{4,12},{8,0},{12,4},{16,24},{20,28},{24,16},{28,20},{1,9},{5... | collective-permute-start | bytes 1671176 | tf_op jit(solution)/shard_map/ppermute | solution.py:49
  60.0 12.7 %collective-permute-start.10 = (bf16[32,2048]{1,0:T(8,128)(2,1)S(1)}, bf16[32,2048]{1,0:T(8,128)(2,1)S(1)}, u32[]{:S(2)}, u32[]{:S(2)}) collective-permute-start(bf16[32,2048]{1,0:T(8,128)(2,1)S(1)} %get-tuple-element.55), channel_id=1, source_target_pairs={{0,2},{1,3},{2,0},{3,1},{4,6},{5,7},{6,4},{7,5},{8,10},{9,11},{10,... | collective-permute-start | bytes 393224 | tf_op jit(solution)/shard_map/ppermute | solution.py:693
  61.9 12.4 %collective-permute-start.12 = (bf16[32,2048]{1,0:T(8,128)(2,1)S(1)}, bf16[32,2048]{1,0:T(8,128)(2,1)S(1)}, u32[]{:S(2)}, u32[]{:S(2)}) collective-permute-start(bf16[32,2048]{1,0:T(8,128)(2,1)S(1)} %get-tuple-element.59), channel_id=1, source_target_pairs={{0,2},{1,3},{2,0},{3,1},{4,6},{5,7},{6,4},{7,5},{8,10},{9,11},{10,... | collective-permute-start | bytes 393224 | tf_op jit(solution)/shard_map/ppermute | solution.py:696
  75.6 2.0 %collective-permute-start.17 = (bf16[2,128,1024]{2,1,0:T(8,128)(2,1)S(1)}, bf16[2,128,1024]{2,1,0:T(8,128)(2,1)S(1)}, u32[]{:S(2)}, u32[]{:S(2)}) collective-permute-start(bf16[2,128,1024]{2,1,0:T(8,128)(2,1)S(1)} %get-tuple-element.63.after_ref), channel_id=1, source_target_pairs={{0,4},{4,0},{8,12},{12,8},{16,20},{20,16},{24,28},{28,24},{1,5},{5... | collective-permute-start | bytes 1572872 | tf_op jit(solution)/shard_map/ppermute | solution.py:49
